TPU v7x, 32 devices: a whole 2x2x4 slice. The times are simulated.
32 devices in a mesh: group: 8 (over z, y), row: 2 (over x), col: 2 (over core).
Axes of the slice: x: 2, y: 2, z: 4, core: 2. Of those that a mesh axis runs over, the one named last changes fastest.
Arguments:
- tokens: bfloat16 [5120, 2048], P(('group', 'col'), 'row'), may hold values from -6 to 6
- lengths: int32 [24], P('group'), may hold values from 1 to 512, as said below
- norm_gain: float32 [2048], P('row'), may hold values from 0.25 to 1.75
- w_query: bfloat16 [2048, 2048], P('row', 'col'), may hold values from -0.125 to 0.125
- w_key: bfloat16 [2048, 1024], P('row', 'col'), may hold values from -0.125 to 0.125
- w_value: bfloat16 [2048, 1024], P('row', 'col'), may hold values from -0.125 to 0.125
- w_head_gate: bfloat16 [2048, 16], P('row', 'col'), may hold values from -0.25 to 0.25
- query_gain: float32 [128], replicated, may hold values from 1 to 2
- key_gain: float32 [128], replicated, may hold values from 1 to 2
- w_out: bfloat16 [2048, 2048], P('col', 'row'), may hold values from -1.5 to 1.5
- ffn_gain: float32 [2048], P('row'), may hold values from 0.25 to 1.75
- w_gate: bfloat16 [2048, 6144], P('row', 'col'), may hold values from -0.125 to 0.125
- w_up: bfloat16 [2048, 6144], P('row', 'col'), may hold values from -0.125 to 0.125
- w_down: bfloat16 [6144, 2048], P('col', 'row'), may hold values from -0.15625 to 0.15625
- grad_out: bfloat16 [5120, 2048], P(('group', 'col'), 'row'), may hold values from -6 to 6
Outputs:
- output: bfloat16 [5120, 2048], P(('group', 'col'), 'row')
- input_grad: float32 [5120, 2048], P(('group', 'col'), 'row')
- grad_norm_gain: float32 [2048], P('row')
- grad_w_query: float32 [2048, 2048], P('row', 'col')
- grad_w_key: float32 [2048, 1024], P('row', 'col')
- grad_w_value: float32 [2048, 1024], P('row', 'col')
- grad_w_head_gate: float32 [2048, 16], P('row', 'col')
- grad_query_gain: float32 [128], replicated
- grad_key_gain: float32 [128], replicated
- grad_w_out: float32 [2048, 2048], P('col', 'row')
- grad_ffn_gain: float32 [2048], P('row')
- grad_w_gate: float32 [2048, 6144], P('row', 'col')
- grad_w_up: float32 [2048, 6144], P('row', 'col')
- grad_w_down: float32 [6144, 2048], P('col', 'row')
Inputs may be any that keep to these rules, and one draw needn't show every extreme that they name: Each group's 3 entries are the lengths of its sequences in token order; they sum to 640.
All inputs are finite; a program needn't handle non-finite values.
Results may differ from a plain program's by a relative error of at most 0.024.
Values may be sent and summed in bfloat16 or wider, within the bound.
A program may use at most 256 MiB of HBM per device.

v0:
```python
import jax
import jax.numpy as jnp
from jax import lax
from jax.sharding import PartitionSpec as P

EPS = 1e-06
THETA = 1000000.0
NEGATIVE = -1e30


def places(lengths_group, count):
    ends = jnp.cumsum(lengths_group)
    index = jnp.arange(count, dtype=jnp.int32)
    passed = (index[:, None] >= ends[None, :]).astype(jnp.int32)
    segment = jnp.sum(passed, axis=1)
    place = index - jnp.sum(passed * lengths_group[None, :], axis=1)
    return (segment, place)


def rope_tables(place, width):
    half = width // 2
    freq = THETA ** (-(jnp.arange(half, dtype=jnp.float32) * 2.0 / width))
    angle = place.astype(jnp.float32)[:, None] * freq[None, :]
    cosines = jnp.concatenate([jnp.cos(angle), jnp.cos(angle)], axis=1)
    sines = jnp.concatenate([jnp.sin(angle), jnp.sin(angle)], axis=1)
    return (cosines, sines)


def rotate(values, cosines, sines):
    half = values.shape[-1] // 2
    turned = jnp.concatenate([-values[..., half:], values[..., :half]], axis=-1)
    return values * cosines + turned * sines


def unrotate(grads, cosines, sines):
    half = grads.shape[-1] // 2
    scaled = grads * sines
    return grads * cosines + jnp.concatenate([scaled[..., half:], -scaled[..., :half]], axis=-1)


def head_norm_back(d_normed, raw_values, inverse, gain):
    scaled = d_normed * gain
    gain_part = jnp.sum(d_normed * raw_values * inverse, axis=(0, 1))
    d_raw = inverse * scaled - raw_values * inverse**3 * jnp.mean(
        scaled * raw_values, axis=-1, keepdims=True
    )
    return (d_raw, gain_part)


def across_features(values):
    return lax.psum(values, "row")


def gather_tokens(values):
    return lax.all_gather(values, "col", axis=0, tiled=True)


def gather_blocks(values):
    return lax.all_gather(values, "row", axis=0, tiled=True)


def reduce_rows(term, rows):
    return lax.psum_scatter(
        term(jnp.int32(0), lax.axis_size("row") * rows), "row", scatter_dimension=0, tiled=True
    )


def reduce_cols(term, rows):
    return lax.psum_scatter(
        term(jnp.int32(0), lax.axis_size("col") * rows).astype(jnp.bfloat16),
        "col",
        scatter_dimension=0,
        tiled=True,
    ).astype(jnp.float32)


def masked_scores(block_query, block_segment, block_place, key_rows, segment, place, scale):
    scores = (
        jnp.einsum("qkgd,skd->kgqs", block_query, key_rows, preferred_element_type=jnp.float32)
        * scale
    )
    allowed = (block_segment[:, None] == segment[None, :]) & (
        place[None, :] <= block_place[:, None]
    )
    return jnp.where(allowed, scores, NEGATIVE)


def body(
    tokens,
    lengths,
    norm_gain,
    w_query,
    w_key,
    w_value,
    w_head_gate,
    query_gain,
    key_gain,
    w_out,
    ffn_gain,
    w_gate,
    w_up,
    w_down,
    grad_out,
):
    row_count = lax.axis_size("row")
    col_count = lax.axis_size("col")
    tok_dev, d_loc = tokens.shape
    group_tok = tok_dev * col_count
    bin_rows = group_tok // row_count
    head_dim = query_gain.shape[0]
    q_cols = w_query.shape[1]
    kv_cols = w_key.shape[1]
    heads_loc = q_cols // head_dim
    kv_loc = kv_cols // head_dim
    share = heads_loc // kv_loc
    width = d_loc * row_count
    ff_loc = w_gate.shape[1]
    scale = head_dim ** (-0.5)
    blocks = bin_rows // bin_rows
    row_at = lax.axis_index("row")
    position = jnp.arange(group_tok, dtype=jnp.int32)
    order = position % bin_rows * row_count + position // bin_rows
    inverse = position % row_count * bin_rows + position // row_count
    segment, place = places(lengths, group_tok)
    all_segment = segment[order]
    all_place = place[order]
    bin_segment = lax.dynamic_slice_in_dim(all_segment, row_at * bin_rows, bin_rows)
    bin_place = lax.dynamic_slice_in_dim(all_place, row_at * bin_rows, bin_rows)
    x_in = tokens.astype(jnp.float32)
    inverse_one = lax.rsqrt(across_features(jnp.sum(x_in * x_in, axis=1)) / width + EPS)
    normed_one = (x_in * inverse_one[:, None] * norm_gain).astype(jnp.bfloat16)
    gathered_one = gather_tokens(normed_one)
    permuted = gathered_one[order]
    w_first = jnp.concatenate([w_query, w_key, w_value, w_head_gate], axis=1)

    def first_term(start, row_total):
        return jnp.dot(permuted, w_first, preferred_element_type=jnp.float32)

    projected = reduce_rows(first_term, bin_rows)
    raw_query = projected[:, :q_cols].reshape(bin_rows, heads_loc, head_dim)
    raw_key = projected[:, q_cols : q_cols + kv_cols].reshape(bin_rows, kv_loc, head_dim)
    raw_value = projected[:, q_cols + kv_cols : q_cols + 2 * kv_cols].reshape(
        bin_rows, kv_loc, head_dim
    )
    logit = projected[:, q_cols + 2 * kv_cols :]
    query_inverse = lax.rsqrt(jnp.mean(raw_query * raw_query, axis=-1, keepdims=True) + EPS)
    key_inverse = lax.rsqrt(jnp.mean(raw_key * raw_key, axis=-1, keepdims=True) + EPS)
    cosines, sines = rope_tables(bin_place, head_dim)
    cos_heads = cosines[:, None, :]
    sin_heads = sines[:, None, :]
    query = rotate(raw_query * query_inverse * query_gain, cos_heads, sin_heads).astype(
        jnp.bfloat16
    )
    key_local = rotate(raw_key * key_inverse * key_gain, cos_heads, sin_heads).astype(jnp.bfloat16)
    value_local = raw_value.astype(jnp.bfloat16)
    key_rows, value_rows = (
        lax.all_gather(key_local, "row", axis=0, tiled=True),
        lax.all_gather(value_local, "row", axis=0, tiled=True),
    )
    query_blocks = query.reshape(blocks, bin_rows, kv_loc, share, head_dim)
    segment_blocks = bin_segment.reshape(blocks, bin_rows)
    place_blocks = bin_place.reshape(blocks, bin_rows)

    def forward_block(item):
        block_query, block_segment, block_place = item
        scores = masked_scores(
            block_query, block_segment, block_place, key_rows, all_segment, all_place, scale
        )
        top_score = jnp.max(scores, axis=-1, keepdims=True)
        raised = jnp.exp(scores - top_score)
        total = jnp.sum(raised, axis=-1, keepdims=True)
        probs = (raised / total).astype(jnp.bfloat16)
        result = jnp.einsum("kgqs,skd->qkgd", probs, value_rows, preferred_element_type=jnp.float32)
        return (result, top_score[..., 0] + jnp.log(total[..., 0]))

    attended_blocks, logsum_blocks = lax.map(
        forward_block, (query_blocks, segment_blocks, place_blocks)
    )
    attended = attended_blocks.reshape(bin_rows, heads_loc, head_dim)
    gate_sigmoid = jax.nn.sigmoid(logit)
    gated = (attended * gate_sigmoid[:, :, None]).reshape(bin_rows, q_cols).astype(jnp.bfloat16)
    gathered_gated = gather_blocks(gated)

    def out_term(start, row_total):
        return jnp.dot(gathered_gated[inverse], w_out, preferred_element_type=jnp.float32)

    attn_branch = reduce_cols(out_term, tok_dev)
    resid = x_in + attn_branch
    inverse_two = lax.rsqrt(across_features(jnp.sum(resid * resid, axis=1)) / width + EPS)
    normed_two = (resid * inverse_two[:, None] * ffn_gain).astype(jnp.bfloat16)
    gathered_two = gather_tokens(normed_two)
    w_pair = jnp.concatenate([w_gate, w_up], axis=1)
    pair_value = lax.psum_scatter(
        jnp.dot(gathered_two, w_pair, preferred_element_type=jnp.float32).astype(jnp.bfloat16),
        "row",
        scatter_dimension=0,
        tiled=True,
    ).astype(jnp.float32)
    gate_part = pair_value[:, :ff_loc]
    up_part = pair_value[:, ff_loc:]
    gate_sig = jax.nn.sigmoid(gate_part)
    silu_part = gate_part * gate_sig
    inner = (silu_part * up_part).astype(jnp.bfloat16)
    gathered_inner = gather_blocks(inner)

    def down_term(start, row_total):
        return jnp.dot(gathered_inner, w_down, preferred_element_type=jnp.float32)

    branch = reduce_cols(down_term, tok_dev)
    output = (resid + branch).astype(jnp.bfloat16)
    d_top = grad_out.astype(jnp.float32)
    gathered_grad = gather_tokens(grad_out)
    grad_down = jnp.einsum(
        "tf,td->fd", gathered_inner, gathered_grad, preferred_element_type=jnp.float32
    )

    def inner_term(start, row_total):
        return jnp.einsum("td,fd->tf", gathered_grad, w_down, preferred_element_type=jnp.float32)

    d_inner = reduce_rows(inner_term, bin_rows)
    d_gate = d_inner * up_part * (gate_sig * (1.0 + gate_part * (1.0 - gate_sig)))
    d_up = d_inner * silu_part
    d_pair = jnp.concatenate([d_gate, d_up], axis=1).astype(jnp.bfloat16)
    gathered_pair = lax.all_gather(d_pair, "row", axis=0, tiled=True)
    whole_grad = jnp.einsum(
        "td,tf->df", gathered_two, gathered_pair, preferred_element_type=jnp.float32
    )
    grad_gate = whole_grad[:, :ff_loc]
    grad_up = whole_grad[:, ff_loc:]

    def norm_term(start, row_total):
        return jnp.einsum("tf,df->td", gathered_pair, w_pair, preferred_element_type=jnp.float32)

    d_normed_two = reduce_cols(norm_term, tok_dev)
    ffn_gain_part = jnp.sum(d_normed_two * resid * inverse_two[:, None], axis=0)
    scaled_two = d_normed_two * ffn_gain
    inner_two = across_features(jnp.sum(scaled_two * resid, axis=1))
    d_resid = (
        d_top
        + inverse_two[:, None] * scaled_two
        - resid * (inverse_two**3 * inner_two / width)[:, None]
    )
    d_branch = d_resid.astype(jnp.bfloat16)
    gathered_branch = gather_tokens(d_branch)
    permuted_branch = gathered_branch[order]
    grad_out_w = jnp.einsum(
        "tq,td->qd", gathered_gated, permuted_branch, preferred_element_type=jnp.float32
    )

    def gated_term(start, row_total):
        return jnp.einsum("td,qd->tq", permuted_branch, w_out, preferred_element_type=jnp.float32)

    d_gated = reduce_rows(gated_term, bin_rows).reshape(bin_rows, heads_loc, head_dim)
    d_attended = (d_gated * gate_sigmoid[:, :, None]).astype(jnp.bfloat16)
    d_logit = jnp.sum(d_gated * attended, axis=-1) * gate_sigmoid * (1.0 - gate_sigmoid)
    d_attended_blocks = d_attended.reshape(blocks, bin_rows, kv_loc, share, head_dim)

    def backward_block(carry, item):
        d_key_sum, d_value_sum = carry
        block_query, block_segment, block_place, block_grad, block_logsum = item
        scores = masked_scores(
            block_query, block_segment, block_place, key_rows, all_segment, all_place, scale
        )
        probs = jnp.exp(scores - block_logsum[..., None])
        d_probs = jnp.einsum(
            "qkgd,skd->kgqs", block_grad, value_rows, preferred_element_type=jnp.float32
        )
        d_scores = (probs * (d_probs - jnp.sum(d_probs * probs, axis=-1, keepdims=True))).astype(
            jnp.bfloat16
        )
        d_query_block = (
            jnp.einsum("kgqs,skd->qkgd", d_scores, key_rows, preferred_element_type=jnp.float32)
            * scale
        )
        d_key_sum = (
            d_key_sum
            + jnp.einsum(
                "kgqs,qkgd->skd", d_scores, block_query, preferred_element_type=jnp.float32
            )
            * scale
        )
        d_value_sum = d_value_sum + jnp.einsum(
            "kgqs,qkgd->skd",
            probs.astype(jnp.bfloat16),
            block_grad,
            preferred_element_type=jnp.float32,
        )
        return ((d_key_sum, d_value_sum), d_query_block)

    zero_rows = jnp.zeros((group_tok, kv_loc, head_dim), jnp.float32)
    (d_key_all, d_value_all), d_query_blocks = lax.scan(
        backward_block,
        (zero_rows, zero_rows),
        (query_blocks, segment_blocks, place_blocks, d_attended_blocks, logsum_blocks),
    )
    d_keys, d_values = (
        lax.psum_scatter(
            d_key_all.astype(jnp.bfloat16), "row", scatter_dimension=0, tiled=True
        ).astype(jnp.float32),
        lax.psum_scatter(
            d_value_all.astype(jnp.bfloat16), "row", scatter_dimension=0, tiled=True
        ).astype(jnp.float32),
    )
    d_query = d_query_blocks.reshape(bin_rows, heads_loc, head_dim)
    d_raw_query, query_gain_part = head_norm_back(
        unrotate(d_query, cos_heads, sin_heads), raw_query, query_inverse, query_gain
    )
    d_raw_key, key_gain_part = head_norm_back(
        unrotate(d_keys, cos_heads, sin_heads), raw_key, key_inverse, key_gain
    )
    d_projected = jnp.concatenate(
        [
            d_raw_query.reshape(bin_rows, q_cols),
            d_raw_key.reshape(bin_rows, kv_cols),
            d_values.reshape(bin_rows, kv_cols),
            d_logit,
        ],
        axis=1,
    ).astype(jnp.bfloat16)
    gathered_first = gather_blocks(d_projected)
    grad_first = jnp.einsum(
        "td,tc->dc", permuted, gathered_first, preferred_element_type=jnp.float32
    )

    def first_back_term(start, row_total):
        return jnp.einsum(
            "tc,dc->td", gathered_first[inverse], w_first, preferred_element_type=jnp.float32
        )

    d_normed_one = reduce_cols(first_back_term, tok_dev)
    norm_gain_part = jnp.sum(d_normed_one * x_in * inverse_one[:, None], axis=0)
    scaled_one = d_normed_one * norm_gain
    inner_one = across_features(jnp.sum(scaled_one * x_in, axis=1))
    input_grad = (
        d_resid
        + inverse_one[:, None] * scaled_one
        - x_in * (inverse_one**3 * inner_one / width)[:, None]
    )
    grad_norm_gain, grad_ffn_gain = lax.psum((norm_gain_part, ffn_gain_part), ("group", "col"))
    grad_query_gain, grad_key_gain = lax.psum(
        (query_gain_part, key_gain_part), ("group", "row", "col")
    )
    grad_query = grad_first[:, :q_cols]
    grad_key = grad_first[:, q_cols : q_cols + kv_cols]
    grad_value = grad_first[:, q_cols + kv_cols : q_cols + 2 * kv_cols]
    grad_head_gate = grad_first[:, q_cols + 2 * kv_cols :]
    summed = (
        lax.psum(grad_query.astype(jnp.bfloat16), "group").astype(jnp.float32),
        lax.psum(grad_key.astype(jnp.bfloat16), "group").astype(jnp.float32),
        lax.psum(grad_value.astype(jnp.bfloat16), "group").astype(jnp.float32),
        lax.psum(grad_head_gate.astype(jnp.bfloat16), "group").astype(jnp.float32),
        lax.psum(grad_out_w.astype(jnp.bfloat16), "group").astype(jnp.float32),
        lax.psum(grad_gate.astype(jnp.bfloat16), "group").astype(jnp.float32),
        lax.psum(grad_up.astype(jnp.bfloat16), "group").astype(jnp.float32),
        lax.psum(grad_down.astype(jnp.bfloat16), "group").astype(jnp.float32),
    )
    return (
        output,
        input_grad,
        grad_norm_gain,
        summed[0],
        summed[1],
        summed[2],
        summed[3],
        grad_query_gain,
        grad_key_gain,
        summed[4],
        grad_ffn_gain,
        summed[5],
        summed[6],
        summed[7],
    )


def solution(mesh):
    in_specs = (
        P(("group", "col"), "row"),
        P("group"),
        P("row"),
        P("row", "col"),
        P("row", "col"),
        P("row", "col"),
        P("row", "col"),
        P(),
        P(),
        P("col", "row"),
        P("row"),
        P("row", "col"),
        P("row", "col"),
        P("col", "row"),
        P(("group", "col"), "row"),
    )
    out_specs = (
        P(("group", "col"), "row"),
        P(("group", "col"), "row"),
        P("row"),
        P("row", "col"),
        P("row", "col"),
        P("row", "col"),
        P("row", "col"),
        P(),
        P(),
        P("col", "row"),
        P("row"),
        P("row", "col"),
        P("row", "col"),
        P("col", "row"),
    )
    return jax.shard_map(body, mesh=mesh, in_specs=in_specs, out_specs=out_specs, check_vma=False)
```

profile of v0, /device:TPU:24, one launch (start us, length us, event | category | flops | bytes accessed | tf_op | source)
XLA Modules:
  0.0 1668.9 jit_solution(9687963277787072502)
XLA Ops:
  17.4 9.9 all-gather.9.cloned.1.call-done
  50.8 60.7 %reduce-scatter.28.cloned.1.call-done = f32[320,2056]{1,0:T(8,128)} async-done(((f32[640,2056]{1,0:T(8,128)}), f32[320,2056]{1,0:T(8,128)}) %reduce-scatter.28.cloned.1.call-update) | async-done | bytes 2631696 | tf_op jit(solution)/shard_map/reduce_scatter | solution.py:63
  132.6 10.8 all_gather.31
  147.3 10.1 all_gather.32
  184.1 25.3 %all-gather.11.cloned.1.call-done = bf16[640,1024]{1,0:T(8,128)(2,1)} async-done(((bf16[320,1024]{1,0:T(8,128)(2,1)}), bf16[640,1024]{1,0:T(8,128)(2,1)}) %all-gather.11.cloned.1.call-update) | async-done | bytes 1310736 | tf_op jit(solution)/shard_map/all_gather | solution.py:59
  250.1 15.2 convolution_convert_fusion.1
  265.4 10.7 fusion.84
  276.1 84.4 %reduce-scatter.14.cloned.1.call-done = bf16[320,6144]{1,0:T(8,128)(2,1)} async-done(((bf16[640,6144]{1,0:T(8,128)(2,1)}), bf16[320,6144]{1,0:T(8,128)(2,1)}) %reduce-scatter.14.cloned.1.call-update) | async-done | bytes 3932176 | tf_op jit(solution)/shard_map/reduce_scatter | solution.py:193
  366.8 90.8 %reduce-scatter.18.cloned.1.call-done = f32[320,3072]{1,0:T(8,128)} async-done(((f32[640,3072]{1,0:T(8,128)}), f32[320,3072]{1,0:T(8,128)}) %reduce-scatter.18.cloned.1.call-update) | async-done | bytes 3932176 | tf_op jit(solution)/shard_map/reduce_scatter | solution.py:63
  466.7 98.0 %all-gather.19.cloned.1.call-done = bf16[640,6144]{1,0:T(8,128)(2,1)} async-done(((bf16[320,6144]{1,0:T(8,128)(2,1)}), bf16[640,6144]{1,0:T(8,128)(2,1)}) %all-gather.19.cloned.1.call-update) | async-done | bytes 7864336 | tf_op jit(solution)/shard_map/all_gather | solution.py:224
  564.7 14.4 convolution_convert_fusion.6
  598.0 10.7 all-gather.21.cloned.1.call-done
  625.4 32.3 %reduce-scatter.22.cloned.1.call-done = f32[320,1024]{1,0:T(8,128)} async-done(((f32[640,1024]{1,0:T(8,128)}), f32[320,1024]{1,0:T(8,128)}) %reduce-scatter.22.cloned.1.call-update) | async-done | bytes 1310736 | tf_op jit(solution)/shard_map/reduce_scatter | solution.py:63
  709.5 12.1 reduce-scatter.24.cloned.1.call-done
  727.4 40.4 %all-gather.23.cloned.1.call-done = bf16[640,2056]{1,0:T(8,128)(2,1)} async-done(((bf16[320,2056]{1,0:T(8,128)(2,1)}), bf16[640,2056]{1,0:T(8,128)(2,1)}) %all-gather.23.cloned.1.call-update) | async-done | bytes 2631696 | tf_op jit(solution)/shard_map/all_gather | solution.py:59
  767.8 9.3 gather_fusion.5
  784.9 38.7 %all-gather.15.cloned.1.call-done = bf16[640,3072]{1,0:T(8,128)(2,1)} async-done(((bf16[320,3072]{1,0:T(8,128)(2,1)}), bf16[640,3072]{1,0:T(8,128)(2,1)}) %all-gather.15.cloned.1.call-update) | async-done | bytes 3932176 | tf_op jit(solution)/shard_map/all_gather | solution.py:59
  833.2 9.6 convolution_convert_fusion.2
  842.8 14.4 convolution_convert_fusion
  873.5 41.7 %all-reduce.1 = (f32[128]{0:T(128)}, f32[128]{0:T(128)}) all-reduce(f32[128]{0:T(128)S(1)} %bitcast_reduce_fusion, f32[128]{0:T(128)S(1)} %get-tuple-element.197), channel_id=1, replica_groups=mesh['group'=8,'row'=2,'col'=2] {'group','row','col'}, use_global_device_ids=true, to_apply=%region_37.38 | all-reduce | flops 256 | bytes 2048 | tf_op jit(solution)/shard_map/psum | solution.py:340
  915.2 36.8 %psum.120 = bf16[1024,8]{0,1:T(8,128)(2,1)S(1)} all-reduce(bf16[1024,8]{0,1:T(8,128)(2,1)S(1)} %slice-done.6), channel_id=1, replica_groups=mesh['group'=8,'row'=2,'col'=2] {'group'}, use_global_device_ids=true, to_apply=%region_34.35 | all-reduce | flops 8192 | bytes 32768 | tf_op jit(solution)/shard_map/psum | solution.py:351
  959.1 31.1 %all-reduce.2 = (f32[1024]{0:T(1024)}, f32[1024]{0:T(1024)}) all-reduce(f32[1024]{0:T(1024)S(1)} %get-tuple-element.199, f32[1024]{0:T(1024)S(1)} %get-tuple-element.195), channel_id=1, replica_groups=mesh['group'=8,'row'=2,'col'=2] {'group','col'}, use_global_device_ids=true, to_apply=%region_30.31 | all-reduce | flops 2048 | bytes 16384 | tf_op jit(solution)/shard_map/psum | solution.py:339
  993.8 635.2 %all-reduce.9.cloned.1.call-done = (bf16[1024,1024]{0,1:T(8,128)(2,1)}, bf16[1024,512]{0,1:T(8,128)(2,1)}, bf16[1024,512]{0,1:T(8,128)(2,1)}, bf16[1024,1024]{1,...) async-done(((bf16[1024,1024]{0,1:T(8,128)(2,1)}, bf16[1024,512]{0,1:T(8,128)(2,1)}, ...) | async-done | bytes 25165840 | tf_op jit(solution)/shard_map/psum | solution.py:348
  1639.8 9.4 convert_element_type.179
  (321 shorter events, 301.2 us)
Async XLA Ops:
  7.2 208.1 %copy-start = (bf16[1024,1024]{1,0:T(8,128)(2,1)S(1)}, bf16[1024,1024]{1,0:T(8,128)(2,1)}, u32[]{:S(2)}) copy-start(bf16[1024,1024]{1,0:T(8,128)(2,1)} %param.24) | copy-start | bytes 6291460
  7.2 20.0 %all-gather.9.cloned.1.call-start = ((), (), s32[]{:S(2)}) async-start(), calls=%async_computation.9 | async-start | bytes 1966080 | tf_op jit(solution)/shard_map/all_gather | solution.py:55
  16.4 95.0 %reduce-scatter.28.cloned.1.call-start = ((), (), s32[]{:S(2)}) async-start(), calls=%async_computation.25 | async-start | bytes 8355840 | tf_op jit(solution)/shard_map/reduce_scatter | solution.py:63
  41.1 168.3 %all-gather.11.cloned.1.call-start = ((), (), s32[]{:S(2)}) async-start(), calls=%async_computation.10 | async-start | bytes 1966080 | tf_op jit(solution)/shard_map/all_gather | solution.py:59
  184.0 44.4 %reduce-scatter.12.cloned.1.call-start = ((), (), s32[]{:S(2)}) async-start(), calls=%async_computation.11 | async-start | bytes 1966080 | tf_op jit(solution)/shard_map/reduce_scatter | solution.py:69
  219.2 30.8 %all-gather.13.cloned.1.call-start = ((), (), s32[]{:S(2)}) async-start(), calls=%async_computation.12 | async-start | bytes 1966080 | tf_op jit(solution)/shard_map/all_gather | solution.py:55
  237.0 28.4 %all-gather.17.cloned.1.call-start = ((), (), s32[]{:S(2)}) async-start(), calls=%async_computation.16 | async-start | bytes 1966080 | tf_op jit(solution)/shard_map/all_gather | solution.py:55
  237.6 122.9 %reduce-scatter.14.cloned.1.call-start = ((), (), s32[]{:S(2)}) async-start(), calls=%async_computation.13 | async-start | bytes 11796480 | tf_op jit(solution)/shard_map/reduce_scatter | solution.py:193
  265.3 192.2 %reduce-scatter.18.cloned.1.call-start = ((), (), s32[]{:S(2)}) async-start(), calls=%async_computation.17 | async-start | bytes 11796480 | tf_op jit(solution)/shard_map/reduce_scatter | solution.py:63
  276.1 288.6 %all-gather.19.cloned.1.call-start = ((), (), s32[]{:S(2)}) async-start(), calls=%async_computation.18 | async-start | bytes 11796480 | tf_op jit(solution)/shard_map/all_gather | solution.py:224
  466.5 121.9 %reduce-scatter.20.cloned.1.call-start = ((), (), s32[]{:S(2)}) async-start(), calls=%async_computation.19 | async-start | bytes 1966080 | tf_op jit(solution)/shard_map/reduce_scatter | solution.py:69
  579.2 29.5 %all-gather.21.cloned.1.call-start = ((), (), s32[]{:S(2)}) async-start(), calls=%async_computation.20 | async-start | bytes 1966080 | tf_op jit(solution)/shard_map/all_gather | solution.py:55
  598.0 59.7 %reduce-scatter.22.cloned.1.call-start = ((), (), s32[]{:S(2)}) async-start(), calls=%async_computation.21 | async-start | bytes 3932160 | tf_op jit(solution)/shard_map/reduce_scatter | solution.py:63
  619.0 88.6 %all-reduce.7.cloned.1.call-start = ((), (), s32[]{:S(2)}) async-start(), calls=%async_computation.26 | async-start | bytes 1310720
  671.3 50.3 %reduce-scatter.24.cloned.1.call-start = ((), (), s32[]{:S(2)}) async-start(), calls=%async_computation.22 | async-start | bytes 983040 | tf_op jit(solution)/shard_map/reduce_scatter | solution.py:297
  694.2 73.5 %all-gather.23.cloned.1.call-start = ((), (), s32[]{:S(2)}) async-start(), calls=%async_computation.23 | async-start | bytes 4177920 | tf_op jit(solution)/shard_map/all_gather | solution.py:59
  726.7 96.9 %all-gather.15.cloned.1.call-start = ((), (), s32[]{:S(2)}) async-start(), calls=%async_computation.14 | async-start | bytes 5898240 | tf_op jit(solution)/shard_map/all_gather | solution.py:59
  727.3 225.3 %reduce-scatter.26.cloned.1.call-start = ((), (), s32[]{:S(2)}) async-start(), calls=%async_computation.24 | async-start | bytes 1966080 | tf_op jit(solution)/shard_map/reduce_scatter | solution.py:69
  784.9 205.4 %reduce-scatter.16.cloned.1.call-start = ((), (), s32[]{:S(2)}) async-start(), calls=%async_computation.15 | async-start | bytes 1966080 | tf_op jit(solution)/shard_map/reduce_scatter | solution.py:69
  832.9 796.1 %all-reduce.9.cloned.1.call-start = ((), (), s32[]{:S(2)}) async-start(), calls=%async_computation.27 | async-start | bytes 50331648 | tf_op jit(solution)/shard_map/psum | solution.py:348
  873.4 116.8 %copy-start.56 = (f32[320]{0:T(512)S(1)}, f32[320]{0:T(512)}, u32[]{:S(2)}) copy-start(f32[320]{0:T(512)} %copy-done.55) | copy-start | bytes 3844
  873.4 116.9 %copy-start.18 = (bf16[320,1024]{1,0:T(8,128)(2,1)S(1)}, bf16[320,1024]{1,0:T(8,128)(2,1)}, u32[]{:S(2)}) copy-start(bf16[320,1024]{1,0:T(8,128)(2,1)} %reduce-scatter.20.cloned.1.call-done) | copy-start | bytes 1966084
  873.4 116.9 %copy-start.10 = (bf16[320,1024]{1,0:T(8,128)(2,1)S(1)}, bf16[320,1024]{1,0:T(8,128)(2,1)}, u32[]{:S(2)}) copy-start(bf16[320,1024]{1,0:T(8,128)(2,1)} %reduce-scatter.12.cloned.1.call-done) | copy-start | bytes 1966084
  873.4 116.9 %copy-start.17 = (bf16[320,1024]{1,0:T(8,128)(2,1)S(1)}, bf16[320,1024]{1,0:T(8,128)(2,1)}, u32[]{:S(2)}) copy-start(bf16[320,1024]{1,0:T(8,128)(2,1)} %param.29) | copy-start | bytes 1966084
  (66 other events, 595.1 us)
Sparse Core Ops, SparseCore 0:
  16.5 10.6 all-gather.8
  41.2 70.1 reduce-scatter.27
  184.1 25.1 all-gather.10
  219.4 9.0 reduce-scatter.11
  237.1 10.5 all-gather.12
  249.2 10.5 all-gather.16
  265.4 95.0 reduce-scatter.13
  363.4 94.1 reduce-scatter.17
  466.6 98.1 all-gather.18
  579.3 9.0 reduce-scatter.19
  598.1 10.5 all-gather.20
  619.2 38.4 reduce-scatter.21
  671.4 31.4 all-reduce.6
  705.6 15.9 reduce-scatter.23
  726.8 40.8 all-gather.22
  769.8 53.7 all-gather.14
  826.4 9.0 reduce-scatter.25
  838.2 9.9 reduce-scatter.15
  873.5 755.4 all-reduce.8
where the time goes:
time: 1680 us; the launch traced here: 1670 us
  waiting for transfers between devices  1160 us (69%)
  blocking collectives  150 us (9%)
  local copies, waits for them, and re-layouts  131 us (8%)
  matrix products  123 us (7%)
  other arithmetic  88.9 us (5%)
    psum x1, waiting for transfers between devices, body(): lax.psum(grad_query.astype(jnp.bfloat16), 'group').astype(jnp.float32)  635 us
    reduce_scatter x3, waiting for transfers between devices, reduce_rows(): lax.psum_scatter(term(jnp.int32(0), lax.axis_size('row') * rows), 'row',...  184 us
    all_gather x3, waiting for transfers between devices, gather_blocks(): return lax.all_gather(values, 'row', axis=0, tiled=True)  104 us
    all_gather x1, waiting for transfers between devices, body(): gathered_pair = lax.all_gather(d_pair, 'row', axis=0, tiled=True)  98 us
    reduce_scatter x1, waiting for transfers between devices, body(): lax.psum_scatter(jnp.dot(gathered_two, w_pair, preferred_element_type=jnp...  84.4 us
    psum x1, blocking collectives, body(): lax.psum((query_gain_part, key_gain_part), ('group', 'row', 'col'))  41.7 us
    psum x1, blocking collectives, body(): lax.psum(grad_head_gate.astype(jnp.bfloat16), 'group').astype(jnp.float32)  36.8 us
  transfers between devices with their start and end apart: 19, of which 14 were waited for; matrix products, arithmetic and copies ran while one was open for 10% of the time, Pallas kernels for 0%

commit v1 on v0

v1 whole, which is shorter than its diff:
```python
import functools

import jax
import jax.numpy as jnp
from jax import lax
from jax.experimental import pallas as pl
from jax.experimental.pallas import tpu as pltpu
from jax.sharding import PartitionSpec as P

EPS = 1e-06
THETA = 1000000.0
NEGATIVE = -1e30
MESH = pl.DeviceIdType.MESH
F32 = jnp.float32
BF16 = jnp.bfloat16


def swap(values, axis):
    return lax.ppermute(values, axis, [(0, 1), (1, 0)])


def swap_groups(values):
    count = lax.axis_size("group")
    return lax.ppermute(values, "group", [(i, i ^ 1) for i in range(count)])


def halves(values, axis, at):
    low, high = jnp.split(values, 2, axis=axis)
    first = at == 0
    return jnp.where(first, low, high), jnp.where(first, high, low)


def ordered(own, other, axis, at):
    first = at == 0
    return jnp.concatenate(
        [jnp.where(first, own, other), jnp.where(first, other, own)], axis=axis
    )


def places(lengths_group, index):
    ends = jnp.cumsum(lengths_group)
    passed = (index[:, None] >= ends[None, :]).astype(jnp.int32)
    segment = jnp.sum(passed, axis=1)
    place = index - jnp.sum(passed * lengths_group[None, :], axis=1)
    return (segment, place)


def rope_tables(place, width):
    half = width // 2
    freq = THETA ** (-(jnp.arange(half, dtype=F32) * 2.0 / width))
    angle = place.astype(F32)[:, None] * freq[None, :]
    cosines = jnp.concatenate([jnp.cos(angle), jnp.cos(angle)], axis=1)
    sines = jnp.concatenate([jnp.sin(angle), jnp.sin(angle)], axis=1)
    return (cosines, sines)


def rotate(values, cosines, sines):
    half = values.shape[-1] // 2
    turned = jnp.concatenate([-values[..., half:], values[..., :half]], axis=-1)
    return values * cosines + turned * sines


def unrotate(grads, cosines, sines):
    half = grads.shape[-1] // 2
    scaled = grads * sines
    return grads * cosines + jnp.concatenate([scaled[..., half:], -scaled[..., :half]], axis=-1)


def head_norm_back(d_normed, raw_values, inverse, gain):
    scaled = d_normed * gain
    gain_part = jnp.sum(d_normed * raw_values * inverse, axis=(0, 1))
    d_raw = inverse * scaled - raw_values * inverse**3 * jnp.mean(
        scaled * raw_values, axis=-1, keepdims=True
    )
    return (d_raw, gain_part)


TILE = 256


def nt(a, b):
    return lax.dot_general(a, b, (((1,), (1,)), ((), ())), preferred_element_type=F32)


def nn(a, b):
    return jnp.dot(a, b, preferred_element_type=F32)


def ffn_kernel(
    count, chunks, h_ref, goal_ref, inner_grad_ref, gate_ref, up_ref, down_ref,
    grads_ref, low_ref, high_ref, branch_ref, back_ref,
    h_all, h_turned, sent, came, w_pair, w_down, acc_branch, acc_back, parts, total,
    stage, reduce_recv,
    gather_send, gather_recv, x_send, x_recv, chain_send, low_recv, high_recv,
    final_up, final_down, final_recv, pass_send, pass_recv, load_sem, weight_sem, keep_sem, fold_send, fold_recv,
):
    rows = h_ref.shape[0]
    tokens = h_all.shape[0]
    tiles = tokens // TILE
    width = h_ref.shape[1]
    wide = w_down.shape[0] // chunks
    line = count // 2
    root = (line - 1) // 2
    root_lag = max(root, line - 1 - root)
    group = lax.axis_index("group")
    at = group // 2
    side = group % 2
    x_peer = {"row": 1 - lax.axis_index("row")}
    core_peer = {"col": 1 - lax.axis_index("col")}
    y_peer = {"group": group + 1 - 2 * side}
    above = {"group": jnp.minimum(group + 2, count - 1)}
    below = {"group": jnp.maximum(group - 2, 0)}
    has_above = at < line - 1
    has_below = at > 0

    def weight_copies(j):
        cols = pl.ds(pl.multiple_of(side * wide * chunks + j * wide, wide), wide)
        mine = pl.ds(pl.multiple_of(j * wide, wide), wide)
        return (
            pltpu.make_async_copy(
                gate_ref.at[:, cols], w_pair.at[j, :, pl.ds(0, wide)], weight_sem.at[0, j]
            ),
            pltpu.make_async_copy(
                up_ref.at[:, cols], w_pair.at[j, :, pl.ds(wide, wide)], weight_sem.at[1, j]
            ),
            pltpu.make_async_copy(down_ref.at[cols, :], w_down.at[mine, :], weight_sem.at[2, j]),
        )

    @pl.loop(0, chunks)
    def _(j):
        for copy in weight_copies(j):
            copy.start()

    barrier = pltpu.get_barrier_semaphore()
    for peer in (x_peer, core_peer, y_peer):
        pl.semaphore_signal(barrier, inc=1, device_id=peer, device_id_type=MESH)

    @pl.when(has_above)
    def _():
        pl.semaphore_signal(barrier, inc=1, device_id=above, device_id_type=MESH)

    @pl.when(has_below)
    def _():
        pl.semaphore_signal(barrier, inc=1, device_id=below, device_id_type=MESH)

    pl.semaphore_wait(barrier, 3 + has_above.astype(jnp.int32) + has_below.astype(jnp.int32))

    def slot(i):
        return pl.ds(i * rows, rows)

    def send(src, dst, s_sem, r_sem, peer):
        return pltpu.make_async_remote_copy(
            src_ref=src, dst_ref=dst, send_sem=s_sem, recv_sem=r_sem,
            device_id=peer, device_id_type=MESH,
        )

    to_y = send(h_ref, h_all.at[slot(2)], gather_send.at[0], gather_recv.at[0], y_peer)
    to_core = send(h_ref, h_all.at[slot(1)], gather_send.at[1], gather_recv.at[1], core_peer)
    forward = send(
        h_all.at[slot(2)], h_all.at[slot(3)], gather_send.at[2], gather_recv.at[2], core_peer
    )
    to_y.start()
    to_core.start()
    h_all[slot(0), :] = h_ref[...]
    acc_branch[...] = jnp.zeros_like(acc_branch)
    acc_back[...] = jnp.zeros_like(acc_back)
    to_y.wait_recv()
    forward.start()
    to_core.wait_recv()
    forward.wait_recv()

    def exchange(j):
        return send(
            sent.at[lax.rem(j, 3)], came.at[j], x_send.at[j], x_recv.at[j], x_peer
        )

    def project(j):
        for copy in weight_copies(j):
            copy.wait()

        @pl.loop(0, tiles)
        def _(i):
            at_rows = pl.ds(pl.multiple_of(i * TILE, TILE), TILE)
            sent[lax.rem(j, 3), at_rows, :] = nn(h_all[at_rows, :], w_pair[j]).astype(BF16)

        exchange(j).start()

    def work(j):
        exchange(j).wait_recv()
        mine = pl.ds(pl.multiple_of(j * wide, wide), wide)

        @pl.loop(0, tiles)
        def _(i):
            at_rows = pl.ds(pl.multiple_of(i * TILE, TILE), TILE)
            pair = sent[lax.rem(j, 3), at_rows, :].astype(F32) + came[j, at_rows, :].astype(F32)
            gate, up = pair[:, :wide], pair[:, wide:]
            grad = inner_grad_ref[at_rows, mine].astype(F32)
            sig = 1.0 / (1.0 + jnp.exp(-gate))
            silu = gate * sig
            parts[at_rows, pl.ds(0, wide)] = (
                grad * up * (sig * (1.0 + gate * (1.0 - sig)))
            ).astype(BF16)
            parts[at_rows, pl.ds(wide, wide)] = (grad * silu).astype(BF16)
            parts[at_rows, pl.ds(2 * wide, wide)] = (silu * up).astype(BF16)
            acc_branch[at_rows, :] += nn(parts[at_rows, pl.ds(2 * wide, wide)], w_down[mine, :])
            acc_back[at_rows, :] += nt(parts[at_rows, pl.ds(0, 2 * wide)], w_pair[j])

        @pl.loop(0, width // TILE)
        def _(i):
            at_rows = pl.ds(pl.multiple_of(i * TILE, TILE), TILE)
            pair = nn(h_turned[at_rows, :], parts[:, pl.ds(0, 2 * wide)])
            total[3 * j, at_rows, :] = pair[:, :wide].astype(BF16)
            total[3 * j + 1, at_rows, :] = pair[:, wide:].astype(BF16)
            total[3 * j + 2, at_rows, :] = nn(
                goal_ref[at_rows, :], parts[:, pl.ds(2 * wide, wide)]
            ).astype(BF16)

    def up_copy(p):
        return send(total.at[p], low_ref.at[p], chain_send.at[p], low_recv.at[p], above)

    def down_copy(p):
        return send(total.at[p], high_ref.at[p], chain_send.at[p], high_recv.at[p], below)

    def home(c, k, of=side):
        start = pl.multiple_of((of * chunks + c) * wide, wide)
        return grads_ref.at[k, :, pl.ds(start, wide)]

    def to_pair(c, k, from_total):
        p = 3 * c + k
        src = total.at[p] if from_total else home(c, k)
        return send(src, home(c, k), pass_send.at[p], pass_recv.at[p], y_peer)

    def from_pair(c, k):
        p = 3 * c + k
        return send(
            home(c, k), home(c, k, 1 - side), pass_send.at[p], pass_recv.at[p], y_peer
        )

    def add(p, which):
        copy = pltpu.make_async_copy(
            (low_ref if which == 0 else high_ref).at[p], stage.at[which], load_sem.at[which]
        )
        copy.start()
        copy.wait()

        @pl.loop(0, width // TILE)
        def _(i):
            at_rows = pl.ds(pl.multiple_of(i * TILE, TILE), TILE)
            total[p, at_rows, :] = (
                total[p, at_rows, :].astype(F32) + stage[which, at_rows, :].astype(F32)
            ).astype(BF16)

    def keep(c, k):
        return pltpu.make_async_copy(total.at[3 * c + k], home(c, k), keep_sem.at[3 * c + k])

    def finals(c, k, upward, from_total):
        p = 3 * c + k
        src = total.at[p] if from_total else home(c, k)
        if upward:
            return send(src, home(c, k), final_up.at[p], final_recv.at[p], above)
        return send(src, home(c, k), final_down.at[p], final_recv.at[p], below)

    lag = jnp.where(at < root, at, jnp.where(at > root, line - 1 - at, root_lag))
    far = jnp.abs(at - root)

    def chain(t):
        c = t - lag
        live = (c >= 0) & (c < chunks)
        for k in range(3):
            p = 3 * c + k

            @pl.when(live & (at < root))
            def _():
                @pl.when(has_below)
                def _():
                    down_wait = up_copy(p)
                    down_wait.wait_recv()
                    add(p, 0)

                up_copy(p).start()

            @pl.when(live & (at > root))
            def _():
                @pl.when(has_above)
                def _():
                    down_copy(p).wait_recv()
                    add(p, 1)

                down_copy(p).start()

            @pl.when(live & (at == root))
            def _():
                if root > 0:
                    up_copy(p).wait_recv()
                    add(p, 0)
                if root < line - 1:
                    down_copy(p).wait_recv()
                    add(p, 1)
                if root > 0:
                    finals(c, k, False, True).start()
                if root < line - 1:
                    finals(c, k, True, True).start()
                to_pair(c, k, True).start()
                keep(c, k).start()

        c = t - root_lag - far
        for k in range(3):

            @pl.when((c >= 0) & (c < chunks) & (at != root))
            def _():
                finals(c, k, True, False).wait_recv()

                @pl.when((at > root) & has_above)
                def _():
                    finals(c, k, True, False).start()

                @pl.when((at < root) & has_below)
                def _():
                    finals(c, k, False, False).start()

                to_pair(c, k, False).start()

    for j in range(min(2, chunks)):
        project(j)

    @pl.loop(0, tiles)
    def _(i):
        at_rows = pl.ds(pl.multiple_of(i * TILE, TILE), TILE)
        h_turned[:, at_rows] = h_all[at_rows, :].T

    @pl.loop(0, chunks)
    def _(t):
        @pl.when(t + 2 < chunks)
        def _():
            @pl.when(t >= 1)
            def _():
                exchange(t - 1).wait_send()

            project(t + 2)

        work(t)
        chain(t)

    folded = ((acc_back, back_ref), (acc_branch, branch_ref))

    def fold_source(n, i):
        if i == 2:
            return w_down.at[slot(n), :]
        return h_all.at[slot(2 * n + i), :]

    def fold_one(n, i):
        return send(
            fold_source(n, i), reduce_recv.at[n, i], fold_send.at[n, i], fold_recv.at[n, i],
            core_peer,
        )

    def fold_two(n):
        return send(
            fold_source(n, 2), reduce_recv.at[n, 2], fold_send.at[n, 2], fold_recv.at[n, 2],
            y_peer,
        )

    to_y.wait_send()
    to_core.wait_send()
    forward.wait_send()
    for n, (acc, _) in enumerate(folded):
        for i in (1, 0):
            fold_source(n, i)[...] = acc[slot(2 * i + 1), :].astype(BF16)
            fold_one(n, i).start()
    for n, (acc, _) in enumerate(folded):
        fold_one(n, 1).wait_recv()
        fold_source(n, 2)[...] = (acc[slot(2), :] + reduce_recv[n, 1].astype(F32)).astype(BF16)
        fold_two(n).start()
    chain(chunks)
    for n, (acc, out) in enumerate(folded):
        fold_one(n, 0).wait_recv()
        fold_two(n).wait_recv()
        out[...] = acc[slot(0), :] + reduce_recv[n, 0].astype(F32) + reduce_recv[n, 2].astype(F32)

    @pl.loop(chunks + 1, chunks + 2 * root_lag + 1)
    def _(t):
        chain(t)

    @pl.loop(0, chunks)
    def _(c):
        for k in range(3):
            p = 3 * c + k
            from_pair(c, k).wait_recv()
            from_pair(c, k).wait_send()

            @pl.when(at == root)
            def _():
                keep(c, k).wait()
                if root > 0:
                    finals(c, k, False, True).wait_send()
                if root < line - 1:
                    finals(c, k, True, True).wait_send()

            @pl.when(at < root)
            def _():
                up_copy(p).wait_send()

                @pl.when(has_below)
                def _():
                    finals(c, k, False, False).wait_send()

            @pl.when(at > root)
            def _():
                down_copy(p).wait_send()

                @pl.when(has_above)
                def _():
                    finals(c, k, True, False).wait_send()

    @pl.loop(max(chunks - 3, 0), chunks)
    def _(j):
        exchange(j).wait_send()

    for n in range(2):
        for i in range(2):
            fold_one(n, i).wait_send()
        fold_two(n).wait_send()


def ffn(h, goal, inner_grad, w_gate, w_up, w_down):
    count = lax.axis_size("group")
    rows, width = h.shape
    hidden = w_gate.shape[1] // 2
    wide = 128
    chunks = hidden // wide
    tokens = 4 * rows
    anywhere = pl.BlockSpec(memory_space=pl.ANY)
    local = pl.BlockSpec(memory_space=pltpu.VMEM)
    dma = pltpu.SemaphoreType.DMA
    pieces = 3 * chunks
    flops = 2 * tokens * width * hidden * 8
    return pl.pallas_call(
        functools.partial(ffn_kernel, count, chunks),
        out_shape=(
            jax.ShapeDtypeStruct((3, width, 2 * hidden), BF16),
            jax.ShapeDtypeStruct((pieces, width, wide), BF16),
            jax.ShapeDtypeStruct((pieces, width, wide), BF16),
            jax.ShapeDtypeStruct((rows, width), F32),
            jax.ShapeDtypeStruct((rows, width), F32),
        ),
        in_specs=[local, local, local, anywhere, anywhere, anywhere],
        out_specs=(anywhere, anywhere, anywhere, local, local),
        scratch_shapes=[
            pltpu.VMEM((tokens, width), BF16),
            pltpu.VMEM((width, tokens), BF16),
            pltpu.VMEM((3, tokens, 2 * wide), BF16),
            pltpu.VMEM((chunks, tokens, 2 * wide), BF16),
            pltpu.VMEM((chunks, width, 2 * wide), BF16),
            pltpu.VMEM((hidden, width), BF16),
            pltpu.VMEM((tokens, width), F32),
            pltpu.VMEM((tokens, width), F32),
            pltpu.VMEM((tokens, 3 * wide), BF16),
            pltpu.VMEM((pieces, width, wide), BF16),
            pltpu.VMEM((2, width, wide), BF16),
            pltpu.VMEM((2, 3, rows, width), BF16),
            dma((3,)), dma((3,)), dma((chunks,)), dma((chunks,)),
            dma((pieces,)), dma((pieces,)), dma((pieces,)),
            dma((pieces,)), dma((pieces,)), dma((pieces,)), dma((pieces,)), dma((pieces,)),
            dma((2,)), dma((3, chunks)), dma((pieces,)), dma((2, 3)), dma((2, 3)),
        ],
        compiler_params=pltpu.CompilerParams(
            collective_id=1, has_side_effects=True, vmem_limit_bytes=63 << 20
        ),
        cost_estimate=pl.CostEstimate(
            flops=flops, bytes_accessed=200 << 20, transcendentals=tokens * hidden
        ),
    )(h, goal, inner_grad, w_gate, w_up, w_down)


def masked_scores(query, keys, segment, place, scale):
    scores = jnp.einsum("qkgd,skd->kgqs", query, keys, preferred_element_type=F32) * scale
    allowed = (segment[:, None] == segment[None, :]) & (place[None, :] <= place[:, None])
    return jnp.where(allowed, scores, NEGATIVE)


def body(
    tokens, lengths, norm_gain, w_query, w_key, w_value, w_head_gate, query_gain, key_gain,
    w_out, ffn_gain, w_gate, w_up, w_down, grad_out,
):
    row_count = lax.axis_size("row")
    rows, d_loc = tokens.shape
    group_tok = 2 * rows
    width = d_loc * row_count
    head_dim = query_gain.shape[0]
    q_half = w_query.shape[1] // 2
    kv_half = w_key.shape[1] // 2
    gate_half = w_head_gate.shape[1] // 2
    heads = q_half // head_dim
    kv_heads = kv_half // head_dim
    share = heads // kv_heads
    main = q_half + 2 * kv_half
    half_hidden = w_gate.shape[1] // 2
    scale = head_dim ** (-0.5)
    row_at = lax.axis_index("row")
    col_at = lax.axis_index("col")
    side = lax.axis_index("group") % 2

    steps = jnp.arange(rows, dtype=jnp.int32)
    index = jnp.concatenate([col_at * rows + steps, (1 - col_at) * rows + steps])
    segment, place = places(lengths, index)

    grad_group = jnp.concatenate([grad_out, swap(grad_out, "col")])
    grad_all = jnp.concatenate([grad_group, swap_groups(grad_group)])
    down_half = lax.dynamic_slice_in_dim(w_down, side * half_hidden, half_hidden, axis=0)
    inner_part = nt(grad_all, down_half)
    inner_grad = (inner_part + swap(inner_part.astype(BF16), "row").astype(F32)).astype(BF16)
    grad_turned = grad_all.T

    x_in = tokens.astype(F32)
    squares = jnp.sum(x_in * x_in, axis=1)
    inverse_one = lax.rsqrt((squares + swap(squares, "row")) / width + EPS)
    normed_one = (x_in * inverse_one[:, None] * norm_gain).astype(BF16)
    permuted = jnp.concatenate([normed_one, swap(normed_one, "col")])
    splits = [halves(w, 1, row_at) for w in (w_query, w_key, w_value, w_head_gate)]
    w_first = jnp.concatenate(
        [own for own, _ in splits[:3]] + [other for _, other in splits[:3]] + list(splits[3]),
        axis=1,
    )
    partial = nn(permuted, w_first)
    away = jnp.concatenate(
        [partial[:, main : 2 * main], partial[:, 2 * main + gate_half :]], axis=1
    ).astype(BF16)
    stay = jnp.concatenate(
        [partial[:, :main], partial[:, 2 * main : 2 * main + gate_half]], axis=1
    )
    projected = stay + swap(away, "row").astype(F32)
    raw_query = projected[:, :q_half].reshape(group_tok, heads, head_dim)
    raw_key = projected[:, q_half : q_half + kv_half].reshape(group_tok, kv_heads, head_dim)
    raw_value = projected[:, q_half + kv_half : main].reshape(group_tok, kv_heads, head_dim)
    logit = projected[:, main:]
    query_inverse = lax.rsqrt(jnp.mean(raw_query * raw_query, axis=-1, keepdims=True) + EPS)
    key_inverse = lax.rsqrt(jnp.mean(raw_key * raw_key, axis=-1, keepdims=True) + EPS)
    cosines, sines = rope_tables(place, head_dim)
    cos_heads = cosines[:, None, :]
    sin_heads = sines[:, None, :]
    query = rotate(raw_query * query_inverse * query_gain, cos_heads, sin_heads).astype(BF16)
    keys = rotate(raw_key * key_inverse * key_gain, cos_heads, sin_heads).astype(BF16)
    values = raw_value.astype(BF16)
    query = query.reshape(group_tok, kv_heads, share, head_dim)

    scores = masked_scores(query, keys, segment, place, scale)
    top = jnp.max(scores, axis=-1, keepdims=True)
    raised = jnp.exp(scores - top)
    probs = raised / jnp.sum(raised, axis=-1, keepdims=True)
    probs_low = probs.astype(BF16)
    attended = jnp.einsum("kgqs,skd->qkgd", probs_low, values, preferred_element_type=F32)
    attended = attended.reshape(group_tok, heads, head_dim)
    gate_sigmoid = jax.nn.sigmoid(logit)
    gated = (attended * gate_sigmoid[:, :, None]).reshape(group_tok, q_half).astype(BF16)
    gated_all = jnp.concatenate([gated, swap(gated, "row")], axis=1)
    w_back = jnp.concatenate(halves(w_out, 0, row_at))

    def sum_cores(values):
        return values[:rows] + swap(values[rows:].astype(BF16), "col").astype(F32)

    resid = x_in + sum_cores(nn(gated_all, w_back))
    squares = jnp.sum(resid * resid, axis=1)
    inverse_two = lax.rsqrt((squares + swap(squares, "row")) / width + EPS)
    normed_two = (resid * inverse_two[:, None] * ffn_gain).astype(BF16)

    ffn_sum, _, _, branch, d_normed_two = ffn(
        normed_two, grad_turned, inner_grad, w_gate, w_up, w_down
    )
    output = (resid + branch).astype(BF16)

    d_top = grad_out.astype(F32)
    ffn_gain_part = jnp.sum(d_normed_two * resid * inverse_two[:, None], axis=0)
    scaled_two = d_normed_two * ffn_gain
    inner_two = jnp.sum(scaled_two * resid, axis=1)
    inner_two = inner_two + swap(inner_two, "row")
    d_resid = (
        d_top
        + inverse_two[:, None] * scaled_two
        - resid * (inverse_two**3 * inner_two / width)[:, None]
    )
    d_branch = d_resid.astype(BF16)
    branch_all = jnp.concatenate([d_branch, swap(d_branch, "col")])
    grad_out_w = lax.dot_general(
        gated_all, branch_all, (((0,), (0,)), ((), ())), preferred_element_type=F32
    )
    d_gated_part = nt(branch_all, w_back)
    d_gated = d_gated_part[:, :q_half] + swap(
        d_gated_part[:, q_half:].astype(BF16), "row"
    ).astype(F32)
    d_gated = d_gated.reshape(group_tok, heads, head_dim)
    d_attended = (d_gated * gate_sigmoid[:, :, None]).astype(BF16)
    d_logit = jnp.sum(d_gated * attended, axis=-1) * gate_sigmoid * (1.0 - gate_sigmoid)
    d_attended = d_attended.reshape(group_tok, kv_heads, share, head_dim)

    d_probs = jnp.einsum("qkgd,skd->kgqs", d_attended, values, preferred_element_type=F32)
    d_scores = (probs * (d_probs - jnp.sum(d_probs * probs, axis=-1, keepdims=True))).astype(BF16)
    d_query = jnp.einsum("kgqs,skd->qkgd", d_scores, keys, preferred_element_type=F32) * scale
    d_keys = jnp.einsum("kgqs,qkgd->skd", d_scores, query, preferred_element_type=F32) * scale
    d_values = jnp.einsum("kgqs,qkgd->skd", probs_low, d_attended, preferred_element_type=F32)
    d_query = d_query.reshape(group_tok, heads, head_dim)
    d_raw_query, query_gain_part = head_norm_back(
        unrotate(d_query, cos_heads, sin_heads), raw_query, query_inverse, query_gain
    )
    d_raw_key, key_gain_part = head_norm_back(
        unrotate(d_keys, cos_heads, sin_heads), raw_key, key_inverse, key_gain
    )
    d_projected = jnp.concatenate(
        [
            d_raw_query.reshape(group_tok, q_half),
            d_raw_key.reshape(group_tok, kv_half),
            d_values.reshape(group_tok, kv_half),
            d_logit,
        ],
        axis=1,
    ).astype(BF16)
    came = swap(d_projected, "row")
    d_first = jnp.concatenate(
        [d_projected[:, :main], came[:, :main], d_projected[:, main:], came[:, main:]], axis=1
    )
    grad_first = lax.dot_general(
        permuted, d_first, (((0,), (0,)), ((), ())), preferred_element_type=F32
    )
    d_normed_one = sum_cores(nt(d_first, w_first))
    norm_gain_part = jnp.sum(d_normed_one * x_in * inverse_one[:, None], axis=0)
    scaled_one = d_normed_one * norm_gain
    inner_one = jnp.sum(scaled_one * x_in, axis=1)
    inner_one = inner_one + swap(inner_one, "row")
    input_grad = (
        d_resid
        + inverse_one[:, None] * scaled_one
        - x_in * (inverse_one**3 * inner_one / width)[:, None]
    )
    grad_norm_gain, grad_ffn_gain = lax.psum((norm_gain_part, ffn_gain_part), ("group", "col"))
    grad_query_gain, grad_key_gain = lax.psum(
        (query_gain_part, key_gain_part), ("group", "row", "col")
    )
    first_sum = lax.psum(grad_first.astype(BF16), "group")
    out_sum = lax.psum(grad_out_w.astype(BF16), "group")

    def piece(start, size):
        own = first_sum[:, start : start + size]
        other = first_sum[:, main + start : main + start + size]
        return ordered(own, other, 1, row_at).astype(F32)

    gates = first_sum[:, 2 * main :]
    grad_head_gate = ordered(gates[:, :gate_half], gates[:, gate_half:], 1, row_at).astype(F32)
    grad_out_full = ordered(*jnp.split(out_sum, 2, axis=0), 0, row_at).astype(F32)
    grad_gate, grad_up, grad_down = (ffn_sum[k].astype(F32) for k in range(3))
    return (
        output,
        input_grad,
        grad_norm_gain,
        piece(0, q_half),
        piece(q_half, kv_half),
        piece(q_half + kv_half, kv_half),
        grad_head_gate,
        grad_query_gain,
        grad_key_gain,
        grad_out_full,
        grad_ffn_gain,
        grad_gate,
        grad_up,
        grad_down.T,
    )


def solution(mesh):
    shards = P(("group", "col"), "row")
    in_specs = (
        shards,
        P("group"),
        P("row"),
        P("row", "col"),
        P("row", "col"),
        P("row", "col"),
        P("row", "col"),
        P(),
        P(),
        P("col", "row"),
        P("row"),
        P("row", "col"),
        P("row", "col"),
        P("col", "row"),
        shards,
    )
    out_specs = (
        shards,
        shards,
        P("row"),
        P("row", "col"),
        P("row", "col"),
        P("row", "col"),
        P("row", "col"),
        P(),
        P(),
        P("col", "row"),
        P("row"),
        P("row", "col"),
        P("row", "col"),
        P("col", "row"),
    )
    return jax.shard_map(body, mesh=mesh, in_specs=in_specs, out_specs=out_specs, check_vma=False)
```

time: 1680 us -> 943 us (0.56)
  waiting for transfers between devices: 1160 us -> 249 us
  Pallas kernels: 0 us -> 335 us
  blocking collectives: 150 us -> 68.8 us
  matrix products: 123 us -> 59.2 us
  local copies, waits for them, and re-layouts: 131 us -> 96.8 us
  starting transfers between devices: 1.96 us -> 21 us
    psum x1, waiting for transfers between devices: 635 us -> 99.8 us  [body(): first_sum = lax.psum(grad_first.astype(BF16), 'group')]
    pallas_call x0 -> x1, Pallas kernels: none -> 335 us  [ffn(): pl.pallas_call(functools.partial(ffn_kernel, count, chunks), out_shape=(j...]
    reduce_scatter x9 -> x0, waiting for transfers between devices: 298 us -> none  [the longest x3 184 us: reduce_rows(): lax.psum_scatter(term(jnp.int32(0), lax.axis_size('row') * rows), 'row',...]
    all_gather x8 -> x0, waiting for transfers between devices: 223 us -> none  [the longest x3 104 us: gather_blocks(): return lax.all_gather(values, 'row', axis=0, tiled=True)]
    ppermute x0 -> x15, waiting for transfers between devices: none -> 149 us  [the longest x14 132 us: swap(): return lax.ppermute(values, axis, [(0, 1), (1, 0)])]
    dot_general x17 -> x12, matrix products: 114 us -> 54 us  [the longest x3 19 us: nt(): lax.dot_general(a, b, (((1,), (1,)), ((), ())), preferred_element_type=F32)]
    psum x5 -> x0, blocking collectives: 56.6 us -> none  [the longest x1 36.8 us: body(): lax.psum(grad_head_gate.astype(jnp.bfloat16), 'group').astype(jnp.float32)]
    gather x6 -> x0, local copies, waits for them, and re-layouts: 32.1 us -> none  [the longest x1 9.3 us: first_back_term(): gathered_first[inverse]]
  transfers between devices with their start and end apart: 19 -> 16, of which waited for: 14 -> 9; matrix products, arithmetic and copies ran while one was open for 10% -> 14% of each run, Pallas kernels for 0% -> 0%
where the time goes in v1:
time: 943 us; the launch traced here: 929 us
  Pallas kernels  335 us (36%)
  waiting for transfers between devices  249 us (26%)
  local copies, waits for them, and re-layouts  96.8 us (10%)
  other arithmetic  83.9 us (9%)
  blocking collectives  68.8 us (7%)
  matrix products  59.2 us (6%)
  starting transfers between devices  21 us (2%)
  between operations  15.4 us (2%)
    pallas_call x1, Pallas kernels, ffn(): pl.pallas_call(functools.partial(ffn_kernel, count, chunks), out_shape=(j...  335 us
    ppermute x14, waiting for transfers between devices, swap(): return lax.ppermute(values, axis, [(0, 1), (1, 0)])  132 us
    psum x1, waiting for transfers between devices, body(): first_sum = lax.psum(grad_first.astype(BF16), 'group')  99.8 us
    psum x1, blocking collectives, body(): lax.psum((query_gain_part, key_gain_part), ('group', 'row', 'col'))  43 us
    unnamed x135, local copies, waits for them, and re-layouts  38.5 us
    psum x1, blocking collectives, body(): lax.psum((norm_gain_part, ffn_gain_part), ('group', 'col'))  25.8 us
    concatenate x1, local copies, waits for them, and re-layouts, body(): jnp.concatenate([own for own, _ in splits[:3]] + [other for _, other in s...  21.2 us
    ppermute x14, starting transfers between devices, swap(): return lax.ppermute(values, axis, [(0, 1), (1, 0)])  19.4 us
  transfers between devices with their start and end apart: 16, of which 9 were waited for; matrix products, arithmetic and copies ran while one was open for 14% of the time, Pallas kernels for 0%

profile of v1, /device:TPU:24, one launch (start us, length us, event | category | flops | bytes accessed | tf_op | source)
XLA Modules:
  0.0 928.8 jit_solution(10465448522486911723)
XLA Ops:
  28.1 21.2 %concatenate.93 = bf16[1024,2056]{0,1:T(8,128)(2,1)} concatenate(bf16[1024,512]{0,1:T(8,128)(2,1)} %get-tuple-element.97, bf16[1024,256]{0,1:T(8,128)(2,1)} %get-tuple-element.144, bf16[1024,256]{0,1:T(8,128)(2,1)} %get-tuple-element.111, bf16[1024,512]{0,1:T(8,128)(2,1)S(1)} %copy-done.18, bf16[1024,256]{0,1:T(8,128)(2,1)} %get-tuple-element.145, ...), dimensions={1} | concatenate | bytes 8421376 | tf_op jit(solution)/shard_map/concatenate | solution.py:520
  53.5 5.7 fusion.74
  65.6 17.1 %collective-permute-done.7 = bf16[640,1024]{0,1:T(8,128)(2,1)} collective-permute-done((bf16[640,1024]{0,1:T(8,128)(2,1)S(1)}, bf16[640,1024]{0,1:T(8,128)(2,1)}, u32[]{:S(2)}, u32[]{:S(2)}) %collective-permute-start.7) | collective-permute-done | bytes 1310752 | tf_op jit(solution)/shard_map/ppermute | solution.py:24
  82.8 5.7 concatenate.106
  88.4 11.6 %fusion.76 = (bf16[1280,1536]{1,0:T(8,128)(2,1)}, f32[1280,1536]{1,0:T(8,128)}) fusion(bf16[1280,1024]{0,1:T(8,128)(2,1)} %concatenate.106, bf16[3072,1024]{1,0:T(8,128)(2,1)} %down_ref.1, s32[]{:T(128)S(6)} %select_n.126), kind=kOutput, calls=%fused_computation.188 | convolution fusion | flops 4028497920 | bytes 17563652 | tf_op jit(solution)/shard_map/dot_general | solution.py:82
  107.3 5.2 fusion.75
  118.1 82.2 %collective-permute-done.3 = bf16[640,512]{0,1:T(8,128)(2,1)S(1)} collective-permute-done((bf16[640,512]{0,1:T(8,128)(2,1)S(1)}, bf16[640,512]{0,1:T(8,128)(2,1)S(1)}, u32[]{:S(2)}, u32[]{:S(2)}) %collective-permute-start.3) | collective-permute-done | bytes 655392 | tf_op jit(solution)/shard_map/ppermute | solution.py:19
  209.3 17.5 %add_convert_fusion.inner_grad_ref = bf16[1280,1536]{1,0:T(8,128)(2,1)} fusion(f32[1280,1536]{1,0:T(8,128)S(1)} %bitcast.170, bf16[1280,1536]{1,0:T(8,128)(2,1)} %collective-permute-done.8), kind=kLoop, calls=%fused_computation.2 | loop fusion | flops 5898240 | bytes 15728640 | tf_op jit(solution)/shard_map/convert_element_type | solution.py:511
  226.8 334.9 %shard_map.254 = (bf16[3,1024,3072]{2,1,0:T(8,128)(2,1)}, bf16[36,1024,128]{2,1,0:T(8,128)(2,1)}, bf16[36,1024,128]{2,1,0:T(8,128)(2,1)}, f32[320,1024]{1,0:T(8,128)}, f32[320,1024]{1,0:T(8,128)}) custom-call(bf16[320,1024]{1,0:T(8,128)(2,1)} %multiply_convert_fusion.1.h_ref, bf16[1024,1280]{1,0:T(8,128)(2,1)} %bitcast.177, ...), custom_call_target="tpu_custom_call" | custom-call | flops 32212254720 | bytes 209715200 | tf_op jit(solution)/shard_map/pallas_call | solution.py:437
  563.9 7.8 collective-permute-start.9
  583.0 15.3 %collective-permute-done.11 = bf16[640,512]{1,0:T(8,128)(2,1)} collective-permute-done((bf16[640,512]{1,0:T(8,128)(2,1)}, bf16[640,512]{1,0:T(8,128)(2,1)}, u32[]{:S(2)}, u32[]{:S(2)}) %collective-permute-start.11) | collective-permute-done | bytes 655392 | tf_op jit(solution)/shard_map/ppermute | solution.py:19
  603.8 7.4 fusion.1
  611.2 4.1 fusion.38
  632.5 25.6 %collective-permute-done.12 = bf16[640,1028]{0,1:T(8,128)(2,1)S(1)} collective-permute-done((bf16[640,1028]{0,1:T(8,128)(2,1)S(1)}, bf16[640,1028]{0,1:T(8,128)(2,1)S(1)}, u32[]{:S(2)}, u32[]{:S(2)}) %collective-permute-start.12) | collective-permute-done | bytes 1315872 | tf_op jit(solution)/shard_map/ppermute | solution.py:19
  659.3 15.8 %concatenate.112 = bf16[640,2056]{0,1:T(8,128)(2,1)} concatenate(bf16[640,512]{0,1:T(8,128)(2,1)} %copy-done.12, bf16[640,256]{0,1:T(8,128)(2,1)} %bitcast.176, bf16[640,256]{0,1:T(8,128)(2,1)} %bitcast.181, bf16[640,1024]{0,1:T(8,128)(2,1)} %slice.175, bf16[640,4]{0,1:T(4,128)(2,1)S(1)} %multiply_convert_fusion.4, bf16[640,4]{0,1:T(4,128)(2,1)S(1)} %slice.176), dimensions={1} | concatenate | bytes 5263360 | tf_op jit(solution)/shard_map/concatenate | solution.py:617
  675.1 7.6 convolution_convert_fusion
  682.7 5.8 fusion.77
  691.0 17.8 %convert_bitcast_fusion = (f32[3072,1024]{0,1:T(8,128)}, f32[1024,3072]{1,0:T(8,128)}, f32[1024,3072]{1,0:T(8,128)}) fusion(bf16[3,1024,3072]{2,1,0:T(8,128)(2,1)} %get-tuple-element.19), kind=kLoop, calls=%fused_computation.1 | loop fusion | flops 9437184 | bytes 56623104 | tf_op jit(solution)/shard_map/transpose | solution.py:663
  708.8 12.7 %copy.99 = f32[3072,1024]{1,0:T(8,128)} copy(f32[3072,1024]{0,1:T(8,128)} %get-tuple-element.81) | data formatting | bytes 25165824
  721.6 43.0 %all-reduce = (f32[128]{0:T(128)}, f32[128]{0:T(128)}) all-reduce(f32[128]{0:T(128)S(1)} %bitcast_reduce_fusion, f32[128]{0:T(128)S(1)} %get-tuple-element.66), channel_id=1, replica_groups=mesh['group'=8,'row'=2,'col'=2] {'group','row','col'}, use_global_device_ids=true, to_apply=%region_20.21 | all-reduce | flops 256 | bytes 2048 | tf_op jit(solution)/shard_map/psum | solution.py:634
  769.0 25.8 %all-reduce.1 = (f32[1024]{0:T(1024)}, f32[1024]{0:T(1024)}) all-reduce(f32[1024]{0:T(1024)S(1)} %get-tuple-element.62, f32[1024]{0:T(1024)S(1)} %get-tuple-element.64), channel_id=1, replica_groups=mesh['group'=8,'row'=2,'col'=2] {'group','col'}, use_global_device_ids=true, to_apply=%region_16.17 | all-reduce | flops 2048 | bytes 16384 | tf_op jit(solution)/shard_map/psum | solution.py:633
  794.8 4.0 fusion.23
  798.8 99.8 %all-reduce.5.cloned.1.call-done = (bf16[1024,2056]{0,1:T(8,128)(2,1)}, bf16[1024,1024]{1,0:T(8,128)(2,1)}) async-done(((bf16[1024,2056]{0,1:T(8,128)(2,1)}, bf16[1024,1024]{1,0:T(8,128)(2,1)}), (bf16[1024,2056]{0,1:T(8,128)(2,1)}, bf16[1024,1024]{1,0:T(8,128)(2,1)})) %all-reduce.5.cloned.1.call-update) | async-done | bytes 6307856 | tf_op jit(solution)/shard_map/psum | solution.py:637
  906.2 5.3 copy.96
  (254 shorter events, 114.4 us)
Async XLA Ops:
  7.2 891.5 %all-reduce.5.cloned.1.call-start = ((), (), s32[]{:S(2)}) async-start(), calls=%async_computation | async-start | bytes 12615680 | tf_op jit(solution)/shard_map/psum | solution.py:637
  8.5 17.6 %collective-permute-start = (f32[320]{0:T(512)S(1)}, f32[320]{0:T(512)S(1)}, u32[]{:S(2)}, u32[]{:S(2)}) collective-permute-start(f32[320]{0:T(512)S(1)} %fusion.19), channel_id=1, source_target_pairs={{0,2},{2,0},{1,3},{3,1},{4,6},{6,4},{5,7},{7,5},{8,10},{10,8},{9,1... | collective-permute-start | bytes 3848 | tf_op jit(solution)/shard_map/ppermute | solution.py:19
  10.1 39.9 %collective-permute-start.6 = (bf16[320,1024]{1,0:T(8,128)(2,1)}, bf16[320,1024]{1,0:T(8,128)(2,1)}, u32[]{:S(2)}, u32[]{:S(2)}) collective-permute-start(bf16[320,1024]{1,0:T(8,128)(2,1)} %param.29), channel_id=1, source_target_pairs={{0,1},{1,0},{2,3},{3,2},{4,5},{5,4},{6,7},{7,6},{8,9},{9,8},{10,11... | collective-permute-start | bytes 1966088 | tf_op jit(solution)/shard_map/ppermute | solution.py:19
  26.1 23.1 %copy-start.46 = (f32[320]{0:T(512)}, f32[320]{0:T(512)S(1)}, u32[]{:S(2)}) copy-start(f32[320]{0:T(512)S(1)} %add_rsqrt_fusion.3) | copy-start | bytes 3844
  27.2 26.3 %collective-permute-start.1 = (bf16[320,1024]{1,0:T(8,128)(2,1)}, bf16[320,1024]{1,0:T(8,128)(2,1)}, u32[]{:S(2)}, u32[]{:S(2)}) collective-permute-start(bf16[320,1024]{1,0:T(8,128)(2,1)} %fusion.21), channel_id=1, source_target_pairs={{0,1},{1,0},{2,3},{3,2},{4,5},{5,4},{6,7},{7,6},{8,9},{9,8},{10,11... | collective-permute-start | bytes 1966088 | tf_op jit(solution)/shard_map/ppermute | solution.py:19
  51.9 30.9 %collective-permute-start.7 = (bf16[640,1024]{0,1:T(8,128)(2,1)S(1)}, bf16[640,1024]{0,1:T(8,128)(2,1)}, u32[]{:S(2)}, u32[]{:S(2)}) collective-permute-start(bf16[640,1024]{0,1:T(8,128)(2,1)S(1)} %pad_maximum_fusion.7), channel_id=1, source_target_pairs={{0,4},{4,0},{8,12},{12,8},{16,20},{20,16},{24,28},{28,24},{1,5},{5... | collective-permute-start | bytes 3932168 | tf_op jit(solution)/shard_map/ppermute | solution.py:24
  60.5 40.1 %collective-permute-start.2 = (bf16[640,1028]{0,1:T(8,128)(2,1)}, bf16[640,1028]{0,1:T(8,128)(2,1)}, u32[]{:S(2)}, u32[]{:S(2)}) collective-permute-start(bf16[640,1028]{0,1:T(8,128)(2,1)} %pad_maximum_fusion.3), channel_id=1, source_target_pairs={{0,2},{2,0},{1,3},{3,1},{4,6},{6,4},{5,7},{7,5},{8,10},{10,8},{9,1... | collective-permute-start | bytes 3947528 | tf_op jit(solution)/shard_map/ppermute | solution.py:19
  100.1 109.2 %collective-permute-start.8 = (bf16[1280,1536]{1,0:T(8,128)(2,1)}, bf16[1280,1536]{1,0:T(8,128)(2,1)}, u32[]{:S(2)}, u32[]{:S(2)}) collective-permute-start(bf16[1280,1536]{1,0:T(8,128)(2,1)} %get-tuple-element.138), channel_id=1, source_target_pairs={{0,2},{2,0},{1,3},{3,1},{4,6},{6,4},{5,7},{7,5},{8,10},{10,8},{9,1... | collective-permute-start | bytes 11796488 | tf_op jit(solution)/shard_map/ppermute | solution.py:19
  116.4 84.0 %copy-start.39 = (bf16[640,512]{0,1:T(8,128)(2,1)}, bf16[640,512]{0,1:T(8,128)(2,1)S(1)}, u32[]{:S(2)}) copy-start(bf16[640,512]{0,1:T(8,128)(2,1)S(1)} %fusion.30) | copy-start | bytes 1966084
  116.4 83.9 %collective-permute-start.3 = (bf16[640,512]{0,1:T(8,128)(2,1)S(1)}, bf16[640,512]{0,1:T(8,128)(2,1)S(1)}, u32[]{:S(2)}, u32[]{:S(2)}) collective-permute-start(bf16[640,512]{0,1:T(8,128)(2,1)S(1)} %fusion.30), channel_id=1, source_target_pairs={{0,2},{2,0},{1,3},{3,1},{4,6},{6,4},{5,7},{7,5},{8,10},{10,8},{9,1... | collective-permute-start | bytes 1966088 | tf_op jit(solution)/shard_map/ppermute | solution.py:19
  118.0 91.3 %slice-start.2 = ((s8[7864320]{0:T(1024)(128)(4,1)}), s8[4194304]{0:T(1024)(128)(4,1)S(1)}, s32[]{:S(2)}) async-start(s8[7864320]{0:T(1024)(128)(4,1)} %bitcast.169), calls=%async_computation.3 | async-start | bytes 8388608
  118.1 83.8 %copy-start.35 = (bf16[512,1024]{1,0:T(8,128)(2,1)}, bf16[512,1024]{1,0:T(8,128)(2,1)S(1)}, u32[]{:S(2)}) copy-start(bf16[512,1024]{1,0:T(8,128)(2,1)S(1)} %get-tuple-element.100) | copy-start | bytes 3145732
  118.1 83.8 %copy-start.37 = (bf16[512,1024]{1,0:T(8,128)(2,1)}, bf16[512,1024]{1,0:T(8,128)(2,1)S(1)}, u32[]{:S(2)}) copy-start(bf16[512,1024]{1,0:T(8,128)(2,1)S(1)} %get-tuple-element.101) | copy-start | bytes 3145732
  202.1 2.2 collective-permute-start.4
  204.6 3.7 collective-permute-start.5
  563.9 13.0 %copy-start.38 = (bf16[512,1024]{1,0:T(8,128)(2,1)S(1)}, bf16[512,1024]{1,0:T(8,128)(2,1)}, u32[]{:S(2)}) copy-start(bf16[512,1024]{1,0:T(8,128)(2,1)} %copy-done.37) | copy-start | bytes 3145732
  563.9 9.4 %collective-permute-start.9 = (f32[320]{0:T(512)S(1)}, f32[320]{0:T(512)S(1)}, u32[]{:S(2)}, u32[]{:S(2)}) collective-permute-start(f32[320]{0:T(512)S(1)} %get-tuple-element.65), channel_id=1, source_target_pairs={{0,2},{2,0},{1,3},{3,1},{4,6},{6,4},{5,7},{7,5},{8,10},{10,8},{9,1... | collective-permute-start | bytes 3848 | tf_op jit(solution)/shard_map/ppermute | solution.py:19
  574.8 2.2 collective-permute-start.10
  580.9 17.4 %collective-permute-start.11 = (bf16[640,512]{1,0:T(8,128)(2,1)}, bf16[640,512]{1,0:T(8,128)(2,1)}, u32[]{:S(2)}, u32[]{:S(2)}) collective-permute-start(bf16[640,512]{1,0:T(8,128)(2,1)} %slice.243), channel_id=1, source_target_pairs={{0,2},{2,0},{1,3},{3,1},{4,6},{6,4},{5,7},{7,5},{8,10},{10,8},{9,1... | collective-permute-start | bytes 1966088 | tf_op jit(solution)/shard_map/ppermute | solution.py:19
  627.6 30.6 %collective-permute-start.12 = (bf16[640,1028]{0,1:T(8,128)(2,1)S(1)}, bf16[640,1028]{0,1:T(8,128)(2,1)S(1)}, u32[]{:S(2)}, u32[]{:S(2)}) collective-permute-start(bf16[640,1028]{0,1:T(8,128)(2,1)S(1)} %pad_maximum_fusion.4), channel_id=1, source_target_pairs={{0,2},{2,0},{1,3},{3,1},{4,6},{6,4},{5,7},{7,5},{8,10},{10,8},{9,1... | collective-permute-start | bytes 3947528 | tf_op jit(solution)/shard_map/ppermute | solution.py:19
  691.0 73.6 %collective-permute-start.13 = (bf16[320,1024]{1,0:T(8,128)(2,1)}, bf16[320,1024]{1,0:T(8,128)(2,1)}, u32[]{:S(2)}, u32[]{:S(2)}) collective-permute-start(bf16[320,1024]{1,0:T(8,128)(2,1)} %slice.242), channel_id=1, source_target_pairs={{0,1},{1,0},{2,3},{3,2},{4,5},{5,4},{6,7},{7,6},{8,9},{9,8},{10,11... | collective-permute-start | bytes 1966088 | tf_op jit(solution)/shard_map/ppermute | solution.py:19
  708.8 55.8 %copy-start.47 = (f32[320]{0:T(512)S(1)}, f32[320]{0:T(512)}, u32[]{:S(2)}) copy-start(f32[320]{0:T(512)} %copy-done.46) | copy-start | bytes 3844
  708.8 55.8 %copy-start.49 = (f32[1024]{0:T(1024)S(1)}, f32[1024]{0:T(1024)}, u32[]{:S(2)}) copy-start(f32[1024]{0:T(1024)} %param.17) | copy-start | bytes 12292
  766.7 28.1 %collective-permute-start.14 = (f32[320]{0:T(512)S(1)}, f32[320]{0:T(512)S(1)}, u32[]{:S(2)}, u32[]{:S(2)}) collective-permute-start(f32[320]{0:T(512)S(1)} %get-tuple-element.63), channel_id=1, source_target_pairs={{0,2},{2,0},{1,3},{3,1},{4,6},{6,4},{5,7},{7,5},{8,10},{10,8},{9,1... | collective-permute-start | bytes 3848 | tf_op jit(solution)/shard_map/ppermute | solution.py:19
  (56 other events, 209.9 us)
Sparse Core Ops, SparseCore 0:
  682.9 215.7 all-reduce.4

commit v2 on v1

v2 whole, which is shorter than its diff:
```python
import functools

import jax
import jax.numpy as jnp
from jax import lax
from jax.experimental import pallas as pl
from jax.experimental.pallas import tpu as pltpu
from jax.sharding import PartitionSpec as P

EPS = 1e-06
THETA = 1000000.0
NEGATIVE = -1e30
MESH = pl.DeviceIdType.MESH
F32 = jnp.float32
BF16 = jnp.bfloat16


def swap(values, axis):
    return lax.ppermute(values, axis, [(0, 1), (1, 0)])


def swap_groups(values):
    count = lax.axis_size("group")
    return lax.ppermute(values, "group", [(i, i ^ 1) for i in range(count)])


def halves(values, axis, at):
    low, high = jnp.split(values, 2, axis=axis)
    first = at == 0
    return jnp.where(first, low, high), jnp.where(first, high, low)


def ordered(own, other, axis, at):
    first = at == 0
    return jnp.concatenate(
        [jnp.where(first, own, other), jnp.where(first, other, own)], axis=axis
    )


def places(lengths_group, index):
    ends = jnp.cumsum(lengths_group)
    passed = (index[:, None] >= ends[None, :]).astype(jnp.int32)
    segment = jnp.sum(passed, axis=1)
    place = index - jnp.sum(passed * lengths_group[None, :], axis=1)
    return (segment, place)


def rope_tables(place, width):
    half = width // 2
    freq = THETA ** (-(jnp.arange(half, dtype=F32) * 2.0 / width))
    angle = place.astype(F32)[:, None] * freq[None, :]
    cosines = jnp.concatenate([jnp.cos(angle), jnp.cos(angle)], axis=1)
    sines = jnp.concatenate([jnp.sin(angle), jnp.sin(angle)], axis=1)
    return (cosines, sines)


def rotate(values, cosines, sines):
    half = values.shape[-1] // 2
    turned = jnp.concatenate([-values[..., half:], values[..., :half]], axis=-1)
    return values * cosines + turned * sines


def unrotate(grads, cosines, sines):
    half = grads.shape[-1] // 2
    scaled = grads * sines
    return grads * cosines + jnp.concatenate([scaled[..., half:], -scaled[..., :half]], axis=-1)


def head_norm_back(d_normed, raw_values, inverse, gain):
    scaled = d_normed * gain
    gain_part = jnp.sum(d_normed * raw_values * inverse, axis=(0, 1))
    d_raw = inverse * scaled - raw_values * inverse**3 * jnp.mean(
        scaled * raw_values, axis=-1, keepdims=True
    )
    return (d_raw, gain_part)


TILE = 256


def nt(a, b):
    return lax.dot_general(a, b, (((1,), (1,)), ((), ())), preferred_element_type=F32)


def nn(a, b):
    return jnp.dot(a, b, preferred_element_type=F32)


def copy_to(src, dst, send_sem, recv_sem, peer):
    return pltpu.make_async_remote_copy(
        src_ref=src, dst_ref=dst, send_sem=send_sem, recv_sem=recv_sem,
        device_id=peer, device_id_type=MESH,
    )


def tile(i, size=TILE):
    return pl.ds(pl.multiple_of(i * size, size), size)


class Place:
    def __init__(self, count):
        group = lax.axis_index("group")
        self.line = count // 2
        self.root = (self.line - 1) // 2
        self.deep = max(self.root, self.line - 1 - self.root)
        self.at = group // 2
        self.side = group % 2
        self.x_peer = {"row": 1 - lax.axis_index("row")}
        self.core_peer = {"col": 1 - lax.axis_index("col")}
        self.y_peer = {"group": group + 1 - 2 * self.side}
        self.above = {"group": jnp.minimum(group + 2, count - 1)}
        self.below = {"group": jnp.maximum(group - 2, 0)}
        self.has_above = self.at < self.line - 1
        self.has_below = self.at > 0

    def meet(self):
        barrier = pltpu.get_barrier_semaphore()

        def greet(peer):
            pl.semaphore_signal(barrier, inc=1, device_id=peer, device_id_type=MESH)

        for peer in (self.x_peer, self.core_peer, self.y_peer):
            greet(peer)
        pl.when(self.has_above)(lambda: greet(self.above))
        pl.when(self.has_below)(lambda: greet(self.below))
        met = 3 + self.has_above.astype(jnp.int32) + self.has_below.astype(jnp.int32)
        pl.semaphore_wait(barrier, met)


class Chain:
    def __init__(self, place, chunks, kinds, total, came, home, add, sems, share=True):
        self.place, self.chunks, self.kinds = place, chunks, kinds
        self.total, self.came, self.home, self.add = total, came, home, add
        self.sems, self.share = sems, share

    def part_copy(self, c, k, upward):
        sent, low, high = self.sems[:3]
        p = self.kinds * c + k
        peer, which, arrived = (
            (self.place.above, 0, low) if upward else (self.place.below, 1, high)
        )
        return copy_to(
            self.total(c, k), self.came(c, k, which), sent.at[p], arrived.at[p], peer
        )

    def final_copy(self, c, k, upward, first):
        up, down, arrived = self.sems[3:6]
        p = self.kinds * c + k
        src = self.total(c, k) if first else self.home(c, k, self.place.side)
        peer, sent = (self.place.above, up) if upward else (self.place.below, down)
        return copy_to(src, self.home(c, k, self.place.side), sent.at[p], arrived.at[p], peer)

    def keep_copy(self, c, k):
        return pltpu.make_async_copy(
            self.total(c, k), self.home(c, k, self.place.side),
            self.sems[6].at[self.kinds * c + k],
        )

    def share_copy(self, c, k, first, of=None):
        p = self.kinds * c + k
        of = self.place.side if of is None else of
        src = self.total(c, k) if first else self.home(c, k, self.place.side)
        return copy_to(
            src, self.home(c, k, of), self.sems[7].at[p], self.sems[8].at[p], self.place.y_peer
        )

    def step(self, t):
        at, line, root, deep = self.place.at, self.place.line, self.place.root, self.place.deep
        c = t - jnp.where(at < root, at, jnp.where(at > root, line - 1 - at, deep))
        live = (c >= 0) & (c < self.chunks)
        for k in range(self.kinds):

            @pl.when(live & (at < root))
            def _():
                @pl.when(self.place.has_below)
                def _():
                    self.part_copy(c, k, True).wait_recv()
                    self.add(c, k, 0)

                self.part_copy(c, k, True).start()

            @pl.when(live & (at > root))
            def _():
                @pl.when(self.place.has_above)
                def _():
                    self.part_copy(c, k, False).wait_recv()
                    self.add(c, k, 1)

                self.part_copy(c, k, False).start()

            @pl.when(live & (at == root))
            def _():
                if root > 0:
                    self.part_copy(c, k, True).wait_recv()
                    self.add(c, k, 0)
                if root < line - 1:
                    self.part_copy(c, k, False).wait_recv()
                    self.add(c, k, 1)
                if root > 0:
                    self.final_copy(c, k, False, True).start()
                if root < line - 1:
                    self.final_copy(c, k, True, True).start()
                if self.share:
                    self.share_copy(c, k, True).start()
                self.keep_copy(c, k).start()

        c = t - deep - jnp.abs(at - root)
        for k in range(self.kinds):

            @pl.when((c >= 0) & (c < self.chunks) & (at != root))
            def _():
                self.final_copy(c, k, True, False).wait_recv()

                @pl.when((at > root) & self.place.has_above)
                def _():
                    self.final_copy(c, k, True, False).start()

                @pl.when((at < root) & self.place.has_below)
                def _():
                    self.final_copy(c, k, False, False).start()

                if self.share:
                    self.share_copy(c, k, False).start()

    def steps(self):
        return self.chunks + 2 * self.place.deep

    def drain(self):
        at, line, root = self.place.at, self.place.line, self.place.root

        @pl.loop(0, self.chunks)
        def _(c):
            for k in range(self.kinds):
                if self.share:
                    self.share_copy(c, k, False, 1 - self.place.side).wait_recv()
                    self.share_copy(c, k, False).wait_send()

                @pl.when(at == root)
                def _():
                    self.keep_copy(c, k).wait()
                    if root > 0:
                        self.final_copy(c, k, False, True).wait_send()
                    if root < line - 1:
                        self.final_copy(c, k, True, True).wait_send()

                @pl.when(at < root)
                def _():
                    self.part_copy(c, k, True).wait_send()

                    @pl.when(self.place.has_below)
                    def _():
                        self.final_copy(c, k, False, False).wait_send()

                @pl.when(at > root)
                def _():
                    self.part_copy(c, k, False).wait_send()

                    @pl.when(self.place.has_above)
                    def _():
                        self.final_copy(c, k, True, False).wait_send()


def chain_semaphores(pieces):
    return [pltpu.SemaphoreType.DMA((pieces,)) for _ in range(9)]


def ffn_kernel(
    count, chunks, h_ref, top_ref, inner_grad_ref, gate_ref, up_ref, down_ref,
    pair_grads_ref, down_grads_ref, pair_came_ref, down_came_ref, branch_ref, back_ref,
    h_all, h_turned, sent, came, w_pair, w_down, acc_branch, acc_back, parts, inner_turned,
    pair_total, down_total, pair_stage, down_stage, reduce_recv,
    gather_send, gather_recv, x_send, x_recv, load_sem, weight_sem, fold_send, fold_recv,
    *chain_sems,
):
    place = Place(count)
    rows, width = h_ref.shape
    tokens = h_all.shape[0]
    tiles = tokens // TILE
    wide = w_down.shape[0] // chunks
    side = place.side

    def weight_copies(j):
        cols = tile(side * chunks + j, wide)
        return (
            pltpu.make_async_copy(
                gate_ref.at[:, cols], w_pair.at[j, :, pl.ds(0, wide)], weight_sem.at[0, j]
            ),
            pltpu.make_async_copy(
                up_ref.at[:, cols], w_pair.at[j, :, pl.ds(wide, wide)], weight_sem.at[1, j]
            ),
            pltpu.make_async_copy(
                down_ref.at[cols, :], w_down.at[tile(j, wide), :], weight_sem.at[2, j]
            ),
        )

    @pl.loop(0, chunks)
    def _(j):
        for copy in weight_copies(j):
            copy.start()

    place.meet()

    def slot(i):
        return pl.ds(i * rows, rows)

    to_y = copy_to(h_ref, h_all.at[slot(2)], gather_send.at[0], gather_recv.at[0], place.y_peer)
    to_core = copy_to(
        h_ref, h_all.at[slot(1)], gather_send.at[1], gather_recv.at[1], place.core_peer
    )
    forward = copy_to(
        h_all.at[slot(2)], h_all.at[slot(3)], gather_send.at[2], gather_recv.at[2],
        place.core_peer,
    )
    to_y.start()
    to_core.start()
    h_all[slot(0), :] = h_ref[...]
    acc_branch[...] = jnp.zeros_like(acc_branch)
    acc_back[...] = jnp.zeros_like(acc_back)
    to_y.wait_recv()
    forward.start()
    to_core.wait_recv()
    forward.wait_recv()

    def exchange(j):
        return copy_to(
            sent.at[lax.rem(j, 3)], came.at[j], x_send.at[j], x_recv.at[j], place.x_peer
        )

    def project(j):
        for copy in weight_copies(j):
            copy.wait()

        @pl.loop(0, tiles)
        def _(i):
            sent[lax.rem(j, 3), tile(i), :] = nn(h_all[tile(i), :], w_pair[j]).astype(BF16)

        exchange(j).start()

    def work(j):
        exchange(j).wait_recv()

        @pl.loop(0, tiles)
        def _(i):
            at_rows = tile(i)
            pair = sent[lax.rem(j, 3), at_rows, :].astype(F32) + came[j, at_rows, :].astype(F32)
            gate, up = pair[:, :wide], pair[:, wide:]
            grad = inner_grad_ref[at_rows, tile(j, wide)].astype(F32)
            sig = 1.0 / (1.0 + jnp.exp(-gate))
            silu = gate * sig
            parts[at_rows, pl.ds(0, wide)] = (
                grad * up * (sig * (1.0 + gate * (1.0 - sig)))
            ).astype(BF16)
            parts[at_rows, pl.ds(wide, wide)] = (grad * silu).astype(BF16)
            inner = (silu * up).astype(BF16)
            inner_turned[:, at_rows] = inner.T
            acc_branch[at_rows, :] += nn(inner, w_down[tile(j, wide), :])
            acc_back[at_rows, :] += nt(parts[at_rows, :], w_pair[j])

        @pl.loop(0, width // TILE)
        def _(i):
            pair = nn(h_turned[tile(i), :], parts[...])
            pair_total[j, 0, tile(i), :] = pair[:, :wide].astype(BF16)
            pair_total[j, 1, tile(i), :] = pair[:, wide:].astype(BF16)
            down_total[j, :, tile(i)] = nn(inner_turned[...], top_ref[:, tile(i)]).astype(BF16)

    def total(c, k):
        return down_total.at[c] if k == 2 else pair_total.at[c, k]

    def landed(c, k, which):
        return down_came_ref.at[which, c] if k == 2 else pair_came_ref.at[which, c, k]

    def home(c, k, of):
        at_cols = tile(of * chunks + c, wide)
        return down_grads_ref.at[at_cols, :] if k == 2 else pair_grads_ref.at[k, :, at_cols]

    def add(c, k, which):
        stage = (down_stage if k == 2 else pair_stage).at[which]
        copy = pltpu.make_async_copy(landed(c, k, which), stage, load_sem.at[which])
        copy.start()
        copy.wait()
        into = total(c, k)

        @pl.loop(0, into.shape[0] // wide)
        def _(i):
            at_rows = tile(i, wide)
            into[at_rows, :] = (
                into[at_rows, :].astype(F32) + stage[at_rows, :].astype(F32)
            ).astype(BF16)

    chain = Chain(place, chunks, 3, total, landed, home, add, chain_sems)

    for j in range(min(2, chunks)):
        project(j)

    @pl.loop(0, tiles)
    def _(i):
        h_turned[:, tile(i)] = h_all[tile(i), :].T

    @pl.loop(0, chunks)
    def _(t):
        @pl.when(t + 2 < chunks)
        def _():
            @pl.when(t >= 1)
            def _():
                exchange(t - 1).wait_send()

            project(t + 2)

        work(t)
        chain.step(t)

    folded = ((acc_back, back_ref), (acc_branch, branch_ref))

    def fold_source(n, i):
        if i == 2:
            return w_down.at[slot(n), :]
        return h_all.at[slot(2 * n + i), :]

    def fold(n, i):
        return copy_to(
            fold_source(n, i), reduce_recv.at[n, i], fold_send.at[n, i], fold_recv.at[n, i],
            place.y_peer if i == 2 else place.core_peer,
        )

    to_y.wait_send()
    to_core.wait_send()
    forward.wait_send()
    for n, (acc, _) in enumerate(folded):
        for i in (1, 0):
            fold_source(n, i)[...] = acc[slot(2 * i + 1), :].astype(BF16)
            fold(n, i).start()
    for n, (acc, _) in enumerate(folded):
        fold(n, 1).wait_recv()
        fold_source(n, 2)[...] = (acc[slot(2), :] + reduce_recv[n, 1].astype(F32)).astype(BF16)
        fold(n, 2).start()
    chain.step(chunks)
    for n, (acc, out) in enumerate(folded):
        fold(n, 0).wait_recv()
        fold(n, 2).wait_recv()
        out[...] = acc[slot(0), :] + reduce_recv[n, 0].astype(F32) + reduce_recv[n, 2].astype(F32)

    @pl.loop(chunks + 1, chain.steps())
    def _(t):
        chain.step(t)

    chain.drain()

    @pl.loop(max(chunks - 3, 0), chunks)
    def _(j):
        exchange(j).wait_send()

    for n in range(2):
        for i in range(3):
            fold(n, i).wait_send()


def ffn(h, top, inner_grad, w_gate, w_up, w_down):
    count = lax.axis_size("group")
    rows, width = h.shape
    hidden = w_gate.shape[1] // 2
    wide = 128
    chunks = hidden // wide
    tokens = 4 * rows
    anywhere = pl.BlockSpec(memory_space=pl.ANY)
    local = pl.BlockSpec(memory_space=pltpu.VMEM)
    dma = pltpu.SemaphoreType.DMA
    pieces = 3 * chunks
    flops = 2 * tokens * width * hidden * 8
    return pl.pallas_call(
        functools.partial(ffn_kernel, count, chunks),
        out_shape=(
            jax.ShapeDtypeStruct((2, width, 2 * hidden), BF16),
            jax.ShapeDtypeStruct((2 * hidden, width), BF16),
            jax.ShapeDtypeStruct((2, chunks, 2, width, wide), BF16),
            jax.ShapeDtypeStruct((2, chunks, wide, width), BF16),
            jax.ShapeDtypeStruct((rows, width), F32),
            jax.ShapeDtypeStruct((rows, width), F32),
        ),
        in_specs=[local, local, local, anywhere, anywhere, anywhere],
        out_specs=(anywhere, anywhere, anywhere, anywhere, local, local),
        scratch_shapes=[
            pltpu.VMEM((tokens, width), BF16),
            pltpu.VMEM((width, tokens), BF16),
            pltpu.VMEM((3, tokens, 2 * wide), BF16),
            pltpu.VMEM((chunks, tokens, 2 * wide), BF16),
            pltpu.VMEM((chunks, width, 2 * wide), BF16),
            pltpu.VMEM((hidden, width), BF16),
            pltpu.VMEM((tokens, width), F32),
            pltpu.VMEM((tokens, width), F32),
            pltpu.VMEM((tokens, 2 * wide), BF16),
            pltpu.VMEM((wide, tokens), BF16),
            pltpu.VMEM((chunks, 2, width, wide), BF16),
            pltpu.VMEM((chunks, wide, width), BF16),
            pltpu.VMEM((2, width, wide), BF16),
            pltpu.VMEM((2, wide, width), BF16),
            pltpu.VMEM((2, 3, rows, width), BF16),
            dma((3,)), dma((3,)), dma((chunks,)), dma((chunks,)),
            dma((2,)), dma((3, chunks)), dma((2, 3)), dma((2, 3)),
            *chain_semaphores(pieces),
        ],
        compiler_params=pltpu.CompilerParams(
            collective_id=1, has_side_effects=True, vmem_limit_bytes=63 << 20
        ),
        cost_estimate=pl.CostEstimate(
            flops=flops, bytes_accessed=200 << 20, transcendentals=tokens * hidden
        ),
    )(h, top, inner_grad, w_gate, w_up, w_down)


MISC = 88


def back_kernel(
    count, own_ref, turned_ref, w_main_ref, gates_ref, w_gates_ref, gated_ref, branch_ref,
    hat_ref, scale_ref, misc_ref,
    grads_ref, back_ref, inner_ref, sums_ref,
    came, across, total, landed, misc, misc_came, misc_landed, misc_home, acc, fold_src, fold_dst,
    inner_src, inner_dst,
    x_send, x_recv, y_send, y_recv, small_send, small_recv, *chain_sems,
):
    place = Place(count)
    side = place.side
    tokens, main = own_ref.shape
    rows = tokens // 2
    cols = 256
    parts = main // cols
    width = turned_ref.shape[0]
    high = gated_ref.shape[0]
    pieces = total.shape[0]
    place.meet()

    def cut(j):
        return pl.ds(j * cols, cols) if isinstance(j, int) else tile(j, cols)

    def over_x(j):
        return copy_to(
            own_ref.at[:, cut(j)], came.at[j], x_send.at[j], x_recv.at[j], place.x_peer
        )

    def over_y(j, mine):
        src = own_ref.at[:, cut(j)] if mine else came.at[j]
        return copy_to(src, across.at[j], y_send.at[j], y_recv.at[j], place.y_peer)

    for j in range(parts):
        over_x(j).start()

    @pl.when(side == 1)
    def _():
        for j in range(parts):
            over_y(j, True).start()

    def add(c, k, which):
        total[c] = (total[c].astype(F32) + landed[which, c].astype(F32)).astype(BF16)

    chain = Chain(
        place, pieces, 1,
        lambda c, k: total.at[c],
        lambda c, k, which: landed.at[which, c],
        lambda c, k, of: grads_ref.at[of * pieces + c],
        add, chain_sems[:9],
    )

    def add_misc(c, k, which):
        misc[...] += misc_landed[which]

    small = Chain(
        place, 1, 1,
        lambda c, k: misc,
        lambda c, k, which: misc_landed.at[which],
        lambda c, k, of: misc_home,
        add_misc, chain_sems[9:], share=False,
    )

    misc[...] = misc_ref[...]
    acc[...] = nt(gates_ref[...], w_gates_ref[...])

    @pl.loop(0, parts)
    def _(t):
        total[t] = nn(gated_ref[...], branch_ref[:, cut(t)]).astype(BF16)
        chain.step(t)
        over_x(t).wait_recv()

        @pl.when(side == 0)
        def _():
            over_y(t, False).start()

        acc[...] += nt(own_ref[:, cut(t)], w_main_ref[:, cut(t)])
        acc[...] += nt(came[t], w_main_ref[:, cut(parts + t)])

    fold = copy_to(fold_src, fold_dst, small_send.at[0], small_recv.at[0], place.core_peer)
    fold_src[...] = acc[rows:, :].astype(BF16)
    fold.start()

    def inner_copy():
        return copy_to(inner_src, inner_dst, small_send.at[1], small_recv.at[1], place.x_peer)

    def misc_copy(n, peer):
        return copy_to(
            misc, misc_came.at[n], small_send.at[2 + n], small_recv.at[2 + n], peer
        )

    row_at = lax.broadcasted_iota(jnp.int32, (MISC, 128), 0)

    def block(j, i):
        if i == 0:
            over_y(j, True).wait_recv()
        at_rows = pl.ds(i * high, high)
        first = jnp.where(side == 0, own_ref[:, cut(j)], came[j])
        total[parts + 2 * j + i] = (
            nn(turned_ref[at_rows, pl.ds(0, tokens)], first)
            + nn(turned_ref[at_rows, pl.ds(tokens, tokens)], across[j])
        ).astype(BF16)

    for n in range(2 * parts):
        block(n // 2, n % 2)
        chain.step(parts + n)
        if n == 0:
            fold.wait_recv()
            grad = acc[:rows, :] + fold_dst[...].astype(F32)
            back_ref[...] = grad
            found = grad * hat_ref[...]
            inner = jnp.sum(found * scale_ref[...], axis=1, keepdims=True)
            inner_src[...] = jnp.broadcast_to(inner, (rows, 128))
            inner_copy().start()
            gain = jnp.sum(found, axis=0, keepdims=True)
            for i in range(width // 128):
                misc[i : i + 1, :] = gain[:, i * 128 : (i + 1) * 128]
            misc_copy(0, place.core_peer).start()
        if n == 1:
            misc_copy(0, place.core_peer).wait()
            both = (row_at < 16) | (row_at >= 80)
            misc[...] += jnp.where(both, misc_came[0], 0.0)
            misc_copy(1, place.x_peer).start()
        if n == 2:
            misc_copy(1, place.x_peer).wait()
            misc[...] += jnp.where(row_at >= 80, misc_came[1], 0.0)
            misc_copy(2, place.y_peer).start()
        if n == 3:
            misc_copy(2, place.y_peer).wait()
            misc[...] += misc_came[2]
            inner_copy().wait()
            inner_ref[...] = inner_src[...] + inner_dst[...]
        if n > 3:
            small.step(n - 4)

    @pl.loop(3 * parts, chain.steps())
    def _(t):
        chain.step(t)

        @pl.when(t - parts - 4 < small.steps())
        def _():
            small.step(t - parts - 4)

    @pl.loop(chain.steps() - parts - 4, small.steps())
    def _(t):
        small.step(t)

    small.drain()
    sums_ref[...] = misc_home[...]
    chain.drain()
    fold.wait_send()
    for j in range(parts):
        over_x(j).wait_send()
        over_y(j, True).wait_send()


def back(own, turned, w_main, gates, w_gates, gated, branch, hat, scale, misc):
    count = lax.axis_size("group")
    tokens, main = own.shape
    rows = tokens // 2
    width = turned.shape[0]
    high = gated.shape[0]
    cols = 256
    parts = main // cols
    pieces = 3 * parts
    anywhere = pl.BlockSpec(memory_space=pl.ANY)
    local = pl.BlockSpec(memory_space=pltpu.VMEM)
    dma = pltpu.SemaphoreType.DMA
    return pl.pallas_call(
        functools.partial(back_kernel, count),
        out_shape=(
            jax.ShapeDtypeStruct((2 * pieces, high, cols), BF16),
            jax.ShapeDtypeStruct((rows, width), F32),
            jax.ShapeDtypeStruct((rows, 128), F32),
            jax.ShapeDtypeStruct((MISC, 128), F32),
        ),
        in_specs=[local] * 10,
        out_specs=(anywhere, local, local, local),
        scratch_shapes=[
            pltpu.VMEM((parts, tokens, cols), BF16),
            pltpu.VMEM((parts, tokens, cols), BF16),
            pltpu.VMEM((pieces, high, cols), BF16),
            pltpu.VMEM((2, pieces, high, cols), BF16),
            pltpu.VMEM((MISC, 128), F32),
            pltpu.VMEM((3, MISC, 128), F32),
            pltpu.VMEM((2, MISC, 128), F32),
            pltpu.VMEM((MISC, 128), F32),
            pltpu.VMEM((tokens, width), F32),
            pltpu.VMEM((rows, width), BF16),
            pltpu.VMEM((rows, width), BF16),
            pltpu.VMEM((rows, 128), F32),
            pltpu.VMEM((rows, 128), F32),
            dma((parts,)), dma((parts,)), dma((parts,)), dma((parts,)), dma((5,)), dma((5,)),
            *chain_semaphores(pieces), *chain_semaphores(1),
        ],
        compiler_params=pltpu.CompilerParams(
            collective_id=2, has_side_effects=True, vmem_limit_bytes=56 << 20
        ),
        cost_estimate=pl.CostEstimate(
            flops=2 * tokens * width * main * 6, bytes_accessed=100 << 20, transcendentals=0
        ),
    )(own, turned, w_main, gates, w_gates, gated, branch, hat, scale, misc)


def masked_scores(query, keys, segment, place, scale):
    scores = jnp.einsum("qkgd,skd->kgqs", query, keys, preferred_element_type=F32) * scale
    allowed = (segment[:, None] == segment[None, :]) & (place[None, :] <= place[:, None])
    return jnp.where(allowed, scores, NEGATIVE)


def body(
    tokens, lengths, norm_gain, w_query, w_key, w_value, w_head_gate, query_gain, key_gain,
    w_out, ffn_gain, w_gate, w_up, w_down, grad_out,
):
    row_count = lax.axis_size("row")
    rows, d_loc = tokens.shape
    group_tok = 2 * rows
    width = d_loc * row_count
    head_dim = query_gain.shape[0]
    q_half = w_query.shape[1] // 2
    kv_half = w_key.shape[1] // 2
    gate_half = w_head_gate.shape[1] // 2
    heads = q_half // head_dim
    kv_heads = kv_half // head_dim
    share = heads // kv_heads
    main = q_half + 2 * kv_half
    half_hidden = w_gate.shape[1] // 2
    scale = head_dim ** (-0.5)
    row_at = lax.axis_index("row")
    col_at = lax.axis_index("col")
    side = lax.axis_index("group") % 2

    steps = jnp.arange(rows, dtype=jnp.int32)
    index = jnp.concatenate([col_at * rows + steps, (1 - col_at) * rows + steps])
    segment, place = places(lengths, index)

    grad_group = jnp.concatenate([grad_out, swap(grad_out, "col")])
    grad_all = jnp.concatenate([grad_group, swap_groups(grad_group)])
    down_half = lax.dynamic_slice_in_dim(w_down, side * half_hidden, half_hidden, axis=0)
    inner_part = nt(grad_all, down_half)
    inner_grad = (inner_part + swap(inner_part.astype(BF16), "row").astype(F32)).astype(BF16)
    x_in = tokens.astype(F32)
    squares = jnp.sum(x_in * x_in, axis=1)
    inverse_one = lax.rsqrt((squares + swap(squares, "row")) / width + EPS)
    normed_one = (x_in * inverse_one[:, None] * norm_gain).astype(BF16)
    permuted = jnp.concatenate([normed_one, swap(normed_one, "col")])
    splits = [halves(w, 1, row_at) for w in (w_query, w_key, w_value, w_head_gate)]
    w_main = jnp.concatenate(
        [own for own, _ in splits[:3]] + [other for _, other in splits[:3]], axis=1
    )
    w_gates = jnp.pad(jnp.concatenate(splits[3], axis=1), ((0, 0), (0, 128 - 2 * gate_half)))
    partial = nn(permuted, w_main)
    partial_gates = nn(permuted, w_gates)
    away = jnp.concatenate(
        [partial[:, main:], partial_gates[:, gate_half : 2 * gate_half]], axis=1
    ).astype(BF16)
    stay = jnp.concatenate([partial[:, :main], partial_gates[:, :gate_half]], axis=1)
    turned = jnp.concatenate([permuted, swap_groups(permuted)]).T
    projected = stay + swap(away, "row").astype(F32)
    raw_query = projected[:, :q_half].reshape(group_tok, heads, head_dim)
    raw_key = projected[:, q_half : q_half + kv_half].reshape(group_tok, kv_heads, head_dim)
    raw_value = projected[:, q_half + kv_half : main].reshape(group_tok, kv_heads, head_dim)
    logit = projected[:, main:]
    query_inverse = lax.rsqrt(jnp.mean(raw_query * raw_query, axis=-1, keepdims=True) + EPS)
    key_inverse = lax.rsqrt(jnp.mean(raw_key * raw_key, axis=-1, keepdims=True) + EPS)
    cosines, sines = rope_tables(place, head_dim)
    cos_heads = cosines[:, None, :]
    sin_heads = sines[:, None, :]
    query = rotate(raw_query * query_inverse * query_gain, cos_heads, sin_heads).astype(BF16)
    keys = rotate(raw_key * key_inverse * key_gain, cos_heads, sin_heads).astype(BF16)
    values = raw_value.astype(BF16)
    query = query.reshape(group_tok, kv_heads, share, head_dim)

    scores = masked_scores(query, keys, segment, place, scale)
    top = jnp.max(scores, axis=-1, keepdims=True)
    raised = jnp.exp(scores - top)
    probs = raised / jnp.sum(raised, axis=-1, keepdims=True)
    probs_low = probs.astype(BF16)
    attended = jnp.einsum("kgqs,skd->qkgd", probs_low, values, preferred_element_type=F32)
    attended = attended.reshape(group_tok, heads, head_dim)
    gate_sigmoid = jax.nn.sigmoid(logit)
    gated = (attended * gate_sigmoid[:, :, None]).reshape(group_tok, q_half).astype(BF16)
    gated_came = swap(gated, "row")
    gated_all = jnp.concatenate([gated, gated_came], axis=1)
    first_side = side == 0
    gated_pair = jnp.concatenate(
        [
            jnp.where(first_side, gated, gated_came),
            swap_groups(jnp.where(first_side, gated_came, gated)),
        ]
    ).T
    w_back = jnp.concatenate(halves(w_out, 0, row_at))

    def sum_cores(values):
        return values[:rows] + swap(values[rows:].astype(BF16), "col").astype(F32)

    resid = x_in + sum_cores(nn(gated_all, w_back))
    squares = jnp.sum(resid * resid, axis=1)
    inverse_two = lax.rsqrt((squares + swap(squares, "row")) / width + EPS)
    normed_two = (resid * inverse_two[:, None] * ffn_gain).astype(BF16)

    pair_sum, down_sum, _, _, branch, d_normed_two = ffn(
        normed_two, grad_all, inner_grad, w_gate, w_up, w_down
    )
    output = (resid + branch).astype(BF16)

    d_top = grad_out.astype(F32)
    ffn_gain_part = jnp.sum(d_normed_two * resid * inverse_two[:, None], axis=0)
    scaled_two = d_normed_two * ffn_gain
    inner_two = jnp.sum(scaled_two * resid, axis=1)
    inner_two = inner_two + swap(inner_two, "row")
    d_resid = (
        d_top
        + inverse_two[:, None] * scaled_two
        - resid * (inverse_two**3 * inner_two / width)[:, None]
    )
    d_branch = d_resid.astype(BF16)
    branch_all = jnp.concatenate([d_branch, swap(d_branch, "col")])
    branch_across = swap_groups(d_branch)
    branch_pair = jnp.concatenate([branch_all, branch_across, swap(branch_across, "col")])
    d_gated_part = nt(branch_all, w_back)
    d_gated = d_gated_part[:, :q_half] + swap(
        d_gated_part[:, q_half:].astype(BF16), "row"
    ).astype(F32)
    d_gated = d_gated.reshape(group_tok, heads, head_dim)
    d_attended = (d_gated * gate_sigmoid[:, :, None]).astype(BF16)
    d_logit = jnp.sum(d_gated * attended, axis=-1) * gate_sigmoid * (1.0 - gate_sigmoid)
    d_attended = d_attended.reshape(group_tok, kv_heads, share, head_dim)

    d_probs = jnp.einsum("qkgd,skd->kgqs", d_attended, values, preferred_element_type=F32)
    d_scores = (probs * (d_probs - jnp.sum(d_probs * probs, axis=-1, keepdims=True))).astype(BF16)
    d_query = jnp.einsum("kgqs,skd->qkgd", d_scores, keys, preferred_element_type=F32) * scale
    d_keys = jnp.einsum("kgqs,qkgd->skd", d_scores, query, preferred_element_type=F32) * scale
    d_values = jnp.einsum("kgqs,qkgd->skd", probs_low, d_attended, preferred_element_type=F32)
    d_query = d_query.reshape(group_tok, heads, head_dim)
    d_raw_query, query_gain_part = head_norm_back(
        unrotate(d_query, cos_heads, sin_heads), raw_query, query_inverse, query_gain
    )
    d_raw_key, key_gain_part = head_norm_back(
        unrotate(d_keys, cos_heads, sin_heads), raw_key, key_inverse, key_gain
    )
    d_main = jnp.concatenate(
        [
            d_raw_query.reshape(group_tok, q_half),
            d_raw_key.reshape(group_tok, kv_half),
            d_values.reshape(group_tok, kv_half),
        ],
        axis=1,
    ).astype(BF16)
    d_gates = d_logit.astype(BF16)
    d_gates = jnp.concatenate([d_gates, swap(d_gates, "row")], axis=1)
    gates_part = lax.dot_general(
        d_gates, permuted, (((0,), (0,)), ((), ())), preferred_element_type=F32
    )
    misc = jnp.concatenate(
        [
            jnp.zeros((8, 128), F32),
            ffn_gain_part.reshape(8, 128),
            gates_part.reshape(64, 128),
            query_gain_part[None],
            key_gain_part[None],
            jnp.zeros((6, 128), F32),
        ]
    )
    hat = x_in * inverse_one[:, None]
    grads, d_normed_one, inner_one, sums = back(
        d_main, turned, w_main, jnp.pad(d_gates, ((0, 0), (0, 128 - 2 * gate_half))), w_gates,
        gated_pair, branch_pair, hat, norm_gain[None], misc,
    )
    input_grad = d_resid + inverse_one[:, None] * (
        d_normed_one * norm_gain - hat * (inner_one[:, :1] / width)
    )
    grad_norm_gain = sums[:8].reshape(d_loc)
    grad_ffn_gain = sums[8:16].reshape(d_loc)
    grad_gates = sums[16:80].reshape(2 * gate_half, d_loc)
    grad_head_gate = ordered(grad_gates[:gate_half], grad_gates[gate_half:], 0, row_at).T
    grads = grads.reshape(2, -1, q_half, 256)
    count = main // 256
    out_sum = grads[:, :count].transpose(0, 2, 1, 3).reshape(2 * q_half, d_loc)
    first_sum = (
        grads[:, count:]
        .reshape(2, count, 2, q_half, 256)
        .transpose(2, 3, 0, 1, 4)
        .reshape(d_loc, 2 * main)
    )

    def piece(start, size):
        own = first_sum[:, start : start + size]
        other = first_sum[:, main + start : main + start + size]
        return ordered(own, other, 1, row_at).astype(F32)

    grad_out_full = ordered(*jnp.split(out_sum, 2, axis=0), 0, row_at).astype(F32)
    return (
        output,
        input_grad,
        grad_norm_gain,
        piece(0, q_half),
        piece(q_half, kv_half),
        piece(q_half + kv_half, kv_half),
        grad_head_gate,
        sums[80],
        sums[81],
        grad_out_full,
        grad_ffn_gain,
        pair_sum[0].astype(F32),
        pair_sum[1].astype(F32),
        down_sum.astype(F32),
    )


def solution(mesh):
    shards = P(("group", "col"), "row")
    in_specs = (
        shards,
        P("group"),
        P("row"),
        P("row", "col"),
        P("row", "col"),
        P("row", "col"),
        P("row", "col"),
        P(),
        P(),
        P("col", "row"),
        P("row"),
        P("row", "col"),
        P("row", "col"),
        P("col", "row"),
        shards,
    )
    out_specs = (
        shards,
        shards,
        P("row"),
        P("row", "col"),
        P("row", "col"),
        P("row", "col"),
        P("row", "col"),
        P(),
        P(),
        P("col", "row"),
        P("row"),
        P("row", "col"),
        P("row", "col"),
        P("col", "row"),
    )
    return jax.shard_map(body, mesh=mesh, in_specs=in_specs, out_specs=out_specs, check_vma=False)
```

time: 943 us -> 818 us (0.87)
  waiting for transfers between devices: 249 us -> 66.1 us
  Pallas kernels: 335 us -> 476 us
  blocking collectives: 68.8 us -> 0 us
  other arithmetic: 83.9 us -> 111 us
  matrix products: 59.2 us -> 44.5 us
  between operations: 15.4 us -> 2.01 us
  starting transfers between devices: 21 us -> 11.3 us
    pallas_call x0 -> x1, Pallas kernels: none -> 122 us  [back(): pl.pallas_call(functools.partial(back_kernel, count), out_shape=(jax.Shap...]
    psum x1 -> x0, waiting for transfers between devices: 99.8 us -> none  [body(): first_sum = lax.psum(grad_first.astype(BF16), 'group')]
    ppermute x14 -> x13, waiting for transfers between devices: 132 us -> 56 us  [swap(): return lax.ppermute(values, axis, [(0, 1), (1, 0)])]
    psum x2 -> x0, blocking collectives: 68.8 us -> none  [the longest x1 43 us: body(): lax.psum((query_gain_part, key_gain_part), ('group', 'row', 'col'))]
    concatenate x2 -> x4, local copies, waits for them, and re-layouts: 36.9 us -> 7.58 us  [the longest x1 2.82 us: unrotate(): jnp.concatenate([scaled[..., half:], -scaled[..., :half]], axis=-1)]
    reshape x0 -> x11, local copies, waits for them, and re-layouts: none -> 23.7 us  [the longest x3 7.95 us: body(): raw_query = projected[:, :q_half].reshape(group_tok, heads, head_dim)]
    convert_element_type x2 -> x3, other arithmetic: 1.68 us -> 20.6 us  [the longest x1 13.2 us: body(): pair_sum[1].astype(F32)]
    pallas_call x1, Pallas kernels: 335 us -> 353 us  [ffn(): pl.pallas_call(functools.partial(ffn_kernel, count, chunks), out_shape=(j...]
  transfers between devices with their start and end apart: 16 -> 17, of which waited for: 9 -> 6; matrix products, arithmetic and copies ran while one was open for 14% -> 23% of each run, Pallas kernels for 0% -> 44%
where the time goes in v2:
time: 818 us; the launch traced here: 809 us
  Pallas kernels  476 us (58%)
  other arithmetic  111 us (14%)
  local copies, waits for them, and re-layouts  98.8 us (12%)
  waiting for transfers between devices  66.1 us (8%)
  matrix products  44.5 us (5%)
  starting transfers between devices  11.3 us (1%)
    pallas_call x1, Pallas kernels, ffn(): pl.pallas_call(functools.partial(ffn_kernel, count, chunks), out_shape=(j...  353 us
    pallas_call x1, Pallas kernels, back(): pl.pallas_call(functools.partial(back_kernel, count), out_shape=(jax.Shap...  122 us
    ppermute x13, waiting for transfers between devices, swap(): return lax.ppermute(values, axis, [(0, 1), (1, 0)])  56 us
    unnamed x197, local copies, waits for them, and re-layouts  20.2 us
  transfers between devices with their start and end apart: 17, of which 6 were waited for; matrix products, arithmetic and copies ran while one was open for 23% of the time, Pallas kernels for 44%

profile of v2, /device:TPU:24, one launch (start us, length us, event | category | flops | bytes accessed | tf_op | source)
XLA Modules:
  0.0 809.0 jit_solution(9749812492519855574)
XLA Ops:
  25.1 4.2 fusion.70
  38.5 3.7 slice.160
  42.2 10.1 %collective-permute-done.7 = bf16[640,1024]{1,0:T(8,128)(2,1)} collective-permute-done((bf16[640,1024]{1,0:T(8,128)(2,1)}, bf16[640,1024]{1,0:T(8,128)(2,1)}, u32[]{:S(2)}, u32[]{:S(2)}) %collective-permute-start.7) | collective-permute-done | bytes 1310752 | tf_op jit(solution)/shard_map/ppermute | solution.py:24
  53.8 9.8 %fusion.68 = (bf16[1280,1536]{1,0:T(8,128)(2,1)}, f32[1280,1536]{1,0:T(8,128)}) fusion(bf16[1280,1024]{1,0:T(8,128)(2,1)S(1)} %constant_dynamic-update-slice_fusion.top_ref, bf16[3072,1024]{1,0:T(8,128)(2,1)} %down_ref.1, s32[]{:T(128)S(6)} %select_n.156), kind=kOutput, calls=%fused_computation.188 | convolution fusion | flops 4028497920 | bytes 17563652 | tf_op jit(solution)/shard_map/dot_general | solution.py:82
  104.2 5.1 fusion.67
  109.4 3.8 fusion.12
  114.3 49.5 %collective-permute-done.3 = bf16[640,512]{0,1:T(8,128)(2,1)S(1)} collective-permute-done((bf16[640,512]{0,1:T(8,128)(2,1)S(1)}, bf16[640,512]{0,1:T(8,128)(2,1)S(1)}, u32[]{:S(2)}, u32[]{:S(2)}) %collective-permute-start.3) | collective-permute-done | bytes 655392 | tf_op jit(solution)/shard_map/ppermute | solution.py:19
  174.1 7.6 add_convert_fusion.inner_grad_ref
  181.7 353.2 %shard_map.254 = (bf16[2,1024,3072]{2,1,0:T(8,128)(2,1)}, bf16[3072,1024]{1,0:T(8,128)(2,1)}, bf16[2,12,2,1024,128]{4,3,2,1,0:T(8,128)(2,1)}, bf16[2,12,128,1024...) custom-call(bf16[320,1024]{1,0:T(8,128)(2,1)} %multiply_convert_fusion.1.h_ref, ...), custom_call_target="tpu_custom_call" | custom-call | flops 32212254720 | bytes 209715200 | tf_op jit(solution)/shard_map/pallas_call | solution.py:469
  548.0 3.2 maximum_bitcast_fusion
  551.2 4.4 copy.355.turned_ref
  561.2 2.8 fusion.14
  565.4 13.2 %bitcast_convert_fusion = (f32[1024,3072]{1,0:T(8,128)}, f32[1024,3072]{1,0:T(8,128)}) fusion(bf16[2,1024,3072]{2,1,0:T(8,128)(2,1)} %get-tuple-element.28), kind=kLoop, calls=%fused_computation.9 | loop fusion | flops 6291456 | bytes 37748736 | tf_op jit(solution)/shard_map/convert_element_type | solution.py:916
  578.6 6.3 convert_element_type.138
  588.7 6.6 fusion.1
  595.3 4.7 fusion.36
  602.4 5.7 fusion.3
  629.2 2.8 pad_maximum_fusion.branch_ref
  637.9 122.5 %shard_map.255 = (bf16[24,512,256]{2,1,0:T(8,128)(2,1)}, f32[320,1024]{1,0:T(8,128)}, f32[320,128]{1,0:T(8,128)}, f32[88,128]{1,0:T(8,128)}) custom-call(bf16[640,1024]{1,0:T(8,128)(2,1)} %pad_maximum_fusion.8.own_ref, bf16[1024,1280]{1,0:T(8,128)(2,1)} %copy.355.turned_ref, bf16[1024,2048]{1,0:T(8,128)(2,1)} %select_dynamic-update-slice_fusion.2.w_main_ref, ...), custom_call_target="tpu_custom_call" | custom-call | flops 8053063680 | bytes 104857600 | tf_op jit(solution)/shard_map/pallas_call | solution.py:679
  764.6 5.3 copy.356
  769.9 7.7 reshape.273
  777.6 3.1 broadcast_select_fusion.9
  787.8 3.8 maximum_convert_fusion.1
  791.6 5.4 copy.359
  (355 shorter events, 162.4 us)
Async XLA Ops:
  2.0 12.4 %collective-permute-start = (f32[320]{0:T(512)S(1)}, f32[320]{0:T(512)S(1)}, u32[]{:S(2)}, u32[]{:S(2)}) collective-permute-start(f32[320]{0:T(512)S(1)} %fusion.16), channel_id=1, source_target_pairs={{0,2},{2,0},{1,3},{3,1},{4,6},{6,4},{5,7},{7,5},{8,10},{10,8},{9,1... | collective-permute-start | bytes 3848 | tf_op jit(solution)/shard_map/ppermute | solution.py:19
  3.5 15.4 %collective-permute-start.6 = (bf16[320,1024]{1,0:T(8,128)(2,1)}, bf16[320,1024]{1,0:T(8,128)(2,1)}, u32[]{:S(2)}, u32[]{:S(2)}) collective-permute-start(bf16[320,1024]{1,0:T(8,128)(2,1)} %param.29), channel_id=1, source_target_pairs={{0,1},{1,0},{2,3},{3,2},{4,5},{5,4},{6,7},{7,6},{8,9},{9,8},{10,11... | collective-permute-start | bytes 1966088 | tf_op jit(solution)/shard_map/ppermute | solution.py:19
  15.7 7.1 collective-permute-start.1
  21.3 31.0 %collective-permute-start.7 = (bf16[640,1024]{1,0:T(8,128)(2,1)}, bf16[640,1024]{1,0:T(8,128)(2,1)}, u32[]{:S(2)}, u32[]{:S(2)}) collective-permute-start(bf16[640,1024]{1,0:T(8,128)(2,1)} %pad_maximum_fusion.6), channel_id=1, source_target_pairs={{0,4},{4,0},{8,12},{12,8},{16,20},{20,16},{24,28},{28,24},{1,5},{5... | collective-permute-start | bytes 3932168 | tf_op jit(solution)/shard_map/ppermute | solution.py:24
  34.8 30.7 %collective-permute-start.2 = (bf16[640,1028]{0,1:T(8,128)(2,1)S(1)}, bf16[640,1028]{0,1:T(8,128)(2,1)S(1)}, u32[]{:S(2)}, u32[]{:S(2)}) collective-permute-start(bf16[640,1028]{0,1:T(8,128)(2,1)S(1)} %copy.319), channel_id=1, source_target_pairs={{0,2},{2,0},{1,3},{3,1},{4,6},{6,4},{5,7},{7,5},{8,10},{10,8},{9,1... | collective-permute-start | bytes 3947528 | tf_op jit(solution)/shard_map/ppermute | solution.py:19
  38.5 13.8 %copy-start.65 = (bf16[1280,1024]{1,0:T(8,128)(2,1)S(1)}, bf16[1280,1024]{1,0:T(8,128)(2,1)}, u32[]{:S(2)}) copy-start(bf16[1280,1024]{1,0:T(8,128)(2,1)} %constant_dynamic-update-slice_fusion.1) | copy-start | bytes 7864324
  63.5 110.6 %collective-permute-start.8 = (bf16[1280,1536]{1,0:T(8,128)(2,1)}, bf16[1280,1536]{1,0:T(8,128)(2,1)}, u32[]{:S(2)}, u32[]{:S(2)}) collective-permute-start(bf16[1280,1536]{1,0:T(8,128)(2,1)} %get-tuple-element.175), channel_id=1, source_target_pairs={{0,2},{2,0},{1,3},{3,1},{4,6},{6,4},{5,7},{7,5},{8,10},{10,8},{9,1... | collective-permute-start | bytes 11796488 | tf_op jit(solution)/shard_map/ppermute | solution.py:19
  70.3 20.2 %copy-start.2 = (f32[640,1028]{1,0:T(8,128)}, f32[640,1028]{1,0:T(8,128)S(1)}, u32[]{:S(2)}) copy-start(f32[640,1028]{1,0:T(8,128)S(1)} %maximum_add_fusion) | copy-start | bytes 7895044
  113.3 50.5 %copy-start.35 = (bf16[640,512]{0,1:T(8,128)(2,1)}, bf16[640,512]{0,1:T(8,128)(2,1)S(1)}, u32[]{:S(2)}) copy-start(bf16[640,512]{0,1:T(8,128)(2,1)S(1)} %fusion.28) | copy-start | bytes 1966084
  113.3 50.5 %collective-permute-start.3 = (bf16[640,512]{0,1:T(8,128)(2,1)S(1)}, bf16[640,512]{0,1:T(8,128)(2,1)S(1)}, u32[]{:S(2)}, u32[]{:S(2)}) collective-permute-start(bf16[640,512]{0,1:T(8,128)(2,1)S(1)} %fusion.28), channel_id=1, source_target_pairs={{0,2},{2,0},{1,3},{3,1},{4,6},{6,4},{5,7},{7,5},{8,10},{10,8},{9,1... | collective-permute-start | bytes 1966088 | tf_op jit(solution)/shard_map/ppermute | solution.py:19
  114.3 51.1 %copy-start.54 = (bf16[512,1024]{1,0:T(8,128)(2,1)}, bf16[512,1024]{1,0:T(8,128)(2,1)S(1)}, u32[]{:S(2)}) copy-start(bf16[512,1024]{1,0:T(8,128)(2,1)S(1)} %get-tuple-element.137) | copy-start | bytes 3145732
  114.3 51.1 %copy-start.56 = (bf16[512,1024]{1,0:T(8,128)(2,1)}, bf16[512,1024]{1,0:T(8,128)(2,1)S(1)}, u32[]{:S(2)}) copy-start(bf16[512,1024]{1,0:T(8,128)(2,1)S(1)} %get-tuple-element.138) | copy-start | bytes 3145732
  165.5 2.2 collective-permute-start.4
  168.1 3.7 collective-permute-start.5
  168.7 379.3 %collective-permute-start.12 = (bf16[640,1024]{1,0:T(8,128)(2,1)}, bf16[640,1024]{1,0:T(8,128)(2,1)}, u32[]{:S(2)}, u32[]{:S(2)}) collective-permute-start(bf16[640,1024]{1,0:T(8,128)(2,1)} %pad_maximum_fusion.5), channel_id=1, source_target_pairs={{0,4},{4,0},{8,12},{12,8},{16,20},{20,16},{24,28},{28,24},{1,5},{5... | collective-permute-start | bytes 3932168 | tf_op jit(solution)/shard_map/ppermute | solution.py:24
  537.8 3.6 collective-permute-start.9
  539.5 18.6 %collective-permute-start.14 = (bf16[640,512]{0,1:T(8,128)(2,1)}, bf16[640,512]{0,1:T(8,128)(2,1)}, u32[]{:S(2)}, u32[]{:S(2)}) collective-permute-start(bf16[640,512]{0,1:T(8,128)(2,1)} %get-tuple-element.142), channel_id=1, source_target_pairs={{0,4},{4,0},{8,12},{12,8},{16,20},{20,16},{24,28},{28,24},{1,5},{5... | collective-permute-start | bytes 1966088 | tf_op jit(solution)/shard_map/ppermute | solution.py:24
  542.7 18.5 %collective-permute-start.10 = (bf16[320,1024]{1,0:T(8,128)(2,1)}, bf16[320,1024]{1,0:T(8,128)(2,1)}, u32[]{:S(2)}, u32[]{:S(2)}) collective-permute-start(bf16[320,1024]{1,0:T(8,128)(2,1)} %fusion.62), channel_id=1, source_target_pairs={{0,1},{1,0},{2,3},{3,2},{4,5},{5,4},{6,7},{7,6},{8,9},{9,8},{10,11... | collective-permute-start | bytes 1966088 | tf_op jit(solution)/shard_map/ppermute | solution.py:19
  560.6 24.2 %collective-permute-start.15 = (bf16[320,1024]{1,0:T(8,128)(2,1)}, bf16[320,1024]{1,0:T(8,128)(2,1)}, u32[]{:S(2)}, u32[]{:S(2)}) collective-permute-start(bf16[320,1024]{1,0:T(8,128)(2,1)} %fusion.62), channel_id=1, source_target_pairs={{0,4},{4,0},{8,12},{12,8},{16,20},{20,16},{24,28},{28,24},{1,5},{5... | collective-permute-start | bytes 1966088 | tf_op jit(solution)/shard_map/ppermute | solution.py:24
  564.0 14.5 %slice-start = ((s8[6291456]{0:T(1024)(128)(4,1)}), s8[4194304]{0:T(1024)(128)(4,1)S(1)}, s32[]{:S(2)}) async-start(s8[6291456]{0:T(1024)(128)(4,1)} %bitcast.153), calls=%async_computation | async-start | bytes 8388608
  564.1 20.8 %collective-permute-start.11 = (bf16[640,512]{1,0:T(8,128)(2,1)S(1)}, bf16[640,512]{1,0:T(8,128)(2,1)S(1)}, u32[]{:S(2)}, u32[]{:S(2)}) collective-permute-start(bf16[640,512]{1,0:T(8,128)(2,1)S(1)} %slice.237), channel_id=1, source_target_pairs={{0,2},{2,0},{1,3},{3,1},{4,6},{6,4},{5,7},{7,5},{8,10},{10,8},{9,1... | collective-permute-start | bytes 1966088 | tf_op jit(solution)/shard_map/ppermute | solution.py:19
  565.4 13.2 %slice-start.1 = ((s8[6291456]{0:T(1024)(128)(4,1)}), s8[2097152]{0:T(1024)(128)(4,1)S(1)}, s32[]{:S(2)}) async-start(s8[6291456]{0:T(1024)(128)(4,1)} %bitcast.153), calls=%async_computation.1 | async-start | bytes 4194304
  584.9 44.3 %collective-permute-start.16 = (bf16[320,1024]{1,0:T(8,128)(2,1)}, bf16[320,1024]{1,0:T(8,128)(2,1)}, u32[]{:S(2)}, u32[]{:S(2)}) collective-permute-start(bf16[320,1024]{1,0:T(8,128)(2,1)} %collective-permute-done.15), channel_id=1, source_target_pairs={{0,1},{1,0},{2,3},{3,2},{4,5},{5,4},{6,7},{7,6},{8,9},{9,8},{10,11... | collective-permute-start | bytes 1966088 | tf_op jit(solution)/shard_map/ppermute | solution.py:19
  601.3 30.8 %collective-permute-start.13 = (bf16[640,4]{1,0:T(8,128)(2,1)S(1)}, bf16[640,4]{1,0:T(8,128)(2,1)}, u32[]{:S(2)}, u32[]{:S(2)}) collective-permute-start(bf16[640,4]{1,0:T(8,128)(2,1)S(1)} %multiply_convert_fusion.3), channel_id=1, source_target_pairs={{0,2},{2,0},{1,3},{3,1},{4,6},{6,4},{5,7},{7,5},{8,10},{10,8},{9,1... | collective-permute-start | bytes 15368 | tf_op jit(solution)/shard_map/ppermute | solution.py:19
  (90 other events, 317.0 us)

commit v3 on v2

--- a/solution.py
+++ b/solution.py
@@ -76,6 +76,10 @@
 
 
 TILE = 256
+HOP = 1
+WIDE = 128
+EARLY = 6
+AHEAD = 3
 
 
 def nt(a, b):
@@ -164,11 +168,25 @@
             src, self.home(c, k, of), self.sems[7].at[p], self.sems[8].at[p], self.place.y_peer
         )
 
-    def step(self, t):
+    def step(self, u, hop=1):
         at, line, root, deep = self.place.at, self.place.line, self.place.root, self.place.deep
-        c = t - jnp.where(at < root, at, jnp.where(at > root, line - 1 - at, deep))
-        live = (c >= 0) & (c < self.chunks)
-        for k in range(self.kinds):
+        behind = jnp.where(at < root, at, jnp.where(at > root, line - 1 - at, deep))
+        self.inward(u - hop * behind)
+        self.outward(u - hop * (deep + jnp.abs(at - root)))
+
+    def kinds_of(self, p):
+        live = (p >= 0) & (p < self.kinds * self.chunks)
+        if self.kinds == 1:
+            return [(live, p, 0)]
+        p = jnp.maximum(p, 0)
+        return [
+            (live & (lax.rem(p, self.kinds) == k), lax.div(p, self.kinds), k)
+            for k in range(self.kinds)
+        ]
+
+    def inward(self, piece):
+        at, line, root = self.place.at, self.place.line, self.place.root
+        for live, c, k in self.kinds_of(piece):
 
             @pl.when(live & (at < root))
             def _():
@@ -204,10 +222,11 @@
                     self.share_copy(c, k, True).start()
                 self.keep_copy(c, k).start()
 
-        c = t - deep - jnp.abs(at - root)
-        for k in range(self.kinds):
-
-            @pl.when((c >= 0) & (c < self.chunks) & (at != root))
+    def outward(self, piece):
+        at, root = self.place.at, self.place.root
+        for live, c, k in self.kinds_of(piece):
+
+            @pl.when(live & (at != root))
             def _():
                 self.final_copy(c, k, True, False).wait_recv()
 
@@ -222,8 +241,8 @@
                 if self.share:
                     self.share_copy(c, k, False).start()
 
-    def steps(self):
-        return self.chunks + 2 * self.place.deep
+    def steps(self, hop=1):
+        return self.kinds * self.chunks + 2 * hop * self.place.deep
 
     def drain(self):
         at, line, root = self.place.at, self.place.line, self.place.root
@@ -265,11 +284,12 @@
 
 
 def ffn_kernel(
-    count, chunks, h_ref, top_ref, inner_grad_ref, gate_ref, up_ref, down_ref,
-    pair_grads_ref, down_grads_ref, pair_came_ref, down_came_ref, branch_ref, back_ref,
-    h_all, h_turned, sent, came, w_pair, w_down, acc_branch, acc_back, parts, inner_turned,
+    count, chunks, h_ref, top_ref, early_ref, gate_ref, up_ref, down_ref,
+    pair_grads_ref, down_grads_ref, pair_came_ref, down_came_ref, branch_ref, branch_out_ref,
+    back_ref,
+    h_all, h_turned, sent, came, top_sent, top_came, grad_part, w_pair, w_down, acc_branch, acc_back, parts, inner_turned,
     pair_total, down_total, pair_stage, down_stage, reduce_recv,
-    gather_send, gather_recv, x_send, x_recv, load_sem, weight_sem, fold_send, fold_recv,
+    gather_send, gather_recv, x_send, x_recv, top_send, top_recv, load_sem, weight_sem, fold_send, fold_recv,
     *chain_sems,
 ):
     place = Place(count)
@@ -313,6 +333,30 @@
     )
     to_y.start()
     to_core.start()
+
+    def top_exchange(j):
+        n = j - EARLY
+        return copy_to(
+            top_sent.at[n], top_came.at[n], top_send.at[n], top_recv.at[n], place.x_peer
+        )
+
+    def top_project(j):
+        @pl.loop(0, tiles)
+        def _(i):
+            top_sent[j - EARLY, tile(i), :] = nt(
+                top_ref[tile(i), :], w_down[tile(j, wide), :]
+            ).astype(BF16)
+
+        top_exchange(j).start()
+
+    @pl.loop(0, chunks)
+    def _(j):
+        weight_copies(j)[2].wait()
+
+    @pl.loop(EARLY, min(EARLY + AHEAD, chunks))
+    def _(j):
+        top_project(j)
+
     h_all[slot(0), :] = h_ref[...]
     acc_branch[...] = jnp.zeros_like(acc_branch)
     acc_back[...] = jnp.zeros_like(acc_back)
@@ -327,7 +371,7 @@
         )
 
     def project(j):
-        for copy in weight_copies(j):
+        for copy in weight_copies(j)[:2]:
             copy.wait()
 
         @pl.loop(0, tiles)
@@ -338,13 +382,22 @@
 
     def work(j):
         exchange(j).wait_recv()
+
+        @pl.when(j < EARLY)
+        def _():
+            grad_part[...] = early_ref[:, tile(j, wide)].astype(F32)
+
+        @pl.when(j >= EARLY)
+        def _():
+            top_exchange(j).wait_recv()
+            grad_part[...] = top_sent[j - EARLY].astype(F32) + top_came[j - EARLY].astype(F32)
 
         @pl.loop(0, tiles)
         def _(i):
             at_rows = tile(i)
             pair = sent[lax.rem(j, 3), at_rows, :].astype(F32) + came[j, at_rows, :].astype(F32)
             gate, up = pair[:, :wide], pair[:, wide:]
-            grad = inner_grad_ref[at_rows, tile(j, wide)].astype(F32)
+            grad = grad_part[at_rows, :]
             sig = 1.0 / (1.0 + jnp.exp(-gate))
             silu = gate * sig
             parts[at_rows, pl.ds(0, wide)] = (
@@ -356,6 +409,7 @@
             acc_branch[at_rows, :] += nn(inner, w_down[tile(j, wide), :])
             acc_back[at_rows, :] += nt(parts[at_rows, :], w_pair[j])
 
+    def gradients(j):
         @pl.loop(0, width // TILE)
         def _(i):
             pair = nn(h_turned[tile(i), :], parts[...])
@@ -398,6 +452,11 @@
 
     @pl.loop(0, chunks)
     def _(t):
+        work(t)
+        chain.step(3 * t - 1, HOP)
+        gradients(t)
+        chain.step(3 * t, HOP)
+
         @pl.when(t + 2 < chunks)
         def _():
             @pl.when(t >= 1)
@@ -406,14 +465,17 @@
 
             project(t + 2)
 
-        work(t)
-        chain.step(t)
-
-    folded = ((acc_back, back_ref), (acc_branch, branch_ref))
+        @pl.when(EARLY + AHEAD + t < chunks)
+        def _():
+            top_project(EARLY + AHEAD + t)
+
+        chain.step(3 * t + 1, HOP)
+
+    chain.step(3 * chunks - 1, HOP)
 
     def fold_source(n, i):
         if i == 2:
-            return w_down.at[slot(n), :]
+            return w_down.at[slot(0), :]
         return h_all.at[slot(2 * n + i), :]
 
     def fold(n, i):
@@ -425,23 +487,27 @@
     to_y.wait_send()
     to_core.wait_send()
     forward.wait_send()
-    for n, (acc, _) in enumerate(folded):
+    for n, acc in enumerate((acc_back, acc_branch)):
         for i in (1, 0):
             fold_source(n, i)[...] = acc[slot(2 * i + 1), :].astype(BF16)
             fold(n, i).start()
-    for n, (acc, _) in enumerate(folded):
-        fold(n, 1).wait_recv()
-        fold_source(n, 2)[...] = (acc[slot(2), :] + reduce_recv[n, 1].astype(F32)).astype(BF16)
-        fold(n, 2).start()
-    chain.step(chunks)
-    for n, (acc, out) in enumerate(folded):
-        fold(n, 0).wait_recv()
-        fold(n, 2).wait_recv()
-        out[...] = acc[slot(0), :] + reduce_recv[n, 0].astype(F32) + reduce_recv[n, 2].astype(F32)
-
-    @pl.loop(chunks + 1, chain.steps())
-    def _(t):
-        chain.step(t)
+    fold(0, 1).wait_recv()
+    fold_source(0, 2)[...] = (acc_back[slot(2), :] + reduce_recv[0, 1].astype(F32)).astype(BF16)
+    fold(0, 2).start()
+    chain.step(3 * chunks, HOP)
+    fold(1, 0).wait_recv()
+    fold(1, 1).wait_recv()
+    branch_ref[...] = acc_branch[slot(0), :] + reduce_recv[1, 0].astype(F32)
+    branch_out_ref[...] = (acc_branch[slot(2), :] + reduce_recv[1, 1].astype(F32)).astype(BF16)
+    fold(0, 0).wait_recv()
+    fold(0, 2).wait_recv()
+    back_ref[...] = (
+        acc_back[slot(0), :] + reduce_recv[0, 0].astype(F32) + reduce_recv[0, 2].astype(F32)
+    )
+
+    @pl.loop(3 * chunks + 1, chain.steps(HOP))
+    def _(u):
+        chain.step(u, HOP)
 
     chain.drain()
 
@@ -449,16 +515,19 @@
     def _(j):
         exchange(j).wait_send()
 
-    for n in range(2):
-        for i in range(3):
-            fold(n, i).wait_send()
-
-
-def ffn(h, top, inner_grad, w_gate, w_up, w_down):
+    @pl.loop(EARLY, chunks)
+    def _(j):
+        top_exchange(j).wait_send()
+
+    for n, i in ((0, 0), (0, 1), (0, 2), (1, 0), (1, 1)):
+        fold(n, i).wait_send()
+
+
+def ffn(h, top, early, w_gate, w_up, w_down):
     count = lax.axis_size("group")
     rows, width = h.shape
     hidden = w_gate.shape[1] // 2
-    wide = 128
+    wide = WIDE
     chunks = hidden // wide
     tokens = 4 * rows
     anywhere = pl.BlockSpec(memory_space=pl.ANY)
@@ -474,15 +543,19 @@
             jax.ShapeDtypeStruct((2, chunks, 2, width, wide), BF16),
             jax.ShapeDtypeStruct((2, chunks, wide, width), BF16),
             jax.ShapeDtypeStruct((rows, width), F32),
+            jax.ShapeDtypeStruct((rows, width), BF16),
             jax.ShapeDtypeStruct((rows, width), F32),
         ),
         in_specs=[local, local, local, anywhere, anywhere, anywhere],
-        out_specs=(anywhere, anywhere, anywhere, anywhere, local, local),
+        out_specs=(anywhere, anywhere, anywhere, anywhere, local, local, local),
         scratch_shapes=[
             pltpu.VMEM((tokens, width), BF16),
             pltpu.VMEM((width, tokens), BF16),
             pltpu.VMEM((3, tokens, 2 * wide), BF16),
             pltpu.VMEM((chunks, tokens, 2 * wide), BF16),
+            pltpu.VMEM((chunks - EARLY, tokens, wide), BF16),
+            pltpu.VMEM((chunks - EARLY, tokens, wide), BF16),
+            pltpu.VMEM((tokens, wide), F32),
             pltpu.VMEM((chunks, width, 2 * wide), BF16),
             pltpu.VMEM((hidden, width), BF16),
             pltpu.VMEM((tokens, width), F32),
@@ -495,6 +568,7 @@
             pltpu.VMEM((2, wide, width), BF16),
             pltpu.VMEM((2, 3, rows, width), BF16),
             dma((3,)), dma((3,)), dma((chunks,)), dma((chunks,)),
+            dma((chunks - EARLY,)), dma((chunks - EARLY,)),
             dma((2,)), dma((3, chunks)), dma((2, 3)), dma((2, 3)),
             *chain_semaphores(pieces),
         ],
@@ -504,7 +578,299 @@
         cost_estimate=pl.CostEstimate(
             flops=flops, bytes_accessed=200 << 20, transcendentals=tokens * hidden
         ),
-    )(h, top, inner_grad, w_gate, w_up, w_down)
+    )(h, top, early, w_gate, w_up, w_down)
+
+
+ROWS = 128
+
+
+def sigmoid(v):
+    return 1.0 / (1.0 + jnp.exp(-v))
+
+
+def column(values):
+    return jnp.broadcast_to(values, (values.shape[0], 128))
+
+
+def front_kernel(
+    count, heads, kv_heads, tok_ref, top_ref, norm_ref, second_ref, q_gain_ref, k_gain_ref,
+    cos_ref, sin_ref, at_ref, start_ref, key_at_ref, w_gates_ref, wq_ref, wk_ref, wv_ref, wo_ref,
+    wd_ref,
+    h_ref, resid_ref, inv_two_ref, hat_ref, inv_one_ref, normed_ref, tops_ref, early_ref,
+    raw_ref, sig_ref, q_ref, k_ref, v_ref, log_ref, attended_ref, gated_ref,
+    wq, wk, wv, wo, wd, kv_send, kv_came, q_send, q_came, gates, early_send, early_came,
+    ss_send, ss_came, fold_src, fold_dst, acc,
+    w_sem, n_send, n_recv, t_send, t_recv, p_send, p_recv, e_send, e_recv, g_send, g_recv,
+    s_send, s_recv,
+):
+    place = Place(count)
+    rows, width = tok_ref.shape
+    tokens = 2 * rows
+    row_at = lax.axis_index("row")
+    side = place.side
+    hd = 128
+    qw, kw = heads * hd, kv_heads * hd
+    hidden = wd_ref.shape[0] // 2
+    scale = hd**-0.5
+
+    loads = []
+    for i, at in enumerate((row_at, 1 - row_at)):
+        q_cols, k_cols = tile(at, qw), tile(at, kw)
+        loads += [
+            pltpu.make_async_copy(wk_ref.at[:, k_cols], wk.at[i], w_sem.at[i, 0]),
+            pltpu.make_async_copy(wv_ref.at[:, k_cols], wv.at[i], w_sem.at[i, 1]),
+            pltpu.make_async_copy(wq_ref.at[:, q_cols], wq.at[i], w_sem.at[i, 2]),
+            pltpu.make_async_copy(wo_ref.at[q_cols, :], wo.at[i], w_sem.at[i, 3]),
+        ]
+    down_rows = pl.ds(pl.multiple_of(side * hidden, WIDE), wd.shape[0])
+    loads.append(pltpu.make_async_copy(wd_ref.at[down_rows, :], wd, w_sem.at[0, 4]))
+    for copy in loads:
+        copy.start()
+    place.meet()
+
+    def slot(i):
+        return pl.ds(i * rows, rows)
+
+    def spread(ref, sends, recvs):
+        own, core, pair, both = (ref.at[slot(i), :] for i in range(4))
+        return (
+            copy_to(own, core, sends.at[0], recvs.at[0], place.core_peer),
+            copy_to(own, pair, sends.at[1], recvs.at[1], place.y_peer),
+            copy_to(pair, both, sends.at[2], recvs.at[2], place.core_peer),
+        )
+
+    tops_ref[slot(0), :] = top_ref[...]
+    tops = spread(tops_ref, t_send, t_recv)
+    tops[0].start()
+    tops[1].start()
+
+    def squares(n):
+        return copy_to(ss_send.at[n], ss_came.at[n], s_send.at[n], s_recv.at[n], place.x_peer)
+
+    x = tok_ref[...].astype(F32)
+    ss_send[0] = column(jnp.sum(x * x, axis=1, keepdims=True))
+    squares(0).start()
+
+    def early(i):
+        return copy_to(
+            early_send.at[slot(i), :], early_came.at[slot(i), :], e_send.at[i], e_recv.at[i],
+            place.x_peer,
+        )
+
+    def early_start(i):
+        early_send[slot(i), :] = nt(tops_ref[slot(i), :], wd[...]).astype(BF16)
+        early(i).start()
+
+    loads[-1].wait()
+    early_start(0)
+    squares(0).wait()
+    inv_one = lax.rsqrt((ss_send[0] + ss_came[0]) / (2 * width) + EPS)
+    inv_one_ref[...] = inv_one
+    hat = tok_ref[...].astype(F32) * inv_one[:, :1]
+    hat_ref[...] = hat
+    normed_ref[slot(0), :] = (hat * norm_ref[...]).astype(BF16)
+    normed = spread(normed_ref, n_send, n_recv)
+    normed[0].start()
+    normed[1].start()
+
+    kv_copy = copy_to(kv_send, kv_came, p_send.at[0], p_recv.at[0], place.x_peer)
+    q_copy = copy_to(q_send, q_came, p_send.at[1], p_recv.at[1], place.x_peer)
+    for copy in loads[:-1]:
+        copy.wait()
+    for i in range(2):
+        if i == 1:
+            normed[0].wait_recv()
+        rows_in = normed_ref[slot(i), :]
+        kv_send[slot(i), pl.ds(0, kw)] = nn(rows_in, wk[1]).astype(BF16)
+        kv_send[slot(i), pl.ds(kw, kw)] = nn(rows_in, wv[1]).astype(BF16)
+    kv_copy.start()
+    for i in range(2):
+        rows_in = normed_ref[slot(i), :]
+        q_send[slot(i), pl.ds(0, qw)] = nn(rows_in, wq[1]).astype(BF16)
+        part = nn(rows_in, w_gates_ref[...])
+        gates[slot(i), :] = part
+        q_send[slot(i), pl.ds(qw, 128)] = part.astype(BF16)
+    q_copy.start()
+    for i in range(2):
+        rows_in = normed_ref[slot(i), :]
+        raw_ref[slot(i), pl.ds(0, qw)] = nn(rows_in, wq[0])
+        raw_ref[slot(i), pl.ds(qw, kw)] = nn(rows_in, wk[0])
+        raw_ref[slot(i), pl.ds(qw + kw, kw)] = nn(rows_in, wv[0])
+
+    def turn(values, gain, at_rows):
+        inverse = lax.rsqrt(jnp.mean(values * values, axis=1, keepdims=True) + EPS)
+        scaled = values * inverse * gain
+        return scaled * cos_ref[at_rows, :] + pltpu.roll(scaled, 64, axis=1) * sin_ref[at_rows, :]
+
+    tops[1].wait_recv()
+    tops[2].start()
+    normed[1].wait_recv()
+    normed[2].start()
+    tops[0].wait_recv()
+    kv_copy.wait_recv()
+
+    @pl.loop(0, tokens // ROWS)
+    def _(i):
+        at_rows = tile(i, ROWS)
+        for n in range(kv_heads):
+            cols = pl.ds(qw + n * hd, hd)
+            key = raw_ref[at_rows, cols] + kv_came[at_rows, pl.ds(n * hd, hd)].astype(F32)
+            raw_ref[at_rows, cols] = key
+            k_ref[at_rows, pl.ds(n * hd, hd)] = turn(key, k_gain_ref[...], at_rows).astype(BF16)
+            cols = pl.ds(qw + kw + n * hd, hd)
+            value = raw_ref[at_rows, cols] + kv_came[at_rows, pl.ds(kw + n * hd, hd)].astype(F32)
+            raw_ref[at_rows, cols] = value
+            v_ref[at_rows, pl.ds(n * hd, hd)] = value.astype(BF16)
+
+    q_copy.wait_recv()
+    early_start(1)
+
+    @pl.loop(0, tokens // ROWS)
+    def _(i):
+        at_rows = tile(i, ROWS)
+        other = q_came[at_rows, pl.ds(qw, 128)].astype(F32)
+        logit = gates[at_rows, :] + pltpu.roll(other, 128 - heads, axis=1)
+        sig_ref[at_rows, :] = sigmoid(logit)
+        for n in range(heads):
+            cols = pl.ds(n * hd, hd)
+            query = raw_ref[at_rows, cols] + q_came[at_rows, cols].astype(F32)
+            raw_ref[at_rows, cols] = query
+            q_ref[at_rows, cols] = turn(query, q_gain_ref[...], at_rows).astype(BF16)
+
+    def head_copy(n):
+        cols = pl.ds(n * hd, hd)
+        return copy_to(
+            gated_ref.at[0, :, cols], gated_ref.at[1, :, cols], g_send.at[n], g_recv.at[n],
+            place.x_peer,
+        )
+
+    for n in range(heads):
+        cols = pl.ds(n * hd, hd)
+        kv = pl.ds(n * kv_heads // heads * hd, hd)
+
+        @pl.loop(0, tokens // ROWS)
+        def _(i):
+            at_rows = tile(i, ROWS)
+            scores = nt(q_ref[at_rows, cols], k_ref[:, kv]) * scale
+            key_at = key_at_ref[:1, :]
+            allowed = (key_at <= at_ref[at_rows, :1]) & (key_at >= start_ref[at_rows, :1])
+            scores = jnp.where(allowed, scores, NEGATIVE)
+            top = jnp.max(scores, axis=1, keepdims=True)
+            raised = jnp.exp(scores - top)
+            total = jnp.sum(raised, axis=1, keepdims=True)
+            result = nn((raised / total).astype(BF16), v_ref[:, kv])
+            log_ref[n, at_rows, :] = column(top + jnp.log(total))
+            attended_ref[at_rows, cols] = result
+            gated_ref[0, at_rows, cols] = (result * sig_ref[at_rows, n : n + 1]).astype(BF16)
+
+        head_copy(n).start()
+        if n == 0:
+            tops[2].wait_recv()
+            early_start(2)
+        if n == 2:
+            early_start(3)
+
+    for i in (1, 0):
+        acc[slot(i), :] = nn(gated_ref[0, slot(i), :], wo[0])
+    for n in range(heads):
+        head_copy(n).wait_recv()
+    fold = copy_to(fold_src, fold_dst, s_send.at[2], s_recv.at[2], place.core_peer)
+    fold_src[...] = (acc[slot(1), :] + nn(gated_ref[1, slot(1), :], wo[1])).astype(BF16)
+    fold.start()
+    acc[slot(0), :] += nn(gated_ref[1, slot(0), :], wo[1])
+    fold.wait_recv()
+    resid = tok_ref[...].astype(F32) + acc[slot(0), :] + fold_dst[...].astype(F32)
+    resid_ref[...] = resid
+    ss_send[1] = column(jnp.sum(resid * resid, axis=1, keepdims=True))
+    squares(1).start()
+    for i in range(4):
+        early(i).wait_recv()
+        early_ref[slot(i), :] = (
+            early_send[slot(i), :].astype(F32) + early_came[slot(i), :].astype(F32)
+        ).astype(BF16)
+    squares(1).wait()
+    inv_two = lax.rsqrt((ss_send[1] + ss_came[1]) / (2 * width) + EPS)
+    inv_two_ref[...] = inv_two
+    h_ref[...] = (resid_ref[...] * inv_two[:, :1] * second_ref[...]).astype(BF16)
+
+    normed[2].wait_recv()
+    for copy in (*tops, *normed, kv_copy, q_copy, fold):
+        copy.wait_send()
+    for i in range(4):
+        early(i).wait_send()
+    for n in range(heads):
+        head_copy(n).wait_send()
+
+
+def front(
+    tok, top, norm_gain, ffn_gain, q_gain, k_gain, cos, sin, at, start, key_at, w_gates,
+    wq, wk, wv, wo, wd,
+):
+    count = lax.axis_size("group")
+    rows, width = tok.shape
+    tokens = 2 * rows
+    hd = 128
+    heads, kv_heads = wq.shape[1] // 2 // hd, wk.shape[1] // 2 // hd
+    qw, kw = heads * hd, kv_heads * hd
+    early = EARLY * WIDE
+    local = pl.BlockSpec(memory_space=pltpu.VMEM)
+    anywhere = pl.BlockSpec(memory_space=pl.ANY)
+    dma = pltpu.SemaphoreType.DMA
+    struct = jax.ShapeDtypeStruct
+    return pl.pallas_call(
+        functools.partial(front_kernel, count, heads, kv_heads),
+        out_shape=(
+            struct((rows, width), BF16),
+            struct((rows, width), F32),
+            struct((rows, 128), F32),
+            struct((rows, width), F32),
+            struct((rows, 128), F32),
+            struct((4 * rows, width), BF16),
+            struct((4 * rows, width), BF16),
+            struct((4 * rows, early), BF16),
+            struct((tokens, qw + 2 * kw), F32),
+            struct((tokens, 128), F32),
+            struct((tokens, qw), BF16),
+            struct((tokens, kw), BF16),
+            struct((tokens, kw), BF16),
+            struct((heads, tokens, 128), F32),
+            struct((tokens, qw), F32),
+            struct((2, tokens, qw), BF16),
+        ),
+        in_specs=[local] * 12 + [anywhere] * 5,
+        out_specs=(local,) * 16,
+        scratch_shapes=[
+            pltpu.VMEM((2, width, qw), BF16),
+            pltpu.VMEM((2, width, kw), BF16),
+            pltpu.VMEM((2, width, kw), BF16),
+            pltpu.VMEM((2, qw, width), BF16),
+            pltpu.VMEM((early, width), BF16),
+            pltpu.VMEM((tokens, 2 * kw), BF16),
+            pltpu.VMEM((tokens, 2 * kw), BF16),
+            pltpu.VMEM((tokens, qw + 128), BF16),
+            pltpu.VMEM((tokens, qw + 128), BF16),
+            pltpu.VMEM((tokens, 128), F32),
+            pltpu.VMEM((4 * rows, early), BF16),
+            pltpu.VMEM((4 * rows, early), BF16),
+            pltpu.VMEM((2, rows, 128), F32),
+            pltpu.VMEM((2, rows, 128), F32),
+            pltpu.VMEM((rows, width), BF16),
+            pltpu.VMEM((rows, width), BF16),
+            pltpu.VMEM((tokens, width), F32),
+            dma((2, 5)), dma((3,)), dma((3,)), dma((3,)), dma((3,)), dma((2,)), dma((2,)),
+            dma((4,)), dma((4,)), dma((heads,)), dma((heads,)), dma((3,)), dma((3,)),
+        ],
+        compiler_params=pltpu.CompilerParams(
+            collective_id=3, has_side_effects=True, vmem_limit_bytes=60 << 20
+        ),
+        cost_estimate=pl.CostEstimate(
+            flops=6 * tokens * width * (qw + kw) * 4, bytes_accessed=40 << 20,
+            transcendentals=heads * tokens * tokens,
+        ),
+    )(
+        tok, top, norm_gain, ffn_gain, q_gain, k_gain, cos, sin, at, start, key_at, w_gates,
+        wq, wk, wv, wo, wd,
+    )
 
 
 MISC = 88
@@ -734,7 +1100,6 @@
     kv_heads = kv_half // head_dim
     share = heads // kv_heads
     main = q_half + 2 * kv_half
-    half_hidden = w_gate.shape[1] // 2
     scale = head_dim ** (-0.5)
     row_at = lax.axis_index("row")
     col_at = lax.axis_index("col")
@@ -743,55 +1108,38 @@
     steps = jnp.arange(rows, dtype=jnp.int32)
     index = jnp.concatenate([col_at * rows + steps, (1 - col_at) * rows + steps])
     segment, place = places(lengths, index)
-
-    grad_group = jnp.concatenate([grad_out, swap(grad_out, "col")])
-    grad_all = jnp.concatenate([grad_group, swap_groups(grad_group)])
-    down_half = lax.dynamic_slice_in_dim(w_down, side * half_hidden, half_hidden, axis=0)
-    inner_part = nt(grad_all, down_half)
-    inner_grad = (inner_part + swap(inner_part.astype(BF16), "row").astype(F32)).astype(BF16)
-    x_in = tokens.astype(F32)
-    squares = jnp.sum(x_in * x_in, axis=1)
-    inverse_one = lax.rsqrt((squares + swap(squares, "row")) / width + EPS)
-    normed_one = (x_in * inverse_one[:, None] * norm_gain).astype(BF16)
-    permuted = jnp.concatenate([normed_one, swap(normed_one, "col")])
-    splits = [halves(w, 1, row_at) for w in (w_query, w_key, w_value, w_head_gate)]
-    w_main = jnp.concatenate(
-        [own for own, _ in splits[:3]] + [other for _, other in splits[:3]], axis=1
-    )
-    w_gates = jnp.pad(jnp.concatenate(splits[3], axis=1), ((0, 0), (0, 128 - 2 * gate_half)))
-    partial = nn(permuted, w_main)
-    partial_gates = nn(permuted, w_gates)
-    away = jnp.concatenate(
-        [partial[:, main:], partial_gates[:, gate_half : 2 * gate_half]], axis=1
-    ).astype(BF16)
-    stay = jnp.concatenate([partial[:, :main], partial_gates[:, :gate_half]], axis=1)
-    turned = jnp.concatenate([permuted, swap_groups(permuted)]).T
-    projected = stay + swap(away, "row").astype(F32)
-    raw_query = projected[:, :q_half].reshape(group_tok, heads, head_dim)
-    raw_key = projected[:, q_half : q_half + kv_half].reshape(group_tok, kv_heads, head_dim)
-    raw_value = projected[:, q_half + kv_half : main].reshape(group_tok, kv_heads, head_dim)
-    logit = projected[:, main:]
+    cosines, sines = rope_tables(place, head_dim)
+    signed = jnp.concatenate([-sines[:, : head_dim // 2], sines[:, head_dim // 2 :]], axis=1)
+    cos_heads = cosines[:, None, :]
+    sin_heads = sines[:, None, :]
+    w_gates = jnp.pad(
+        jnp.concatenate(halves(w_head_gate, 1, row_at), axis=1),
+        ((0, 0), (0, 128 - 2 * gate_half)),
+    )
+    (
+        normed_two, resid, inverse_two, hat, inverse_one, permuted_pair, grad_all, early_grad,
+        raw, gate_sigmoid, query, keys, values, logsum, attended, gated_both,
+    ) = front(
+        tokens, grad_out, norm_gain[None], ffn_gain[None], query_gain[None], key_gain[None],
+        cosines, signed,
+        jnp.broadcast_to(index[:, None], (group_tok, 128)),
+        jnp.broadcast_to((index - place)[:, None], (group_tok, 128)),
+        jnp.broadcast_to(index[None], (8, group_tok)),
+        w_gates, w_query, w_key, w_value, w_out, w_down,
+    )
+    inverse_one, inverse_two = inverse_one[:, 0], inverse_two[:, 0]
+    gate_sigmoid = gate_sigmoid[:, :heads]
+    permuted = permuted_pair[:group_tok]
+    turned = permuted_pair.T
+    raw_query = raw[:, :q_half].reshape(group_tok, heads, head_dim)
+    raw_key = raw[:, q_half : q_half + kv_half].reshape(group_tok, kv_heads, head_dim)
     query_inverse = lax.rsqrt(jnp.mean(raw_query * raw_query, axis=-1, keepdims=True) + EPS)
     key_inverse = lax.rsqrt(jnp.mean(raw_key * raw_key, axis=-1, keepdims=True) + EPS)
-    cosines, sines = rope_tables(place, head_dim)
-    cos_heads = cosines[:, None, :]
-    sin_heads = sines[:, None, :]
-    query = rotate(raw_query * query_inverse * query_gain, cos_heads, sin_heads).astype(BF16)
-    keys = rotate(raw_key * key_inverse * key_gain, cos_heads, sin_heads).astype(BF16)
-    values = raw_value.astype(BF16)
     query = query.reshape(group_tok, kv_heads, share, head_dim)
-
-    scores = masked_scores(query, keys, segment, place, scale)
-    top = jnp.max(scores, axis=-1, keepdims=True)
-    raised = jnp.exp(scores - top)
-    probs = raised / jnp.sum(raised, axis=-1, keepdims=True)
-    probs_low = probs.astype(BF16)
-    attended = jnp.einsum("kgqs,skd->qkgd", probs_low, values, preferred_element_type=F32)
+    keys = keys.reshape(group_tok, kv_heads, head_dim)
+    values = values.reshape(group_tok, kv_heads, head_dim)
     attended = attended.reshape(group_tok, heads, head_dim)
-    gate_sigmoid = jax.nn.sigmoid(logit)
-    gated = (attended * gate_sigmoid[:, :, None]).reshape(group_tok, q_half).astype(BF16)
-    gated_came = swap(gated, "row")
-    gated_all = jnp.concatenate([gated, gated_came], axis=1)
+    gated, gated_came = gated_both[0], gated_both[1]
     first_side = side == 0
     gated_pair = jnp.concatenate(
         [
@@ -799,20 +1147,17 @@
             swap_groups(jnp.where(first_side, gated_came, gated)),
         ]
     ).T
+    splits = [halves(w, 1, row_at) for w in (w_query, w_key, w_value)]
+    w_main = jnp.concatenate([own for own, _ in splits] + [other for _, other in splits], axis=1)
     w_back = jnp.concatenate(halves(w_out, 0, row_at))
 
     def sum_cores(values):
         return values[:rows] + swap(values[rows:].astype(BF16), "col").astype(F32)
 
-    resid = x_in + sum_cores(nn(gated_all, w_back))
-    squares = jnp.sum(resid * resid, axis=1)
-    inverse_two = lax.rsqrt((squares + swap(squares, "row")) / width + EPS)
-    normed_two = (resid * inverse_two[:, None] * ffn_gain).astype(BF16)
-
-    pair_sum, down_sum, _, _, branch, d_normed_two = ffn(
-        normed_two, grad_all, inner_grad, w_gate, w_up, w_down
-    )
-    output = (resid + branch).astype(BF16)
+    pair_sum, down_sum, _, _, branch, branch_out, d_normed_two = ffn(
+        normed_two, grad_all, early_grad, w_gate, w_up, w_down
+    )
+    output = (resid + branch + swap_groups(branch_out).astype(F32)).astype(BF16)
 
     d_top = grad_out.astype(F32)
     ffn_gain_part = jnp.sum(d_normed_two * resid * inverse_two[:, None], axis=0)
@@ -837,6 +1182,9 @@
     d_logit = jnp.sum(d_gated * attended, axis=-1) * gate_sigmoid * (1.0 - gate_sigmoid)
     d_attended = d_attended.reshape(group_tok, kv_heads, share, head_dim)
 
+    scores = masked_scores(query, keys, segment, place, scale)
+    probs = jnp.exp(scores - logsum[:, :, 0].reshape(kv_heads, share, group_tok, 1))
+    probs_low = probs.astype(BF16)
     d_probs = jnp.einsum("qkgd,skd->kgqs", d_attended, values, preferred_element_type=F32)
     d_scores = (probs * (d_probs - jnp.sum(d_probs * probs, axis=-1, keepdims=True))).astype(BF16)
     d_query = jnp.einsum("kgqs,skd->qkgd", d_scores, keys, preferred_element_type=F32) * scale
@@ -872,7 +1220,6 @@
             jnp.zeros((6, 128), F32),
         ]
     )
-    hat = x_in * inverse_one[:, None]
     grads, d_normed_one, inner_one, sums = back(
         d_main, turned, w_main, jnp.pad(d_gates, ((0, 0), (0, 128 - 2 * gate_half))), w_gates,
         gated_pair, branch_pair, hat, norm_gain[None], misc,

time: 818 us -> 768 us (0.939)
  Pallas kernels: 476 us -> 568 us
  waiting for transfers between devices: 66.1 us -> 9.71 us
  local copies, waits for them, and re-layouts: 98.8 us -> 68.9 us
  matrix products: 44.5 us -> 17.1 us
  other arithmetic: 111 us -> 84.2 us
    pallas_call x0 -> x1, Pallas kernels: none -> 113 us  [front(): pl.pallas_call(functools.partial(front_kernel, count, heads, kv_heads), o...]
    ppermute x13 -> x5, waiting for transfers between devices: 56 us -> 3.11 us  [swap(): return lax.ppermute(values, axis, [(0, 1), (1, 0)])]
    pallas_call x1, Pallas kernels: 353 us -> 332 us  [ffn(): pl.pallas_call(functools.partial(ffn_kernel, count, chunks), out_shape=(j...]
    convert_element_type x5 -> x0, other arithmetic: 11.2 us -> none  [the longest x1 7.57 us: body(): (inner_part + swap(inner_part.astype(BF16), 'row').astype(F32)).astype(BF16)]
    dot_general x2 -> x1, matrix products: 12.6 us -> 1.56 us  [nt(): lax.dot_general(a, b, (((1,), (1,)), ((), ())), preferred_element_type=F32)]
    unnamed x197 -> x121, local copies, waits for them, and re-layouts: 20.2 us -> 9.73 us
    dot_general x4 -> x1, matrix products: 12.2 us -> 3.79 us  [masked_scores(): jnp.einsum('qkgd,skd->kgqs', query, keys, preferred_element_type=F32)]
  transfers between devices with their start and end apart: 17 -> 8, of which waited for: 6 -> 2; matrix products, arithmetic and copies ran while one was open for 23% -> 20% of each run, Pallas kernels for 44% -> 16%
where the time goes in v3:
time: 768 us; the launch traced here: 757 us
  Pallas kernels  568 us (74%)
  other arithmetic  84.2 us (11%)
  local copies, waits for them, and re-layouts  68.9 us (9%)
  matrix products  17.1 us (2%)
  waiting for transfers between devices  9.71 us (1%)
    pallas_call x1, Pallas kernels, ffn(): pl.pallas_call(functools.partial(ffn_kernel, count, chunks), out_shape=(j...  332 us
    pallas_call x1, Pallas kernels, back(): pl.pallas_call(functools.partial(back_kernel, count), out_shape=(jax.Shap...  124 us
    pallas_call x1, Pallas kernels, front(): pl.pallas_call(functools.partial(front_kernel, count, heads, kv_heads), o...  113 us
  transfers between devices with their start and end apart: 8, of which 2 were waited for; matrix products, arithmetic and copies ran while one was open for 20% of the time, Pallas kernels for 16%

profile of v3, /device:TPU:24, one launch (start us, length us, event | category | flops | bytes accessed | tf_op | source)
XLA Modules:
  0.0 756.5 jit_solution(18232154979932677295)
XLA Ops:
  9.8 112.6 %shard_map.254 = (bf16[320,1024]{1,0:T(8,128)(2,1)}, f32[320,1024]{1,0:T(8,128)}, f32[320,128]{1,0:T(8,128)}, f32[320,1024]{1,0:T(8,128)}, f32[320,128]{1,0:T(8,...) custom-call(bf16[320,1024]{1,0:T(8,128)(2,1)} %tok_ref.1, ...), custom_call_target="tpu_custom_call" | custom-call | flops 12079595520 | bytes 41943040 | tf_op jit(solution)/shard_map/pallas_call | solution.py:820
  123.6 331.5 %shard_map.255 = (bf16[2,1024,3072]{2,1,0:T(8,128)(2,1)}, bf16[3072,1024]{1,0:T(8,128)(2,1)}, bf16[2,12,2,1024,128]{4,3,2,1,0:T(8,128)(2,1)}, bf16[2,12,128,1024...) custom-call(bf16[320,1024]{1,0:T(8,128)(2,1)} %get-tuple-element.40.h_ref, ...), custom_call_target="tpu_custom_call" | custom-call | flops 32212254720 | bytes 209715200 | tf_op jit(solution)/shard_map/pallas_call | solution.py:538
  462.0 2.5 collective-permute-start.5
  473.4 13.9 %bitcast_convert_fusion = (f32[1024,3072]{1,0:T(8,128)}, f32[1024,3072]{1,0:T(8,128)}) fusion(bf16[2,1024,3072]{2,1,0:T(8,128)(2,1)} %get-tuple-element.62), kind=kLoop, calls=%fused_computation.8 | loop fusion | flops 6291456 | bytes 37748736 | tf_op jit(solution)/shard_map/convert_element_type | solution.py:1263
  498.4 4.6 copy.282
  503.0 9.3 %convert_element_type.90 = f32[3072,1024]{1,0:T(8,128)} convert(bf16[3072,1024]{1,0:T(8,128)(2,1)} %get-tuple-element.63) | non-fusion elementwise | flops 3145728 | bytes 18874368 | tf_op jit(solution)/shard_map/convert_element_type | solution.py:1264
  518.8 3.8 fusion.44
  525.0 6.6 collective-permute-done.6
  531.6 3.1 collective-permute-done.3
  539.8 2.9 copy.305
  542.7 6.0 fusion.24
  548.8 2.4 fusion
  557.8 5.6 multiply_reduce_fusion.2
  578.1 5.0 pad_maximum_fusion.branch_ref
  585.2 2.4 concatenate.90.misc_ref
  587.6 123.5 %shard_map.256 = (bf16[24,512,256]{2,1,0:T(8,128)(2,1)}, f32[320,1024]{1,0:T(8,128)}, f32[320,128]{1,0:T(8,128)}, f32[88,128]{1,0:T(8,128)}) custom-call(bf16[640,1024]{1,0:T(8,128)(2,1)} %pad_maximum_fusion.2.own_ref, bf16[1024,1280]{1,0:T(8,128)(2,1)} %bitcast.157, bf16[1024,2048]{1,0:T(8,128)(2,1)} %select_dynamic-update-slice_fusion.2.w_main_ref, ...), custom_call_target="tpu_custom_call" | custom-call | flops 8053063680 | bytes 104857600 | tf_op jit(solution)/shard_map/pallas_call | solution.py:1045
  712.9 2.5 slice.144
  715.4 5.3 copy.286
  720.6 7.7 %reshape.261 = bf16[1024,2048]{1,0:T(8,128)(2,1)} reshape(bf16[2,512,2,4,256]{4,3,2,1,0:T(4,128)(2,1)} %copy.286) | data formatting | bytes 8388608 | tf_op jit(solution)/shard_map/reshape | solution.py:1241
  728.4 3.1 broadcast_select_fusion.7
  736.2 2.6 maximum_convert_fusion.1
  738.8 5.4 copy.289
  749.0 2.7 maximum_convert_fusion
  753.3 3.1 multiply_add_fusion
  (236 shorter events, 86.7 us)
Async XLA Ops:
  123.5 331.6 %copy-start.54 = (f32[1024]{0:T(1024)S(1)}, f32[1024]{0:T(1024)}, u32[]{:S(2)}) copy-start(f32[1024]{0:T(1024)} %param.25) | copy-start | bytes 12292
  457.2 55.1 %collective-permute-start.1 = (f32[320]{0:T(512)S(1)}, f32[320]{0:T(512)S(1)}, u32[]{:S(2)}, u32[]{:S(2)}) collective-permute-start(f32[320]{0:T(512)S(1)} %get-tuple-element.149), channel_id=1, source_target_pairs={{0,2},{2,0},{1,3},{3,1},{4,6},{6,4},{5,7},{7,5},{8,10},{10,8},{9,1... | collective-permute-start | bytes 3848 | tf_op jit(solution)/shard_map/ppermute | solution.py:19
  462.0 60.7 %collective-permute-start.5 = (bf16[640,512]{0,1:T(8,128)(2,1)}, bf16[640,512]{0,1:T(8,128)(2,1)}, u32[]{:S(2)}, u32[]{:S(2)}) collective-permute-start(bf16[640,512]{0,1:T(8,128)(2,1)} %get-tuple-element.179), channel_id=1, source_target_pairs={{0,4},{4,0},{8,12},{12,8},{16,20},{20,16},{24,28},{28,24},{1,5},{5... | collective-permute-start | bytes 1966088 | tf_op jit(solution)/shard_map/ppermute | solution.py:24
  464.4 288.4 %collective-permute-start = (bf16[320,1024]{1,0:T(8,128)(2,1)}, bf16[320,1024]{1,0:T(8,128)(2,1)}, u32[]{:S(2)}, u32[]{:S(2)}) collective-permute-start(bf16[320,1024]{1,0:T(8,128)(2,1)} %get-tuple-element.44), channel_id=1, source_target_pairs={{0,4},{4,0},{8,12},{12,8},{16,20},{20,16},{24,28},{28,24},{1,5},{5... | collective-permute-start | bytes 1966088 | tf_op jit(solution)/shard_map/ppermute | solution.py:24
  473.4 14.3 %copy-start.40 = (f32[4,640,128]{2,1,0:T(8,128)S(1)}, f32[4,640,128]{2,1,0:T(8,128)}, u32[]{:S(2)}) copy-start(f32[4,640,128]{2,1,0:T(8,128)} %get-tuple-element.51) | copy-start | bytes 3932164
  473.4 14.7 %copy-start.22 = (f32[640,1024]{1,0:T(8,128)S(1)}, f32[640,1024]{1,0:T(8,128)}, u32[]{:S(2)}) copy-start(f32[640,1024]{1,0:T(8,128)} %get-tuple-element.48) | copy-start | bytes 7864324
  491.0 27.8 %copy-start.11 = (bf16[640,512]{0,1:T(8,128)(2,1)}, bf16[640,512]{0,1:T(8,128)(2,1)S(1)}, u32[]{:S(2)}) copy-start(bf16[640,512]{0,1:T(8,128)(2,1)S(1)} %copy.309) | copy-start | bytes 1966084
  503.0 9.3 %copy-start.3 = (f32[320,1024]{1,0:T(8,128)S(1)}, f32[320,1024]{1,0:T(8,128)}, u32[]{:S(2)}) copy-start(f32[320,1024]{1,0:T(8,128)} %get-tuple-element.39) | copy-start | bytes 3932164
  503.0 9.3 %copy-start.5 = (f32[320,1024]{1,0:T(8,128)S(1)}, f32[320,1024]{1,0:T(8,128)}, u32[]{:S(2)}) copy-start(f32[320,1024]{1,0:T(8,128)} %get-tuple-element.46) | copy-start | bytes 3932164
  503.0 9.3 %copy-start.26 = (bf16[320,1024]{1,0:T(8,128)(2,1)S(1)}, bf16[320,1024]{1,0:T(8,128)(2,1)}, u32[]{:S(2)}) copy-start(bf16[320,1024]{1,0:T(8,128)(2,1)} %top_ref.1) | copy-start | bytes 1966084
  512.7 4.0 collective-permute-start.2
  514.7 16.9 %collective-permute-start.6 = (bf16[320,1024]{1,0:T(8,128)(2,1)S(1)}, bf16[320,1024]{1,0:T(8,128)(2,1)}, u32[]{:S(2)}, u32[]{:S(2)}) collective-permute-start(bf16[320,1024]{1,0:T(8,128)(2,1)S(1)} %fusion.38), channel_id=1, source_target_pairs={{0,4},{4,0},{8,12},{12,8},{16,20},{20,16},{24,28},{28,24},{1,5},{5... | collective-permute-start | bytes 1966088 | tf_op jit(solution)/shard_map/ppermute | solution.py:24
  518.4 16.3 %collective-permute-start.3 = (bf16[640,512]{1,0:T(8,128)(2,1)S(1)}, bf16[640,512]{1,0:T(8,128)(2,1)S(1)}, u32[]{:S(2)}, u32[]{:S(2)}) collective-permute-start(bf16[640,512]{1,0:T(8,128)(2,1)S(1)} %slice.192), channel_id=1, source_target_pairs={{0,2},{2,0},{1,3},{3,1},{4,6},{6,4},{5,7},{7,5},{8,10},{10,8},{9,1... | collective-permute-start | bytes 1966088 | tf_op jit(solution)/shard_map/ppermute | solution.py:19
  522.6 12.1 %copy-start.45 = (f32[640,512]{1,0:T(8,128)S(1)}, f32[640,512]{1,0:T(8,128)}, u32[]{:S(2)}) copy-start(f32[640,512]{1,0:T(8,128)} %get-tuple-element.55) | copy-start | bytes 3932164
  531.6 46.0 %collective-permute-start.7 = (bf16[320,1024]{1,0:T(8,128)(2,1)}, bf16[320,1024]{1,0:T(8,128)(2,1)}, u32[]{:S(2)}, u32[]{:S(2)}) collective-permute-start(bf16[320,1024]{1,0:T(8,128)(2,1)} %collective-permute-done.6), channel_id=1, source_target_pairs={{0,1},{1,0},{2,3},{3,2},{4,5},{5,4},{6,7},{7,6},{8,9},{9,8},{10,11... | collective-permute-start | bytes 1966088 | tf_op jit(solution)/shard_map/ppermute | solution.py:19
  539.1 44.0 %collective-permute-start.4 = (bf16[640,4]{1,0:T(8,128)(2,1)S(1)}, bf16[640,4]{1,0:T(8,128)(2,1)}, u32[]{:S(2)}, u32[]{:S(2)}) collective-permute-start(bf16[640,4]{1,0:T(8,128)(2,1)S(1)} %get-tuple-element.184), channel_id=1, source_target_pairs={{0,2},{2,0},{1,3},{3,1},{4,6},{6,4},{5,7},{7,5},{8,10},{10,8},{9,1... | collective-permute-start | bytes 15368 | tf_op jit(solution)/shard_map/ppermute | solution.py:19
  539.7 9.0 %slice-start = ((s8[6553600]{0:T(1024)(128)(4,1)}), s8[2359296]{0:T(1024)(128)(4,1)S(1)}, s32[]{:S(2)}) async-start(s8[6553600]{0:T(1024)(128)(4,1)} %bitcast.139), calls=%async_computation | async-start | bytes 4718592
  542.7 6.1 copy-start.14
  542.7 6.1 copy-start.47
  557.8 8.5 %copy-start.1 = (bf16[2,2,640,640]{2,3,1,0:T(8,128)(2,1)S(1)}, bf16[2,2,640,640]{2,3,1,0:T(8,128)(2,1)}, u32[]{:S(2)}) copy-start(bf16[2,2,640,640]{2,3,1,0:T(8,128)(2,1)} %copy-done) | copy-start | bytes 9830404
  577.6 6.5 copy-start.12
  738.8 6.3 copy-start.34
  738.8 6.3 copy-start.35
  746.7 6.2 copy-start.38
  (44 other events, 125.9 us)

commit v4 on v3

--- a/solution.py
+++ b/solution.py
@@ -13,10 +13,6 @@
 MESH = pl.DeviceIdType.MESH
 F32 = jnp.float32
 BF16 = jnp.bfloat16
-
-
-def swap(values, axis):
-    return lax.ppermute(values, axis, [(0, 1), (1, 0)])
 
 
 def swap_groups(values):
@@ -52,27 +48,6 @@
     cosines = jnp.concatenate([jnp.cos(angle), jnp.cos(angle)], axis=1)
     sines = jnp.concatenate([jnp.sin(angle), jnp.sin(angle)], axis=1)
     return (cosines, sines)
-
-
-def rotate(values, cosines, sines):
-    half = values.shape[-1] // 2
-    turned = jnp.concatenate([-values[..., half:], values[..., :half]], axis=-1)
-    return values * cosines + turned * sines
-
-
-def unrotate(grads, cosines, sines):
-    half = grads.shape[-1] // 2
-    scaled = grads * sines
-    return grads * cosines + jnp.concatenate([scaled[..., half:], -scaled[..., :half]], axis=-1)
-
-
-def head_norm_back(d_normed, raw_values, inverse, gain):
-    scaled = d_normed * gain
-    gain_part = jnp.sum(d_normed * raw_values * inverse, axis=(0, 1))
-    d_raw = inverse * scaled - raw_values * inverse**3 * jnp.mean(
-        scaled * raw_values, axis=-1, keepdims=True
-    )
-    return (d_raw, gain_part)
 
 
 TILE = 256
@@ -876,44 +851,187 @@
 MISC = 88
 
 
-def back_kernel(
-    count, own_ref, turned_ref, w_main_ref, gates_ref, w_gates_ref, gated_ref, branch_ref,
-    hat_ref, scale_ref, misc_ref,
-    grads_ref, back_ref, inner_ref, sums_ref,
-    came, across, total, landed, misc, misc_came, misc_landed, misc_home, acc, fold_src, fold_dst,
-    inner_src, inner_dst,
-    x_send, x_recv, y_send, y_recv, small_send, small_recv, *chain_sems,
+def tn(a, b):
+    return lax.dot_general(a, b, (((0,), (0,)), ((), ())), preferred_element_type=F32)
+
+
+def rear_kernel(
+    count, heads, kv_heads, back_ref, resid_ref, inv_two_ref, second_ref, top_ref, raw_ref,
+    sig_ref, q_ref, k_ref, v_ref, log_ref, attended_ref, cos_ref, sin_ref, at_ref, start_ref,
+    key_at_ref, q_gain_ref, k_gain_ref, turned_ref, gated_ref, w_gates_ref, hat_ref, inv_one_ref,
+    norm_ref, wq_ref, wk_ref, wv_ref, wo_ref,
+    grads_ref, input_ref, sums_ref,
+    w_main, wo, branch, dg_own, dg_send, dg_came, dk, dv, gates, gates_came, own, came, across,
+    total, landed, misc, misc_came, misc_landed, misc_home, acc, fold_src, fold_dst, in_send,
+    in_came,
+    w_sem, b_send, b_recv, d_send, d_recv, x_send, x_recv, y_send, y_recv, s_send, s_recv,
+    *chain_sems,
 ):
     place = Place(count)
+    row_at = lax.axis_index("row")
     side = place.side
-    tokens, main = own_ref.shape
-    rows = tokens // 2
-    cols = 256
-    parts = main // cols
-    width = turned_ref.shape[0]
+    rows, width = back_ref.shape
+    tokens = 2 * rows
+    hd = 128
+    cols = 2 * hd
+    qw = heads * hd
+    parts = heads // 2 + kv_heads
     high = gated_ref.shape[0]
     pieces = total.shape[0]
+    scale = hd**-0.5
+
+    loads = []
+    for i, at in enumerate((row_at, 1 - row_at)):
+        for n in range(kv_heads):
+            q_cols, k_cols = tile(at * kv_heads + n, cols), tile(at * kv_heads + n, hd)
+            first, second = w_main.at[i * parts + 2 * n], w_main.at[i * parts + 2 * n + 1]
+            loads += [
+                pltpu.make_async_copy(wq_ref.at[:, q_cols], first, w_sem.at[i, n, 0]),
+                pltpu.make_async_copy(
+                    wk_ref.at[:, k_cols], second.at[:, pl.ds(0, hd)], w_sem.at[i, n, 1]
+                ),
+                pltpu.make_async_copy(
+                    wv_ref.at[:, k_cols], second.at[:, pl.ds(hd, hd)], w_sem.at[i, n, 2]
+                ),
+            ]
+        loads.append(pltpu.make_async_copy(wo_ref.at[tile(at, qw), :], wo.at[i], w_sem.at[i, 0, 3]))
+    for copy in loads:
+        copy.start()
     place.meet()
 
-    def cut(j):
-        return pl.ds(j * cols, cols) if isinstance(j, int) else tile(j, cols)
+    def slot(i):
+        return pl.ds(i * rows, rows)
+
+    def inner_copy(n):
+        return copy_to(in_send.at[n], in_came.at[n], s_send.at[n], s_recv.at[n], place.x_peer)
+
+    def store_row(at, values):
+        for i in range(width // 128):
+            misc[at + i : at + i + 1, :] = values[:, i * 128 : (i + 1) * 128]
+
+    misc[...] = jnp.zeros_like(misc)
+    grad = back_ref[...]
+    in_send[0] = column(jnp.sum(grad * second_ref[...] * resid_ref[...], axis=1, keepdims=True))
+    inner_copy(0).start()
+    inv_two = inv_two_ref[:, :1]
+    store_row(8, jnp.sum(back_ref[...] * resid_ref[...] * inv_two, axis=0, keepdims=True))
+    inner_copy(0).wait()
+    inner = (in_send[0, :, :1] + in_came[0, :, :1]) * inv_two * inv_two * inv_two / (2 * width)
+    d_resid = (
+        top_ref[...].astype(F32)
+        + inv_two * (back_ref[...] * second_ref[...])
+        - resid_ref[...] * inner
+    )
+    input_ref[...] = d_resid
+    branch[slot(0), :] = d_resid.astype(BF16)
+    to_core = copy_to(
+        branch.at[slot(0), :], branch.at[slot(1), :], b_send.at[0], b_recv.at[0], place.core_peer
+    )
+    to_pair = copy_to(
+        branch.at[slot(0), :], branch.at[slot(2), :], b_send.at[1], b_recv.at[1], place.y_peer
+    )
+    forward = copy_to(
+        branch.at[slot(2), :], branch.at[slot(3), :], b_send.at[2], b_recv.at[2],
+        place.core_peer,
+    )
+    to_core.start()
+    to_pair.start()
+
+    def dg_copy(n):
+        at_cols = pl.ds(n * cols, cols)
+        return copy_to(
+            dg_send.at[:, at_cols], dg_came.at[:, at_cols], d_send.at[n], d_recv.at[n],
+            place.x_peer,
+        )
+
+    for copy in loads:
+        copy.wait()
+    halves_of = heads // 2
+    dg_send[slot(0), :] = nt(branch[slot(0), :], wo[1]).astype(BF16)
+    to_core.wait_recv()
+    dg_send[slot(1), :] = nt(branch[slot(1), :], wo[1]).astype(BF16)
+    for n in range(halves_of):
+        dg_copy(n).start()
+    for i in range(2):
+        dg_own[slot(i), :] = nt(branch[slot(i), :], wo[0])
+    dk[...] = jnp.zeros_like(dk)
+    dv[...] = jnp.zeros_like(dv)
+    gates[...] = jnp.zeros_like(gates)
+
+    def unturn(values, at_rows):
+        return values * cos_ref[at_rows, :] - pltpu.roll(values, 64, axis=1) * sin_ref[at_rows, :]
+
+    def norm_back(values, raw, gain, at_rows, into):
+        normed = unturn(values, at_rows)
+        inverse = lax.rsqrt(jnp.mean(raw * raw, axis=1, keepdims=True) + EPS)
+        misc[into : into + 1, :] += jnp.sum(normed * raw * inverse, axis=0, keepdims=True)
+        scaled = normed * gain
+        inner = jnp.mean(scaled * raw, axis=1, keepdims=True)
+        return inverse * scaled - raw * (inverse * inverse * inverse * inner)
+
+    lane = lax.broadcasted_iota(jnp.int32, (ROWS, 128), 1)
+
+    def head(n):
+        at_cols = pl.ds(n * hd, hd)
+        kv = n * kv_heads // heads
+        kv_cols = pl.ds(kv * hd, hd)
+
+        @pl.loop(0, tokens // ROWS)
+        def _(i):
+            at_rows = tile(i, ROWS)
+            query = q_ref[at_rows, at_cols]
+            d_gated = dg_own[at_rows, at_cols] + dg_came[at_rows, at_cols].astype(F32)
+            sig = sig_ref[at_rows, n : n + 1]
+            d_att = (d_gated * sig).astype(BF16)
+            d_logit = jnp.sum(d_gated * attended_ref[at_rows, at_cols], axis=1, keepdims=True)
+            d_logit = d_logit * sig * (1.0 - sig)
+            gates[at_rows, :] = jnp.where(lane == n, d_logit.astype(BF16), gates[at_rows, :])
+            scores = nt(query, k_ref[:, kv_cols]) * scale
+            key_at = key_at_ref[:1, :]
+            allowed = (key_at <= at_ref[at_rows, :1]) & (key_at >= start_ref[at_rows, :1])
+            probs = jnp.exp(jnp.where(allowed, scores, NEGATIVE) - log_ref[n, at_rows, :1])
+            d_probs = nt(d_att, v_ref[:, kv_cols])
+            mean = jnp.sum(d_probs * probs, axis=1, keepdims=True)
+            d_scores = (probs * (d_probs - mean)).astype(BF16)
+            dv[:, kv_cols] += tn(probs.astype(BF16), d_att)
+            dk[:, kv_cols] += tn(d_scores, query)
+            d_query = nn(d_scores, k_ref[:, kv_cols]) * scale
+            own[2 * (n // 2), at_rows, pl.ds(n % 2 * hd, hd)] = norm_back(
+                d_query, raw_ref[at_rows, at_cols], q_gain_ref[...], at_rows, 80
+            ).astype(BF16)
+
+    def key_value(n):
+        kv_cols = pl.ds(n * hd, hd)
+
+        @pl.loop(0, tokens // ROWS)
+        def _(i):
+            at_rows = tile(i, ROWS)
+            raw = raw_ref[at_rows, pl.ds(qw + n * hd, hd)]
+            own[2 * n + 1, at_rows, pl.ds(0, hd)] = norm_back(
+                dk[at_rows, kv_cols] * scale, raw, k_gain_ref[...], at_rows, 81
+            ).astype(BF16)
+            own[2 * n + 1, at_rows, pl.ds(hd, hd)] = dv[at_rows, kv_cols].astype(BF16)
 
     def over_x(j):
-        return copy_to(
-            own_ref.at[:, cut(j)], came.at[j], x_send.at[j], x_recv.at[j], place.x_peer
-        )
+        return copy_to(own.at[j], came.at[j], x_send.at[j], x_recv.at[j], place.x_peer)
 
     def over_y(j, mine):
-        src = own_ref.at[:, cut(j)] if mine else came.at[j]
+        src = own.at[j] if mine else came.at[j]
         return copy_to(src, across.at[j], y_send.at[j], y_recv.at[j], place.y_peer)
 
-    for j in range(parts):
+    def send_chunk(j):
         over_x(j).start()
 
-    @pl.when(side == 1)
-    def _():
-        for j in range(parts):
+        @pl.when(side == 1)
+        def _():
             over_y(j, True).start()
+
+    def take_chunk(j):
+        over_x(j).wait_recv()
+
+        @pl.when(side == 0)
+        def _():
+            over_y(j, False).start()
 
     def add(c, k, which):
         total[c] = (total[c].astype(F32) + landed[which, c].astype(F32)).astype(BF16)
@@ -937,122 +1055,159 @@
         add_misc, chain_sems[9:], share=False,
     )
 
-    misc[...] = misc_ref[...]
-    acc[...] = nt(gates_ref[...], w_gates_ref[...])
-
-    @pl.loop(0, parts)
-    def _(t):
-        total[t] = nn(gated_ref[...], branch_ref[:, cut(t)]).astype(BF16)
+    outs = pieces - 2 * parts
+
+    def out_piece(t):
+        at_cols = pl.ds(t * cols, cols)
+        total[t] = nn(gated_ref[...], branch[:, at_cols]).astype(BF16)
         chain.step(t)
-        over_x(t).wait_recv()
-
-        @pl.when(side == 0)
-        def _():
-            over_y(t, False).start()
-
-        acc[...] += nt(own_ref[:, cut(t)], w_main_ref[:, cut(t)])
-        acc[...] += nt(came[t], w_main_ref[:, cut(parts + t)])
-
-    fold = copy_to(fold_src, fold_dst, small_send.at[0], small_recv.at[0], place.core_peer)
+
+    def block(j):
+        over_y(j, True).wait_recv()
+        first = jnp.where(side == 0, own[j], came[j])
+        for i in range(2):
+            at_rows = pl.ds(i * high, high)
+            total[outs + 2 * j + i] = (
+                nn(turned_ref[at_rows, pl.ds(0, tokens)], first)
+                + nn(turned_ref[at_rows, pl.ds(tokens, tokens)], across[j])
+            ).astype(BF16)
+            chain.step(outs + 2 * j + i)
+
+    for n in range(kv_heads):
+        dg_copy(n).wait_recv()
+        head(2 * n)
+        if n == 0:
+            to_pair.wait_recv()
+            forward.start()
+        else:
+            take_chunk(2 * n - 2)
+        head(2 * n + 1)
+        key_value(n)
+        send_chunk(2 * n)
+        send_chunk(2 * n + 1)
+        if n == 0:
+            forward.wait_recv()
+            for t in range(outs):
+                out_piece(t)
+        else:
+            take_chunk(2 * n - 1)
+            block(2 * n - 2)
+            block(2 * n - 1)
+
+    def gates_copy():
+        return copy_to(gates, gates_came, s_send.at[2], s_recv.at[2], place.x_peer)
+
+    gates_copy().start()
+    last = 2 * (kv_heads - 1)
+    acc[...] = nt(own[0], w_main[0])
+    for j in range(1, parts):
+        acc[...] += nt(own[j], w_main[j])
+    for j in range(last):
+        acc[...] += nt(came[j], w_main[parts + j])
+    for j in range(last, parts):
+        take_chunk(j)
+        acc[...] += nt(came[j], w_main[parts + j])
+    gates_copy().wait_recv()
+    moved = pltpu.roll(gates_came[...].astype(F32), heads, axis=1)
+    both = gates[...].astype(F32) + moved
+    both = both.astype(BF16)
+    acc[...] += nt(both, w_gates_ref[...])
+    fold = copy_to(fold_src, fold_dst, s_send.at[3], s_recv.at[3], place.core_peer)
     fold_src[...] = acc[rows:, :].astype(BF16)
     fold.start()
-
-    def inner_copy():
-        return copy_to(inner_src, inner_dst, small_send.at[1], small_recv.at[1], place.x_peer)
+    gate_grads = nn(turned_ref[:, pl.ds(0, tokens)], both).T
+    for i in range(width // 128):
+        misc[16 + 8 * i : 24 + 8 * i, :] = gate_grads[:8, i * 128 : (i + 1) * 128]
 
     def misc_copy(n, peer):
-        return copy_to(
-            misc, misc_came.at[n], small_send.at[2 + n], small_recv.at[2 + n], peer
-        )
-
-    row_at = lax.broadcasted_iota(jnp.int32, (MISC, 128), 0)
-
-    def block(j, i):
-        if i == 0:
-            over_y(j, True).wait_recv()
-        at_rows = pl.ds(i * high, high)
-        first = jnp.where(side == 0, own_ref[:, cut(j)], came[j])
-        total[parts + 2 * j + i] = (
-            nn(turned_ref[at_rows, pl.ds(0, tokens)], first)
-            + nn(turned_ref[at_rows, pl.ds(tokens, tokens)], across[j])
-        ).astype(BF16)
-
-    for n in range(2 * parts):
-        block(n // 2, n % 2)
-        chain.step(parts + n)
-        if n == 0:
-            fold.wait_recv()
-            grad = acc[:rows, :] + fold_dst[...].astype(F32)
-            back_ref[...] = grad
-            found = grad * hat_ref[...]
-            inner = jnp.sum(found * scale_ref[...], axis=1, keepdims=True)
-            inner_src[...] = jnp.broadcast_to(inner, (rows, 128))
-            inner_copy().start()
-            gain = jnp.sum(found, axis=0, keepdims=True)
-            for i in range(width // 128):
-                misc[i : i + 1, :] = gain[:, i * 128 : (i + 1) * 128]
-            misc_copy(0, place.core_peer).start()
-        if n == 1:
-            misc_copy(0, place.core_peer).wait()
-            both = (row_at < 16) | (row_at >= 80)
-            misc[...] += jnp.where(both, misc_came[0], 0.0)
-            misc_copy(1, place.x_peer).start()
-        if n == 2:
-            misc_copy(1, place.x_peer).wait()
-            misc[...] += jnp.where(row_at >= 80, misc_came[1], 0.0)
-            misc_copy(2, place.y_peer).start()
-        if n == 3:
-            misc_copy(2, place.y_peer).wait()
-            misc[...] += misc_came[2]
-            inner_copy().wait()
-            inner_ref[...] = inner_src[...] + inner_dst[...]
-        if n > 3:
-            small.step(n - 4)
-
-    @pl.loop(3 * parts, chain.steps())
-    def _(t):
-        chain.step(t)
-
-        @pl.when(t - parts - 4 < small.steps())
-        def _():
-            small.step(t - parts - 4)
-
-    @pl.loop(chain.steps() - parts - 4, small.steps())
-    def _(t):
-        small.step(t)
+        return copy_to(misc, misc_came.at[n], s_send.at[4 + n], s_recv.at[4 + n], peer)
+
+    row_of = lax.broadcasted_iota(jnp.int32, (MISC, 128), 0)
+    block(last)
+    fold.wait_recv()
+    grad = acc[:rows, :] + fold_dst[...].astype(F32)
+    found = grad * hat_ref[...]
+    in_send[1] = column(jnp.sum(found * norm_ref[...], axis=1, keepdims=True))
+    inner_copy(1).start()
+    acc[:rows, :] = grad
+    store_row(0, jnp.sum(found, axis=0, keepdims=True))
+    misc_copy(0, place.core_peer).start()
+    block(last + 1)
+    misc_copy(0, place.core_peer).wait()
+    misc[...] += jnp.where((row_of < 16) | (row_of >= 80), misc_came[0], 0.0)
+    misc_copy(1, place.x_peer).start()
+    chain.step(pieces)
+    misc_copy(1, place.x_peer).wait()
+    misc[...] += jnp.where(row_of >= 80, misc_came[1], 0.0)
+    misc_copy(2, place.y_peer).start()
+    inner_copy(1).wait()
+    inner = (in_send[1, :, :1] + in_came[1, :, :1]) / (2 * width)
+    input_ref[...] += inv_one_ref[:, :1] * (acc[:rows, :] * norm_ref[...] - hat_ref[...] * inner)
+    chain.step(pieces + 1)
+    misc_copy(2, place.y_peer).wait()
+    misc[...] += misc_came[2]
+
+    @pl.loop(pieces + 2, chain.steps())
+    def _(u):
+        chain.step(u)
+        small.step(u - pieces - 2)
+
+    @pl.loop(chain.steps() - pieces - 2, small.steps())
+    def _(u):
+        small.step(u)
 
     small.drain()
     sums_ref[...] = misc_home[...]
     chain.drain()
-    fold.wait_send()
+    for copy in (to_core, to_pair, forward, gates_copy(), fold):
+        copy.wait_send()
+    for n in range(halves_of):
+        dg_copy(n).wait_send()
     for j in range(parts):
         over_x(j).wait_send()
         over_y(j, True).wait_send()
 
 
-def back(own, turned, w_main, gates, w_gates, gated, branch, hat, scale, misc):
+def rear(
+    back, resid, inv_two, ffn_gain, top, raw, sig, query, keys, values, log, attended, cos, sin,
+    at, start, key_at, q_gain, k_gain, turned, gated, w_gates, hat, inv_one, norm_gain,
+    wq, wk, wv, wo,
+):
     count = lax.axis_size("group")
-    tokens, main = own.shape
-    rows = tokens // 2
-    width = turned.shape[0]
+    rows, width = back.shape
+    tokens = 2 * rows
+    hd = 128
+    heads, kv_heads = query.shape[1] // hd, keys.shape[1] // hd
+    qw, kw = heads * hd, kv_heads * hd
+    cols = 2 * hd
+    parts = heads // 2 + kv_heads
     high = gated.shape[0]
-    cols = 256
-    parts = main // cols
-    pieces = 3 * parts
+    pieces = 2 * parts + width // cols
     anywhere = pl.BlockSpec(memory_space=pl.ANY)
     local = pl.BlockSpec(memory_space=pltpu.VMEM)
     dma = pltpu.SemaphoreType.DMA
+    struct = jax.ShapeDtypeStruct
     return pl.pallas_call(
-        functools.partial(back_kernel, count),
+        functools.partial(rear_kernel, count, heads, kv_heads),
         out_shape=(
-            jax.ShapeDtypeStruct((2 * pieces, high, cols), BF16),
-            jax.ShapeDtypeStruct((rows, width), F32),
-            jax.ShapeDtypeStruct((rows, 128), F32),
-            jax.ShapeDtypeStruct((MISC, 128), F32),
+            struct((2 * pieces, high, cols), BF16),
+            struct((rows, width), F32),
+            struct((MISC, 128), F32),
         ),
-        in_specs=[local] * 10,
-        out_specs=(anywhere, local, local, local),
+        in_specs=[local] * 25 + [anywhere] * 4,
+        out_specs=(anywhere, local, local),
         scratch_shapes=[
+            pltpu.VMEM((2 * parts, width, cols), BF16),
+            pltpu.VMEM((2, qw, width), BF16),
+            pltpu.VMEM((4 * rows, width), BF16),
+            pltpu.VMEM((tokens, qw), F32),
+            pltpu.VMEM((tokens, qw), BF16),
+            pltpu.VMEM((tokens, qw), BF16),
+            pltpu.VMEM((tokens, kw), F32),
+            pltpu.VMEM((tokens, kw), F32),
+            pltpu.VMEM((tokens, 128), BF16),
+            pltpu.VMEM((tokens, 128), BF16),
+            pltpu.VMEM((parts, tokens, cols), BF16),
             pltpu.VMEM((parts, tokens, cols), BF16),
             pltpu.VMEM((parts, tokens, cols), BF16),
             pltpu.VMEM((pieces, high, cols), BF16),
@@ -1064,81 +1219,63 @@
             pltpu.VMEM((tokens, width), F32),
             pltpu.VMEM((rows, width), BF16),
             pltpu.VMEM((rows, width), BF16),
-            pltpu.VMEM((rows, 128), F32),
-            pltpu.VMEM((rows, 128), F32),
-            dma((parts,)), dma((parts,)), dma((parts,)), dma((parts,)), dma((5,)), dma((5,)),
+            pltpu.VMEM((2, rows, 128), F32),
+            pltpu.VMEM((2, rows, 128), F32),
+            dma((2, kv_heads, 4)), dma((3,)), dma((3,)), dma((heads // 2,)), dma((heads // 2,)),
+            dma((parts,)), dma((parts,)), dma((parts,)), dma((parts,)), dma((7,)), dma((7,)),
             *chain_semaphores(pieces), *chain_semaphores(1),
         ],
         compiler_params=pltpu.CompilerParams(
-            collective_id=2, has_side_effects=True, vmem_limit_bytes=56 << 20
+            collective_id=2, has_side_effects=True, vmem_limit_bytes=60 << 20
         ),
         cost_estimate=pl.CostEstimate(
-            flops=2 * tokens * width * main * 6, bytes_accessed=100 << 20, transcendentals=0
+            flops=2 * tokens * width * (qw + 2 * kw) * 6, bytes_accessed=100 << 20,
+            transcendentals=heads * tokens * tokens,
         ),
-    )(own, turned, w_main, gates, w_gates, gated, branch, hat, scale, misc)
-
-
-def masked_scores(query, keys, segment, place, scale):
-    scores = jnp.einsum("qkgd,skd->kgqs", query, keys, preferred_element_type=F32) * scale
-    allowed = (segment[:, None] == segment[None, :]) & (place[None, :] <= place[:, None])
-    return jnp.where(allowed, scores, NEGATIVE)
+    )(
+        back, resid, inv_two, ffn_gain, top, raw, sig, query, keys, values, log, attended, cos,
+        sin, at, start, key_at, q_gain, k_gain, turned, gated, w_gates, hat, inv_one, norm_gain,
+        wq, wk, wv, wo,
+    )
 
 
 def body(
     tokens, lengths, norm_gain, w_query, w_key, w_value, w_head_gate, query_gain, key_gain,
     w_out, ffn_gain, w_gate, w_up, w_down, grad_out,
 ):
-    row_count = lax.axis_size("row")
     rows, d_loc = tokens.shape
     group_tok = 2 * rows
-    width = d_loc * row_count
     head_dim = query_gain.shape[0]
     q_half = w_query.shape[1] // 2
     kv_half = w_key.shape[1] // 2
     gate_half = w_head_gate.shape[1] // 2
-    heads = q_half // head_dim
-    kv_heads = kv_half // head_dim
-    share = heads // kv_heads
-    main = q_half + 2 * kv_half
-    scale = head_dim ** (-0.5)
     row_at = lax.axis_index("row")
     col_at = lax.axis_index("col")
     side = lax.axis_index("group") % 2
 
     steps = jnp.arange(rows, dtype=jnp.int32)
     index = jnp.concatenate([col_at * rows + steps, (1 - col_at) * rows + steps])
-    segment, place = places(lengths, index)
+    place = places(lengths, index)[1]
     cosines, sines = rope_tables(place, head_dim)
     signed = jnp.concatenate([-sines[:, : head_dim // 2], sines[:, head_dim // 2 :]], axis=1)
-    cos_heads = cosines[:, None, :]
-    sin_heads = sines[:, None, :]
+    positions = (
+        jnp.broadcast_to(index[:, None], (group_tok, 128)),
+        jnp.broadcast_to((index - place)[:, None], (group_tok, 128)),
+        jnp.broadcast_to(index[None], (8, group_tok)),
+    )
     w_gates = jnp.pad(
         jnp.concatenate(halves(w_head_gate, 1, row_at), axis=1),
         ((0, 0), (0, 128 - 2 * gate_half)),
     )
+    gains = (query_gain[None], key_gain[None])
     (
         normed_two, resid, inverse_two, hat, inverse_one, permuted_pair, grad_all, early_grad,
         raw, gate_sigmoid, query, keys, values, logsum, attended, gated_both,
     ) = front(
-        tokens, grad_out, norm_gain[None], ffn_gain[None], query_gain[None], key_gain[None],
-        cosines, signed,
-        jnp.broadcast_to(index[:, None], (group_tok, 128)),
-        jnp.broadcast_to((index - place)[:, None], (group_tok, 128)),
-        jnp.broadcast_to(index[None], (8, group_tok)),
+        tokens, grad_out, norm_gain[None], ffn_gain[None], *gains, cosines, signed, *positions,
         w_gates, w_query, w_key, w_value, w_out, w_down,
     )
-    inverse_one, inverse_two = inverse_one[:, 0], inverse_two[:, 0]
-    gate_sigmoid = gate_sigmoid[:, :heads]
-    permuted = permuted_pair[:group_tok]
     turned = permuted_pair.T
-    raw_query = raw[:, :q_half].reshape(group_tok, heads, head_dim)
-    raw_key = raw[:, q_half : q_half + kv_half].reshape(group_tok, kv_heads, head_dim)
-    query_inverse = lax.rsqrt(jnp.mean(raw_query * raw_query, axis=-1, keepdims=True) + EPS)
-    key_inverse = lax.rsqrt(jnp.mean(raw_key * raw_key, axis=-1, keepdims=True) + EPS)
-    query = query.reshape(group_tok, kv_heads, share, head_dim)
-    keys = keys.reshape(group_tok, kv_heads, head_dim)
-    values = values.reshape(group_tok, kv_heads, head_dim)
-    attended = attended.reshape(group_tok, heads, head_dim)
     gated, gated_came = gated_both[0], gated_both[1]
     first_side = side == 0
     gated_pair = jnp.concatenate(
@@ -1147,113 +1284,46 @@
             swap_groups(jnp.where(first_side, gated_came, gated)),
         ]
     ).T
-    splits = [halves(w, 1, row_at) for w in (w_query, w_key, w_value)]
-    w_main = jnp.concatenate([own for own, _ in splits] + [other for _, other in splits], axis=1)
-    w_back = jnp.concatenate(halves(w_out, 0, row_at))
-
-    def sum_cores(values):
-        return values[:rows] + swap(values[rows:].astype(BF16), "col").astype(F32)
 
     pair_sum, down_sum, _, _, branch, branch_out, d_normed_two = ffn(
         normed_two, grad_all, early_grad, w_gate, w_up, w_down
     )
     output = (resid + branch + swap_groups(branch_out).astype(F32)).astype(BF16)
 
-    d_top = grad_out.astype(F32)
-    ffn_gain_part = jnp.sum(d_normed_two * resid * inverse_two[:, None], axis=0)
-    scaled_two = d_normed_two * ffn_gain
-    inner_two = jnp.sum(scaled_two * resid, axis=1)
-    inner_two = inner_two + swap(inner_two, "row")
-    d_resid = (
-        d_top
-        + inverse_two[:, None] * scaled_two
-        - resid * (inverse_two**3 * inner_two / width)[:, None]
-    )
-    d_branch = d_resid.astype(BF16)
-    branch_all = jnp.concatenate([d_branch, swap(d_branch, "col")])
-    branch_across = swap_groups(d_branch)
-    branch_pair = jnp.concatenate([branch_all, branch_across, swap(branch_across, "col")])
-    d_gated_part = nt(branch_all, w_back)
-    d_gated = d_gated_part[:, :q_half] + swap(
-        d_gated_part[:, q_half:].astype(BF16), "row"
-    ).astype(F32)
-    d_gated = d_gated.reshape(group_tok, heads, head_dim)
-    d_attended = (d_gated * gate_sigmoid[:, :, None]).astype(BF16)
-    d_logit = jnp.sum(d_gated * attended, axis=-1) * gate_sigmoid * (1.0 - gate_sigmoid)
-    d_attended = d_attended.reshape(group_tok, kv_heads, share, head_dim)
-
-    scores = masked_scores(query, keys, segment, place, scale)
-    probs = jnp.exp(scores - logsum[:, :, 0].reshape(kv_heads, share, group_tok, 1))
-    probs_low = probs.astype(BF16)
-    d_probs = jnp.einsum("qkgd,skd->kgqs", d_attended, values, preferred_element_type=F32)
-    d_scores = (probs * (d_probs - jnp.sum(d_probs * probs, axis=-1, keepdims=True))).astype(BF16)
-    d_query = jnp.einsum("kgqs,skd->qkgd", d_scores, keys, preferred_element_type=F32) * scale
-    d_keys = jnp.einsum("kgqs,qkgd->skd", d_scores, query, preferred_element_type=F32) * scale
-    d_values = jnp.einsum("kgqs,qkgd->skd", probs_low, d_attended, preferred_element_type=F32)
-    d_query = d_query.reshape(group_tok, heads, head_dim)
-    d_raw_query, query_gain_part = head_norm_back(
-        unrotate(d_query, cos_heads, sin_heads), raw_query, query_inverse, query_gain
-    )
-    d_raw_key, key_gain_part = head_norm_back(
-        unrotate(d_keys, cos_heads, sin_heads), raw_key, key_inverse, key_gain
-    )
-    d_main = jnp.concatenate(
-        [
-            d_raw_query.reshape(group_tok, q_half),
-            d_raw_key.reshape(group_tok, kv_half),
-            d_values.reshape(group_tok, kv_half),
-        ],
-        axis=1,
-    ).astype(BF16)
-    d_gates = d_logit.astype(BF16)
-    d_gates = jnp.concatenate([d_gates, swap(d_gates, "row")], axis=1)
-    gates_part = lax.dot_general(
-        d_gates, permuted, (((0,), (0,)), ((), ())), preferred_element_type=F32
-    )
-    misc = jnp.concatenate(
-        [
-            jnp.zeros((8, 128), F32),
-            ffn_gain_part.reshape(8, 128),
-            gates_part.reshape(64, 128),
-            query_gain_part[None],
-            key_gain_part[None],
-            jnp.zeros((6, 128), F32),
-        ]
-    )
-    grads, d_normed_one, inner_one, sums = back(
-        d_main, turned, w_main, jnp.pad(d_gates, ((0, 0), (0, 128 - 2 * gate_half))), w_gates,
-        gated_pair, branch_pair, hat, norm_gain[None], misc,
-    )
-    input_grad = d_resid + inverse_one[:, None] * (
-        d_normed_one * norm_gain - hat * (inner_one[:, :1] / width)
+    grads, input_grad, sums = rear(
+        d_normed_two, resid, inverse_two, ffn_gain[None], grad_out, raw, gate_sigmoid, query,
+        keys, values, logsum, attended, cosines, signed, *positions, *gains, turned, gated_pair,
+        w_gates, hat, inverse_one, norm_gain[None], w_query, w_key, w_value, w_out,
     )
     grad_norm_gain = sums[:8].reshape(d_loc)
     grad_ffn_gain = sums[8:16].reshape(d_loc)
-    grad_gates = sums[16:80].reshape(2 * gate_half, d_loc)
+    grad_gates = sums[16:80].reshape(8, 2 * gate_half, 128).transpose(1, 0, 2)
+    grad_gates = grad_gates.reshape(2 * gate_half, d_loc)
     grad_head_gate = ordered(grad_gates[:gate_half], grad_gates[gate_half:], 0, row_at).T
+
     grads = grads.reshape(2, -1, q_half, 256)
-    count = main // 256
+    count = d_loc // 256
     out_sum = grads[:, :count].transpose(0, 2, 1, 3).reshape(2 * q_half, d_loc)
-    first_sum = (
-        grads[:, count:]
-        .reshape(2, count, 2, q_half, 256)
-        .transpose(2, 3, 0, 1, 4)
-        .reshape(d_loc, 2 * main)
-    )
-
-    def piece(start, size):
-        own = first_sum[:, start : start + size]
-        other = first_sum[:, main + start : main + start + size]
-        return ordered(own, other, 1, row_at).astype(F32)
-
     grad_out_full = ordered(*jnp.split(out_sum, 2, axis=0), 0, row_at).astype(F32)
+    chunks = grads[:, count:].reshape(2, kv_half // head_dim, 2, 2, q_half, 256)
+
+    def collect(at, start, size):
+        def side_of(n):
+            pieces = [
+                chunks[n, i, at, :, :, start : start + size].reshape(d_loc, size)
+                for i in range(chunks.shape[1])
+            ]
+            return jnp.concatenate(pieces, axis=1)
+
+        return ordered(side_of(0), side_of(1), 1, row_at).astype(F32)
+
     return (
         output,
         input_grad,
         grad_norm_gain,
-        piece(0, q_half),
-        piece(q_half, kv_half),
-        piece(q_half + kv_half, kv_half),
+        collect(0, 0, 256),
+        collect(1, 0, 128),
+        collect(1, 128, 128),
         grad_head_gate,
         sums[80],
         sums[81],

time: 768 us -> 686 us (0.89)
  local copies, waits for them, and re-layouts: 68.9 us -> 16.8 us
  Pallas kernels: 568 us -> 614 us
  other arithmetic: 84.2 us -> 43.1 us
  matrix products: 17.1 us -> 0 us
  waiting for transfers between devices: 9.71 us -> 0.01 us
    pallas_call x1, Pallas kernels: 124 us -> 164 us  [rear(): pl.pallas_call(functools.partial(rear_kernel, count, heads, kv_heads), ou...]
    reshape x14 -> x0, local copies, waits for them, and re-layouts: 22 us -> none  [the longest x1 7.74 us: body(): first_sum = grads[:, count:].reshape(2, count, 2, q_half, 256).transpose(...]
    dot_general x7 -> x0, matrix products: 17.1 us -> none  [the longest x1 6.04 us: body(): jnp.einsum('kgqs,qkgd->skd', probs_low, d_attended, preferred_element_typ...]
    reduce_sum x8 -> x1, other arithmetic: 11.5 us -> 0.74 us  [places(): place = index - jnp.sum(passed * lengths_group[None, :], axis=1)]
    unnamed x121 -> x13, local copies, waits for them, and re-layouts: 9.73 us -> 1.51 us
  transfers between devices with their start and end apart: 8 -> 2, of which waited for: 2 -> 0; matrix products, arithmetic and copies ran while one was open for 20% -> 7% of each run, Pallas kernels for 16% -> 74%
where the time goes in v4:
time: 686 us; the launch traced here: 676 us
  Pallas kernels  614 us (90%)
  other arithmetic  43.1 us (6%)
  local copies, waits for them, and re-layouts  16.8 us (2%)
    pallas_call x1, Pallas kernels, ffn(): pl.pallas_call(functools.partial(ffn_kernel, count, chunks), out_shape=(j...  337 us
    pallas_call x1, Pallas kernels, rear(): pl.pallas_call(functools.partial(rear_kernel, count, heads, kv_heads), ou...  164 us
    pallas_call x1, Pallas kernels, front(): pl.pallas_call(functools.partial(front_kernel, count, heads, kv_heads), o...  113 us
  transfers between devices with their start and end apart: 2, of which 0 were waited for; matrix products, arithmetic and copies ran while one was open for 7% of the time, Pallas kernels for 74%

profile of v4, /device:TPU:24, one launch (start us, length us, event | category | flops | bytes accessed | tf_op | source)
XLA Modules:
  0.0 676.3 jit_solution(187032456408284076)
XLA Ops:
  0.7 0.8 reduce-window.8
  2.4 1.2 fusion
  3.6 0.9 pad_maximum_fusion.6.cos_ref
  5.5 0.9 pad_maximum_fusion.7.sin_ref
  7.2 0.9 broadcast_in_dim.19.start_ref
  8.0 0.9 broadcast_in_dim.18.at_ref
  9.5 112.6 %shard_map.254 = (bf16[320,1024]{1,0:T(8,128)(2,1)}, f32[320,1024]{1,0:T(8,128)}, f32[320,128]{1,0:T(8,128)}, f32[320,1024]{1,0:T(8,128)}, f32[320,128]{1,0:T(8,...) custom-call(bf16[320,1024]{1,0:T(8,128)(2,1)} %tok_ref.1, ...), custom_call_target="tpu_custom_call" | custom-call | flops 12079595520 | bytes 41943040 | tf_op jit(solution)/shard_map/pallas_call | solution.py:795
  122.1 1.7 copy.46
  123.8 1.0 select_bitcast_fusion.1
  124.8 1.2 collective-permute-start.1
  126.0 337.1 %shard_map.255 = (bf16[2,1024,3072]{2,1,0:T(8,128)(2,1)}, bf16[3072,1024]{1,0:T(8,128)(2,1)}, bf16[2,12,2,1024,128]{4,3,2,1,0:T(8,128)(2,1)}, bf16[2,12,128,1024...) custom-call(bf16[320,1024]{1,0:T(8,128)(2,1)} %get-tuple-element.39.h_ref, ...), custom_call_target="tpu_custom_call" | custom-call | flops 32212254720 | bytes 209715200 | tf_op jit(solution)/shard_map/pallas_call | solution.py:513
  463.2 13.1 %bitcast_convert_fusion = (f32[1024,3072]{1,0:T(8,128)}, f32[1024,3072]{1,0:T(8,128)}) fusion(bf16[2,1024,3072]{2,1,0:T(8,128)(2,1)} %get-tuple-element.60), kind=kLoop, calls=%fused_computation | loop fusion | flops 6291456 | bytes 37748736 | tf_op jit(solution)/shard_map/convert_element_type | solution.py:1333
  476.2 2.7 copy.45
  478.9 9.1 %convert_element_type.54 = f32[3072,1024]{1,0:T(8,128)} convert(bf16[3072,1024]{1,0:T(8,128)(2,1)} %get-tuple-element.61) | non-fusion elementwise | flops 3145728 | bytes 18874368 | tf_op jit(solution)/shard_map/convert_element_type | solution.py:1334
  488.0 2.2 maximum_bitcast_fusion.gated_ref
  490.2 164.3 %shard_map.256 = (bf16[24,512,256]{2,1,0:T(8,128)(2,1)}, f32[320,1024]{1,0:T(8,128)}, f32[88,128]{1,0:T(8,128)}) custom-call(f32[320,1024]{1,0:T(8,128)} %get-tuple-element.44.back_ref, f32[320,1024]{1,0:T(8,128)} %get-tuple-element.38.resid_ref, f32[320,128]{1,0:T(8,128)} %get-tuple-element.45.inv_two_ref, f32[1,1024]{1,0:T(1,128)} %bitcast.85, ...), custom_call_target="tpu_custom_call" | custom-call | flops 8053063680 | bytes 104857600 | tf_op jit(solution)/shard_map/pallas_call | solution.py:1190
  654.6 1.7 slice_bitcast_fusion
  656.3 2.5 slice.106
  661.7 2.4 maximum_convert_fusion.1
  665.0 1.6 maximum_convert_fusion.3
  666.9 1.6 maximum_convert_fusion.2
  669.0 2.6 maximum_convert_fusion
  672.7 2.3 add_convert_fusion
  675.0 1.1 copy.53
  (38 shorter events, 8.9 us)
Async XLA Ops:
  124.8 363.2 %collective-permute-start.1 = (bf16[640,512]{0,1:T(8,128)(2,1)}, bf16[640,512]{0,1:T(8,128)(2,1)}, u32[]{:S(2)}, u32[]{:S(2)}) collective-permute-start(bf16[640,512]{0,1:T(8,128)(2,1)} %get-tuple-element.81), channel_id=1, source_target_pairs={{0,4},{4,0},{8,12},{12,8},{16,20},{20,16},{24,28},{28,24},{1,5},{5... | collective-permute-start | bytes 1966088 | tf_op jit(solution)/shard_map/ppermute | solution.py:20
  463.1 209.6 %collective-permute-start = (bf16[320,1024]{1,0:T(8,128)(2,1)}, bf16[320,1024]{1,0:T(8,128)(2,1)}, u32[]{:S(2)}, u32[]{:S(2)}) collective-permute-start(bf16[320,1024]{1,0:T(8,128)(2,1)} %get-tuple-element.43), channel_id=1, source_target_pairs={{0,4},{4,0},{8,12},{12,8},{16,20},{20,16},{24,28},{28,24},{1,5},{5... | collective-permute-start | bytes 1966088 | tf_op jit(solution)/shard_map/ppermute | solution.py:20
  463.1 13.1 %copy-start = (bf16[1280,1024]{1,0:T(8,128)(2,1)S(1)}, bf16[1280,1024]{1,0:T(8,128)(2,1)}, u32[]{:S(2)}) copy-start(bf16[1280,1024]{1,0:T(8,128)(2,1)} %get-tuple-element.53) | copy-start | bytes 7864324
  660.6 1.1 copy-start.4
  669.0 3.7 copy-start.2
  669.0 3.7 copy-start.3
  671.6 3.4 copy-start.1

commit v5 on v4

--- a/solution.py
+++ b/solution.py
@@ -51,10 +51,11 @@
 
 
 TILE = 256
-HOP = 1
+HOP = 2
 WIDE = 128
 EARLY = 6
-AHEAD = 3
+AHEAD = 2
+LATE = 3
 
 
 def nt(a, b):
@@ -260,11 +261,11 @@
 
 def ffn_kernel(
     count, chunks, h_ref, top_ref, early_ref, gate_ref, up_ref, down_ref,
-    pair_grads_ref, down_grads_ref, pair_came_ref, down_came_ref, branch_ref, branch_out_ref,
-    back_ref,
+    pair_grads_ref, down_grads_ref, late_pair_ref, late_down_ref, pair_came_ref, down_came_ref,
+    branch_ref, branch_out_ref, back_ref,
     h_all, h_turned, sent, came, top_sent, top_came, grad_part, w_pair, w_down, acc_branch, acc_back, parts, inner_turned,
     pair_total, down_total, pair_stage, down_stage, reduce_recv,
-    gather_send, gather_recv, x_send, x_recv, top_send, top_recv, load_sem, weight_sem, fold_send, fold_recv,
+    gather_send, gather_recv, x_send, x_recv, top_send, top_recv, late_sem, load_sem, weight_sem, fold_send, fold_recv,
     *chain_sems,
 ):
     place = Place(count)
@@ -324,27 +325,25 @@
 
         top_exchange(j).start()
 
-    @pl.loop(0, chunks)
-    def _(j):
-        weight_copies(j)[2].wait()
-
-    @pl.loop(EARLY, min(EARLY + AHEAD, chunks))
-    def _(j):
-        top_project(j)
-
-    h_all[slot(0), :] = h_ref[...]
-    acc_branch[...] = jnp.zeros_like(acc_branch)
-    acc_back[...] = jnp.zeros_like(acc_back)
-    to_y.wait_recv()
-    forward.start()
-    to_core.wait_recv()
-    forward.wait_recv()
-
     def exchange(j):
         return copy_to(
             sent.at[lax.rem(j, 3)], came.at[j], x_send.at[j], x_recv.at[j], place.x_peer
         )
 
+    def first_half(i):
+        at_rows = pl.ds(2 * i * rows, 2 * rows)
+        n = i * chunks
+        return copy_to(
+            sent.at[0, at_rows, :], came.at[0, at_rows, :], x_send.at[n], x_recv.at[n],
+            place.x_peer,
+        )
+
+    def project_half(i):
+        for n in range(2):
+            at_rows = slot(2 * i + n)
+            sent[0, at_rows, :] = nn(h_all[at_rows, :], w_pair[0]).astype(BF16)
+        first_half(i).start()
+
     def project(j):
         for copy in weight_copies(j)[:2]:
             copy.wait()
@@ -353,10 +352,15 @@
         def _(i):
             sent[lax.rem(j, 3), tile(i), :] = nn(h_all[tile(i), :], w_pair[j]).astype(BF16)
 
-        exchange(j).start()
-
     def work(j):
-        exchange(j).wait_recv()
+        @pl.when(j == 0)
+        def _():
+            first_half(0).wait_recv()
+            first_half(1).wait_recv()
+
+        @pl.when(j > 0)
+        def _():
+            exchange(j).wait_recv()
 
         @pl.when(j < EARLY)
         def _():
@@ -416,33 +420,70 @@
                 into[at_rows, :].astype(F32) + stage[at_rows, :].astype(F32)
             ).astype(BF16)
 
-    chain = Chain(place, chunks, 3, total, landed, home, add, chain_sems)
-
-    for j in range(min(2, chunks)):
-        project(j)
+    ours = chunks - LATE
+    chain = Chain(place, ours, 3, total, landed, home, add, chain_sems)
+
+    def late_copies(c):
+        return (
+            pltpu.make_async_copy(pair_total.at[c], late_pair_ref.at[c - ours], late_sem.at[0, c - ours]),
+            pltpu.make_async_copy(down_total.at[c], late_down_ref.at[c - ours], late_sem.at[1, c - ours]),
+        )
+
+    h_all[slot(0), :] = h_ref[...]
+    for copy in weight_copies(0)[:2]:
+        copy.wait()
+    to_core.wait_recv()
+    project_half(0)
+
+    @pl.loop(0, chunks)
+    def _(j):
+        weight_copies(j)[2].wait()
+
+    @pl.loop(EARLY, min(EARLY + AHEAD, chunks))
+    def _(j):
+        top_project(j)
+
+    acc_branch[...] = jnp.zeros_like(acc_branch)
+    acc_back[...] = jnp.zeros_like(acc_back)
+    to_y.wait_recv()
+    forward.start()
+    forward.wait_recv()
+    project_half(1)
+    project(1)
 
     @pl.loop(0, tiles)
     def _(i):
         h_turned[:, tile(i)] = h_all[tile(i), :].T
+
+    first_half(0).wait_send()
+    first_half(1).wait_send()
+    exchange(1).start()
 
     @pl.loop(0, chunks)
     def _(t):
         work(t)
         chain.step(3 * t - 1, HOP)
         gradients(t)
+
+        @pl.when(t >= ours)
+        def _():
+            for copy in late_copies(t):
+                copy.start()
+
         chain.step(3 * t, HOP)
 
         @pl.when(t + 2 < chunks)
         def _():
-            @pl.when(t >= 1)
+            @pl.when(t >= 2)
             def _():
                 exchange(t - 1).wait_send()
 
             project(t + 2)
-
-        @pl.when(EARLY + AHEAD + t < chunks)
+            exchange(t + 2).start()
+
+        @pl.when((t + AHEAD >= EARLY + AHEAD) & (t + AHEAD < chunks))
         def _():
-            top_project(EARLY + AHEAD + t)
+            top_project(t + AHEAD)
 
         chain.step(3 * t + 1, HOP)
 
@@ -480,9 +521,14 @@
         acc_back[slot(0), :] + reduce_recv[0, 0].astype(F32) + reduce_recv[0, 2].astype(F32)
     )
 
-    @pl.loop(3 * chunks + 1, chain.steps(HOP))
+    @pl.loop(3 * chunks + 1, max(3 * chunks + 1, chain.steps(HOP)))
     def _(u):
         chain.step(u, HOP)
+
+    @pl.loop(ours, chunks)
+    def _(c):
+        for copy in late_copies(c):
+            copy.wait()
 
     chain.drain()
 
@@ -508,21 +554,23 @@
     anywhere = pl.BlockSpec(memory_space=pl.ANY)
     local = pl.BlockSpec(memory_space=pltpu.VMEM)
     dma = pltpu.SemaphoreType.DMA
-    pieces = 3 * chunks
+    pieces = 3 * (chunks - LATE)
     flops = 2 * tokens * width * hidden * 8
     return pl.pallas_call(
         functools.partial(ffn_kernel, count, chunks),
         out_shape=(
             jax.ShapeDtypeStruct((2, width, 2 * hidden), BF16),
             jax.ShapeDtypeStruct((2 * hidden, width), BF16),
-            jax.ShapeDtypeStruct((2, chunks, 2, width, wide), BF16),
-            jax.ShapeDtypeStruct((2, chunks, wide, width), BF16),
+            jax.ShapeDtypeStruct((LATE, 2, width, wide), BF16),
+            jax.ShapeDtypeStruct((LATE, wide, width), BF16),
+            jax.ShapeDtypeStruct((2, chunks - LATE, 2, width, wide), BF16),
+            jax.ShapeDtypeStruct((2, chunks - LATE, wide, width), BF16),
             jax.ShapeDtypeStruct((rows, width), F32),
             jax.ShapeDtypeStruct((rows, width), BF16),
             jax.ShapeDtypeStruct((rows, width), F32),
         ),
         in_specs=[local, local, local, anywhere, anywhere, anywhere],
-        out_specs=(anywhere, anywhere, anywhere, anywhere, local, local, local),
+        out_specs=(anywhere,) * 6 + (local,) * 3,
         scratch_shapes=[
             pltpu.VMEM((tokens, width), BF16),
             pltpu.VMEM((width, tokens), BF16),
@@ -542,9 +590,9 @@
             pltpu.VMEM((2, width, wide), BF16),
             pltpu.VMEM((2, wide, width), BF16),
             pltpu.VMEM((2, 3, rows, width), BF16),
-            dma((3,)), dma((3,)), dma((chunks,)), dma((chunks,)),
+            dma((3,)), dma((3,)), dma((chunks + 1,)), dma((chunks + 1,)),
             dma((chunks - EARLY,)), dma((chunks - EARLY,)),
-            dma((2,)), dma((3, chunks)), dma((2, 3)), dma((2, 3)),
+            dma((2, LATE)), dma((2,)), dma((3, chunks)), dma((2, 3)), dma((2, 3)),
             *chain_semaphores(pieces),
         ],
         compiler_params=pltpu.CompilerParams(
@@ -859,12 +907,12 @@
     count, heads, kv_heads, back_ref, resid_ref, inv_two_ref, second_ref, top_ref, raw_ref,
     sig_ref, q_ref, k_ref, v_ref, log_ref, attended_ref, cos_ref, sin_ref, at_ref, start_ref,
     key_at_ref, q_gain_ref, k_gain_ref, turned_ref, gated_ref, w_gates_ref, hat_ref, inv_one_ref,
-    norm_ref, wq_ref, wk_ref, wv_ref, wo_ref,
-    grads_ref, input_ref, sums_ref,
+    norm_ref, wq_ref, wk_ref, wv_ref, wo_ref, late_pair_ref, late_down_ref, pair_in, down_in,
+    grads_ref, input_ref, sums_ref, pair_grads_ref, down_grads_ref,
     w_main, wo, branch, dg_own, dg_send, dg_came, dk, dv, gates, gates_came, own, came, across,
     total, landed, misc, misc_came, misc_landed, misc_home, acc, fold_src, fold_dst, in_send,
-    in_came,
-    w_sem, b_send, b_recv, d_send, d_recv, x_send, x_recv, y_send, y_recv, s_send, s_recv,
+    in_came, late_pair, late_down, late_pair_came, late_down_came,
+    w_sem, late_sem, b_send, b_recv, d_send, d_recv, x_send, x_recv, y_send, y_recv, s_send, s_recv,
     *chain_sems,
 ):
     place = Place(count)
@@ -897,8 +945,32 @@
         loads.append(pltpu.make_async_copy(wo_ref.at[tile(at, qw), :], wo.at[i], w_sem.at[i, 0, 3]))
     for copy in loads:
         copy.start()
+    late_loads = (
+        pltpu.make_async_copy(late_pair_ref, late_pair, late_sem.at[0]),
+        pltpu.make_async_copy(late_down_ref, late_down, late_sem.at[1]),
+    )
+    for copy in late_loads:
+        copy.start()
     place.meet()
 
+    def late_total(c, k):
+        return late_down.at[c] if k == 2 else late_pair.at[c, k]
+
+    def late_landed(c, k, which):
+        return late_down_came.at[which, c] if k == 2 else late_pair_came.at[which, c, k]
+
+    def late_home(c, k, of):
+        chunks = down_grads_ref.shape[0] // 2 // WIDE
+        at_cols = tile(of * chunks + chunks - LATE + c, WIDE)
+        return down_grads_ref.at[at_cols, :] if k == 2 else pair_grads_ref.at[k, :, at_cols]
+
+    def late_add(c, k, which):
+        into, came_in = late_total(c, k), late_landed(c, k, which)
+        into[...] = (into[...].astype(F32) + came_in[...].astype(F32)).astype(BF16)
+
+    late = Chain(
+        place, LATE, 3, late_total, late_landed, late_home, late_add, chain_sems[18:]
+    )
     def slot(i):
         return pl.ds(i * rows, rows)
 
@@ -913,6 +985,9 @@
     grad = back_ref[...]
     in_send[0] = column(jnp.sum(grad * second_ref[...] * resid_ref[...], axis=1, keepdims=True))
     inner_copy(0).start()
+    for copy in late_loads:
+        copy.wait()
+    late.step(0, HOP)
     inv_two = inv_two_ref[:, :1]
     store_row(8, jnp.sum(back_ref[...] * resid_ref[...] * inv_two, axis=0, keepdims=True))
     inner_copy(0).wait()
@@ -936,6 +1011,7 @@
     )
     to_core.start()
     to_pair.start()
+    late.step(1, HOP)
 
     def dg_copy(n):
         at_cols = pl.ds(n * cols, cols)
@@ -952,6 +1028,7 @@
     dg_send[slot(1), :] = nt(branch[slot(1), :], wo[1]).astype(BF16)
     for n in range(halves_of):
         dg_copy(n).start()
+    late.step(2, HOP)
     for i in range(2):
         dg_own[slot(i), :] = nt(branch[slot(i), :], wo[0])
     dk[...] = jnp.zeros_like(dk)
@@ -1052,15 +1129,20 @@
         lambda c, k: misc,
         lambda c, k, which: misc_landed.at[which],
         lambda c, k, of: misc_home,
-        add_misc, chain_sems[9:], share=False,
-    )
-
+        add_misc, chain_sems[9:18], share=False,
+    )
+
+    left = 3 * LATE
     outs = pieces - 2 * parts
 
+    def step(u):
+        if u < late.steps(HOP):
+            late.step(u, HOP)
+        if u >= left:
+            chain.step(u - left, HOP)
+
     def out_piece(t):
-        at_cols = pl.ds(t * cols, cols)
-        total[t] = nn(gated_ref[...], branch[:, at_cols]).astype(BF16)
-        chain.step(t)
+        total[t] = nn(gated_ref[...], branch[:, pl.ds(t * cols, cols)]).astype(BF16)
 
     def block(j):
         over_y(j, True).wait_recv()
@@ -1071,50 +1153,58 @@
                 nn(turned_ref[at_rows, pl.ds(0, tokens)], first)
                 + nn(turned_ref[at_rows, pl.ds(tokens, tokens)], across[j])
             ).astype(BF16)
-            chain.step(outs + 2 * j + i)
-
+
+    def gates_copy():
+        return copy_to(gates, gates_came, s_send.at[2], s_recv.at[2], place.x_peer)
+
+    step(3)
     for n in range(kv_heads):
         dg_copy(n).wait_recv()
         head(2 * n)
-        if n == 0:
-            to_pair.wait_recv()
-            forward.start()
-        else:
-            take_chunk(2 * n - 2)
         head(2 * n + 1)
         key_value(n)
         send_chunk(2 * n)
         send_chunk(2 * n + 1)
         if n == 0:
-            forward.wait_recv()
-            for t in range(outs):
-                out_piece(t)
-        else:
-            take_chunk(2 * n - 1)
-            block(2 * n - 2)
-            block(2 * n - 1)
-
-    def gates_copy():
-        return copy_to(gates, gates_came, s_send.at[2], s_recv.at[2], place.x_peer)
-
+            to_pair.wait_recv()
+            forward.start()
+            step(4)
     gates_copy().start()
-    last = 2 * (kv_heads - 1)
-    acc[...] = nt(own[0], w_main[0])
-    for j in range(1, parts):
+
+    def back_own(j):
         acc[...] += nt(own[j], w_main[j])
-    for j in range(last):
-        acc[...] += nt(came[j], w_main[parts + j])
-    for j in range(last, parts):
+
+    def back_came(j):
         take_chunk(j)
         acc[...] += nt(came[j], w_main[parts + j])
+
+    step(5)
+    acc[...] = jnp.zeros_like(acc)
+    for j in range(parts):
+        back_own(j)
+    step(6)
+    back_came(0)
+    step(7)
+    back_came(1)
+    for u in range(8, left):
+        step(u)
+    forward.wait_recv()
+    for t in range(outs):
+        out_piece(t)
+        step(left + t)
+        if t + 2 < parts:
+            back_came(t + 2)
+    at = left + outs
+
     gates_copy().wait_recv()
     moved = pltpu.roll(gates_came[...].astype(F32), heads, axis=1)
-    both = gates[...].astype(F32) + moved
-    both = both.astype(BF16)
+    both = (gates[...].astype(F32) + moved).astype(BF16)
     acc[...] += nt(both, w_gates_ref[...])
     fold = copy_to(fold_src, fold_dst, s_send.at[3], s_recv.at[3], place.core_peer)
     fold_src[...] = acc[rows:, :].astype(BF16)
     fold.start()
+    block(0)
+    step(at)
     gate_grads = nn(turned_ref[:, pl.ds(0, tokens)], both).T
     for i in range(width // 128):
         misc[16 + 8 * i : 24 + 8 * i, :] = gate_grads[:8, i * 128 : (i + 1) * 128]
@@ -1123,7 +1213,6 @@
         return copy_to(misc, misc_came.at[n], s_send.at[4 + n], s_recv.at[4 + n], peer)
 
     row_of = lax.broadcasted_iota(jnp.int32, (MISC, 128), 0)
-    block(last)
     fold.wait_recv()
     grad = acc[:rows, :] + fold_dst[...].astype(F32)
     found = grad * hat_ref[...]
@@ -1132,33 +1221,45 @@
     acc[:rows, :] = grad
     store_row(0, jnp.sum(found, axis=0, keepdims=True))
     misc_copy(0, place.core_peer).start()
-    block(last + 1)
+    step(at + 1)
+    block(1)
+    step(at + 2)
     misc_copy(0, place.core_peer).wait()
     misc[...] += jnp.where((row_of < 16) | (row_of >= 80), misc_came[0], 0.0)
     misc_copy(1, place.x_peer).start()
-    chain.step(pieces)
+    step(at + 3)
+    block(2)
+    step(at + 4)
     misc_copy(1, place.x_peer).wait()
     misc[...] += jnp.where(row_of >= 80, misc_came[1], 0.0)
     misc_copy(2, place.y_peer).start()
     inner_copy(1).wait()
     inner = (in_send[1, :, :1] + in_came[1, :, :1]) / (2 * width)
     input_ref[...] += inv_one_ref[:, :1] * (acc[:rows, :] * norm_ref[...] - hat_ref[...] * inner)
-    chain.step(pieces + 1)
+    step(at + 5)
+    block(3)
     misc_copy(2, place.y_peer).wait()
     misc[...] += misc_came[2]
-
-    @pl.loop(pieces + 2, chain.steps())
+    small.step(0)
+    step(at + 6)
+    small.step(1)
+    step(at + 7)
+
+    @pl.loop(pieces, chain.steps(HOP))
     def _(u):
-        chain.step(u)
-        small.step(u - pieces - 2)
-
-    @pl.loop(chain.steps() - pieces - 2, small.steps())
+        if late.steps(HOP) > left + pieces:
+            late.step(u + left, HOP)
+        small.step(u - pieces + 2)
+        chain.step(u, HOP)
+
+    @pl.loop(chain.steps(HOP) - pieces + 2, small.steps())
     def _(u):
         small.step(u)
 
     small.drain()
     sums_ref[...] = misc_home[...]
     chain.drain()
+    late.drain()
     for copy in (to_core, to_pair, forward, gates_copy(), fold):
         copy.wait_send()
     for n in range(halves_of):
@@ -1171,7 +1272,7 @@
 def rear(
     back, resid, inv_two, ffn_gain, top, raw, sig, query, keys, values, log, attended, cos, sin,
     at, start, key_at, q_gain, k_gain, turned, gated, w_gates, hat, inv_one, norm_gain,
-    wq, wk, wv, wo,
+    wq, wk, wv, wo, late_pair, late_down, pair_sum, down_sum,
 ):
     count = lax.axis_size("group")
     rows, width = back.shape
@@ -1193,9 +1294,12 @@
             struct((2 * pieces, high, cols), BF16),
             struct((rows, width), F32),
             struct((MISC, 128), F32),
+            struct(pair_sum.shape, BF16),
+            struct(down_sum.shape, BF16),
         ),
-        in_specs=[local] * 25 + [anywhere] * 4,
-        out_specs=(anywhere, local, local),
+        in_specs=[local] * 25 + [anywhere] * 8,
+        out_specs=(anywhere, local, local, anywhere, anywhere),
+        input_output_aliases={31: 3, 32: 4},
         scratch_shapes=[
             pltpu.VMEM((2 * parts, width, cols), BF16),
             pltpu.VMEM((2, qw, width), BF16),
@@ -1221,9 +1325,13 @@
             pltpu.VMEM((rows, width), BF16),
             pltpu.VMEM((2, rows, 128), F32),
             pltpu.VMEM((2, rows, 128), F32),
-            dma((2, kv_heads, 4)), dma((3,)), dma((3,)), dma((heads // 2,)), dma((heads // 2,)),
+            pltpu.VMEM(late_pair.shape, BF16),
+            pltpu.VMEM(late_down.shape, BF16),
+            pltpu.VMEM((2,) + late_pair.shape, BF16),
+            pltpu.VMEM((2,) + late_down.shape, BF16),
+            dma((2, kv_heads, 4)), dma((2,)), dma((3,)), dma((3,)), dma((heads // 2,)), dma((heads // 2,)),
             dma((parts,)), dma((parts,)), dma((parts,)), dma((parts,)), dma((7,)), dma((7,)),
-            *chain_semaphores(pieces), *chain_semaphores(1),
+            *chain_semaphores(pieces), *chain_semaphores(1), *chain_semaphores(3 * LATE),
         ],
         compiler_params=pltpu.CompilerParams(
             collective_id=2, has_side_effects=True, vmem_limit_bytes=60 << 20
@@ -1235,7 +1343,7 @@
     )(
         back, resid, inv_two, ffn_gain, top, raw, sig, query, keys, values, log, attended, cos,
         sin, at, start, key_at, q_gain, k_gain, turned, gated, w_gates, hat, inv_one, norm_gain,
-        wq, wk, wv, wo,
+        wq, wk, wv, wo, late_pair, late_down, pair_sum, down_sum,
     )
 
 
@@ -1285,15 +1393,16 @@
         ]
     ).T
 
-    pair_sum, down_sum, _, _, branch, branch_out, d_normed_two = ffn(
+    pair_sum, down_sum, late_pair, late_down, _, _, branch, branch_out, d_normed_two = ffn(
         normed_two, grad_all, early_grad, w_gate, w_up, w_down
     )
     output = (resid + branch + swap_groups(branch_out).astype(F32)).astype(BF16)
 
-    grads, input_grad, sums = rear(
+    grads, input_grad, sums, pair_sum, down_sum = rear(
         d_normed_two, resid, inverse_two, ffn_gain[None], grad_out, raw, gate_sigmoid, query,
         keys, values, logsum, attended, cosines, signed, *positions, *gains, turned, gated_pair,
         w_gates, hat, inverse_one, norm_gain[None], w_query, w_key, w_value, w_out,
+        late_pair, late_down, pair_sum, down_sum,
     )
     grad_norm_gain = sums[:8].reshape(d_loc)
     grad_ffn_gain = sums[8:16].reshape(d_loc)

time: 686 us -> 656 us (0.956)
  Pallas kernels: 614 us -> 581 us
  local copies, waits for them, and re-layouts: 16.8 us -> 24.1 us
    pallas_call x1, Pallas kernels: 337 us -> 267 us  [ffn(): pl.pallas_call(functools.partial(ffn_kernel, count, chunks), out_shape=(j...]
    pallas_call x1, Pallas kernels: 164 us -> 201 us  [rear(): pl.pallas_call(functools.partial(rear_kernel, count, heads, kv_heads), ou...]
  transfers between devices with their start and end apart: 2 -> 2, of which waited for: 0 -> 0; matrix products, arithmetic and copies ran while one was open for 7% -> 7% of each run, Pallas kernels for 74% -> 72%
where the time goes in v5:
time: 656 us; the launch traced here: 646 us
  Pallas kernels  581 us (89%)
  other arithmetic  37.8 us (6%)
  local copies, waits for them, and re-layouts  24.1 us (4%)
    pallas_call x1, Pallas kernels, ffn(): pl.pallas_call(functools.partial(ffn_kernel, count, chunks), out_shape=(j...  267 us
    pallas_call x1, Pallas kernels, rear(): pl.pallas_call(functools.partial(rear_kernel, count, heads, kv_heads), ou...  201 us
    pallas_call x1, Pallas kernels, front(): pl.pallas_call(functools.partial(front_kernel, count, heads, kv_heads), o...  113 us
  transfers between devices with their start and end apart: 2, of which 0 were waited for; matrix products, arithmetic and copies ran while one was open for 7% of the time, Pallas kernels for 72%

profile of v5, /device:TPU:24, one launch (start us, length us, event | category | flops | bytes accessed | tf_op | source)
XLA Modules:
  0.0 645.8 jit_solution(17780503417988611582)
XLA Ops:
  3.4 1.2 fusion
  9.5 112.6 %shard_map.254 = (bf16[320,1024]{1,0:T(8,128)(2,1)}, f32[320,1024]{1,0:T(8,128)}, f32[320,128]{1,0:T(8,128)}, f32[320,1024]{1,0:T(8,128)}, f32[320,128]{1,0:T(8,...) custom-call(bf16[320,1024]{1,0:T(8,128)(2,1)} %tok_ref.1, ...), custom_call_target="tpu_custom_call" | custom-call | flops 12079595520 | bytes 41943040 | tf_op jit(solution)/shard_map/pallas_call | solution.py:843
  122.2 1.7 copy.48
  124.8 1.2 collective-permute-start.1
  126.0 266.8 %shard_map.255 = (bf16[2,1024,3072]{2,1,0:T(8,128)(2,1)}, bf16[3072,1024]{1,0:T(8,128)(2,1)}, bf16[3,2,1024,128]{3,2,1,0:T(8,128)(2,1)}, bf16[3,128,1024]{2,1,0:...) custom-call(bf16[320,1024]{1,0:T(8,128)(2,1)} %get-tuple-element.43., ...), custom_call_target="tpu_custom_call" | custom-call | flops 32212254720 | bytes 209715200 | tf_op jit(solution)/shard_map/pallas_call | solution.py:559
  393.5 4.4 copy.47
  397.9 2.2 maximum_bitcast_fusion.gated_ref
  400.2 201.2 %shard_map.256 = (bf16[24,512,256]{2,1,0:T(8,128)(2,1)}, f32[320,1024]{1,0:T(8,128)}, f32[88,128]{1,0:T(8,128)}, bf16[2,1024,3072]{2,1,0:T(8,128)(2,1)}, bf16[3072,1024]{1,0:T(8,128)(2,1)}) custom-call(f32[320,1024]{1,0:T(8,128)} %get-tuple-element.48.back_ref, ...), custom_call_target="tpu_custom_call", output_to_operand_aliasing={{3}: (31, {}), {4}: (32, {})} | custom-call | flops 8053063680 | bytes 104857600 | tf_op jit(solution)/shard_map/pallas_call | solution.py:1291
  601.3 1.7 slice_bitcast_fusion
  603.1 2.6 slice.106
  605.6 1.5 fusion.1
  607.1 1.2 fusion.2
  609.9 1.2 copy.52
  611.9 1.2 copy.53
  613.1 6.7 %convert_element_type.54 = f32[3072,1024]{1,0:T(8,128)} convert(bf16[3072,1024]{1,0:T(8,128)(2,1)S(1)} %bitcast.62) | non-fusion elementwise | flops 3145728 | bytes 18874368 | tf_op jit(solution)/shard_map/convert_element_type | solution.py:1443
  619.9 9.5 %bitcast_convert_fusion = (f32[1024,3072]{1,0:T(8,128)}, f32[1024,3072]{1,0:T(8,128)}) fusion(bf16[2,1024,3072]{2,1,0:T(8,128)(2,1)S(1)} %bitcast.60), kind=kLoop, calls=%fused_computation | loop fusion | flops 6291456 | bytes 37748736 | tf_op jit(solution)/shard_map/convert_element_type | solution.py:1442
  630.0 2.4 maximum_convert_fusion.1
  632.8 1.6 maximum_convert_fusion.2
  634.7 1.6 maximum_convert_fusion.3
  636.8 2.6 maximum_convert_fusion
  639.4 1.3 slice_bitcast_fusion.4
  640.7 1.3 slice_bitcast_fusion.2
  642.0 2.3 add_convert_fusion
  644.3 1.1 copy.57
  (76 shorter events, 13.4 us)
Async XLA Ops:
  124.8 273.1 %collective-permute-start.1 = (bf16[640,512]{0,1:T(8,128)(2,1)}, bf16[640,512]{0,1:T(8,128)(2,1)}, u32[]{:S(2)}, u32[]{:S(2)}) collective-permute-start(bf16[640,512]{0,1:T(8,128)(2,1)} %get-tuple-element.89), channel_id=1, source_target_pairs={{0,4},{4,0},{8,12},{12,8},{16,20},{20,16},{24,28},{28,24},{1,5},{5... | collective-permute-start | bytes 1966088 | tf_op jit(solution)/shard_map/ppermute | solution.py:20
  392.8 249.2 %collective-permute-start = (bf16[320,1024]{1,0:T(8,128)(2,1)}, bf16[320,1024]{1,0:T(8,128)(2,1)}, u32[]{:S(2)}, u32[]{:S(2)}) collective-permute-start(bf16[320,1024]{1,0:T(8,128)(2,1)} %get-tuple-element.47), channel_id=1, source_target_pairs={{0,4},{4,0},{8,12},{12,8},{16,20},{20,16},{24,28},{28,24},{1,5},{5... | collective-permute-start | bytes 1966088 | tf_op jit(solution)/shard_map/ppermute | solution.py:20
  605.6 2.7 copy-start.17
  607.1 6.0 slice-start.3
  608.9 4.2 slice-start.4
  611.1 8.7 %slice-start = ((s8[12582912]{0:T(1024)(128)(4,1)}), s8[4194304]{0:T(1024)(128)(4,1)S(1)}, s32[]{:S(2)}) async-start(s8[12582912]{0:T(1024)(128)(4,1)} %bitcast.59), calls=%async_computation | async-start | bytes 8388608
  613.1 6.7 %slice-start.1 = ((s8[12582912]{0:T(1024)(128)(4,1)}), s8[4194304]{0:T(1024)(128)(4,1)S(1)}, s32[]{:S(2)}) async-start(s8[12582912]{0:T(1024)(128)(4,1)} %bitcast.59), calls=%async_computation.1 | async-start | bytes 8388608
  613.1 6.7 %slice-start.2 = ((s8[12582912]{0:T(1024)(128)(4,1)}), s8[4194304]{0:T(1024)(128)(4,1)S(1)}, s32[]{:S(2)}) async-start(s8[12582912]{0:T(1024)(128)(4,1)} %bitcast.59), calls=%async_computation.2 | async-start | bytes 8388608
  619.8 9.5 %copy-start.16 = (f32[4,1024]{1,0:T(4,128)S(1)}, f32[4,1024]{1,0:T(4,128)}, u32[]{:S(2)}) copy-start(f32[4,1024]{1,0:T(4,128)} %get-tuple-element.99) | copy-start | bytes 49156
  619.8 10.2 %copy-start.1 = (bf16[64,8,4,256]{3,1,2,0:T(8,128)(2,1)S(1)}, bf16[64,8,4,256]{3,1,2,0:T(8,128)(2,1)}, u32[]{:S(2)}) copy-start(bf16[64,8,4,256]{3,1,2,0:T(8,128)(2,1)} %copy.52) | copy-start | bytes 3145732
  619.8 10.2 %copy-start.2 = (bf16[64,8,4,256]{3,1,2,0:T(8,128)(2,1)S(1)}, bf16[64,8,4,256]{3,1,2,0:T(8,128)(2,1)}, u32[]{:S(2)}) copy-start(bf16[64,8,4,256]{3,1,2,0:T(8,128)(2,1)} %copy.53) | copy-start | bytes 3145732
  630.0 2.5 copy-start.12
  630.0 2.5 copy-start.13
  630.0 2.5 copy-start.14
  630.0 2.5 copy-start.15
  632.7 1.7 copy-start.8
  632.7 1.6 copy-start.9
  632.8 1.6 copy-start.10
  634.7 1.6 copy-start.3
  634.7 1.6 copy-start.4
  634.7 1.7 copy-start.5
  636.8 5.2 copy-start
  636.8 5.2 copy-start.7
  639.4 4.9 copy-start.6
  (1 other events, 1.6 us)

commit v6 on v5

--- a/solution.py
+++ b/solution.py
@@ -611,6 +611,15 @@
     return 1.0 / (1.0 + jnp.exp(-v))
 
 
+def each_tile(start, count, size=160):
+    def run(step):
+        @pl.loop(0, count // size)
+        def _(i):
+            step(pl.ds(pl.multiple_of(start + i * size, 32), size))
+
+    return run
+
+
 def column(values):
     return jnp.broadcast_to(values, (values.shape[0], 128))
 
@@ -619,9 +628,9 @@
     count, heads, kv_heads, tok_ref, top_ref, norm_ref, second_ref, q_gain_ref, k_gain_ref,
     cos_ref, sin_ref, at_ref, start_ref, key_at_ref, w_gates_ref, wq_ref, wk_ref, wv_ref, wo_ref,
     wd_ref,
-    h_ref, resid_ref, inv_two_ref, hat_ref, inv_one_ref, normed_ref, tops_ref, early_ref,
+    h_ref, resid_ref, inv_two_ref, hat_ref, inv_one_ref, turned_ref, tops_ref, early_ref,
     raw_ref, sig_ref, q_ref, k_ref, v_ref, log_ref, attended_ref, gated_ref,
-    wq, wk, wv, wo, wd, kv_send, kv_came, q_send, q_came, gates, early_send, early_came,
+    normed_all, wq, wk, wv, wo, wd, kv_send, kv_came, q_send, q_came, gates, early_send, early_came,
     ss_send, ss_came, fold_src, fold_dst, acc,
     w_sem, n_send, n_recv, t_send, t_recv, p_send, p_recv, e_send, e_recv, g_send, g_recv,
     s_send, s_recv,
@@ -681,7 +690,10 @@
         )
 
     def early_start(i):
-        early_send[slot(i), :] = nt(tops_ref[slot(i), :], wd[...]).astype(BF16)
+        @each_tile(i * rows, rows)
+        def _(at_rows):
+            early_send[at_rows, :] = nt(tops_ref[at_rows, :], wd[...]).astype(BF16)
+
         early(i).start()
 
     loads[-1].wait()
@@ -691,8 +703,8 @@
     inv_one_ref[...] = inv_one
     hat = tok_ref[...].astype(F32) * inv_one[:, :1]
     hat_ref[...] = hat
-    normed_ref[slot(0), :] = (hat * norm_ref[...]).astype(BF16)
-    normed = spread(normed_ref, n_send, n_recv)
+    normed_all[slot(0), :] = (hat * norm_ref[...]).astype(BF16)
+    normed = spread(normed_all, n_send, n_recv)
     normed[0].start()
     normed[1].start()
 
@@ -703,22 +715,32 @@
     for i in range(2):
         if i == 1:
             normed[0].wait_recv()
-        rows_in = normed_ref[slot(i), :]
-        kv_send[slot(i), pl.ds(0, kw)] = nn(rows_in, wk[1]).astype(BF16)
-        kv_send[slot(i), pl.ds(kw, kw)] = nn(rows_in, wv[1]).astype(BF16)
+
+        @each_tile(i * rows, rows)
+        def _(at_rows):
+            rows_in = normed_all[at_rows, :]
+            kv_send[at_rows, pl.ds(0, kw)] = nn(rows_in, wk[1]).astype(BF16)
+            kv_send[at_rows, pl.ds(kw, kw)] = nn(rows_in, wv[1]).astype(BF16)
+
     kv_copy.start()
-    for i in range(2):
-        rows_in = normed_ref[slot(i), :]
-        q_send[slot(i), pl.ds(0, qw)] = nn(rows_in, wq[1]).astype(BF16)
+
+    @each_tile(0, tokens)
+    def _(at_rows):
+        rows_in = normed_all[at_rows, :]
+        q_send[at_rows, pl.ds(0, qw)] = nn(rows_in, wq[1]).astype(BF16)
         part = nn(rows_in, w_gates_ref[...])
-        gates[slot(i), :] = part
-        q_send[slot(i), pl.ds(qw, 128)] = part.astype(BF16)
+        gates[at_rows, :] = part
+        q_send[at_rows, pl.ds(qw, 128)] = part.astype(BF16)
+
     q_copy.start()
-    for i in range(2):
-        rows_in = normed_ref[slot(i), :]
-        raw_ref[slot(i), pl.ds(0, qw)] = nn(rows_in, wq[0])
-        raw_ref[slot(i), pl.ds(qw, kw)] = nn(rows_in, wk[0])
-        raw_ref[slot(i), pl.ds(qw + kw, kw)] = nn(rows_in, wv[0])
+
+    @each_tile(0, tokens)
+    def _(at_rows):
+        rows_in = normed_all[at_rows, :]
+        raw_ref[at_rows, pl.ds(0, qw)] = nn(rows_in, wq[0])
+        raw_ref[at_rows, pl.ds(qw, kw)] = nn(rows_in, wk[0])
+        raw_ref[at_rows, pl.ds(qw + kw, kw)] = nn(rows_in, wv[0])
+
 
     def turn(values, gain, at_rows):
         inverse = lax.rsqrt(jnp.mean(values * values, axis=1, keepdims=True) + EPS)
@@ -793,19 +815,38 @@
         if n == 2:
             early_start(3)
 
-    for i in (1, 0):
-        acc[slot(i), :] = nn(gated_ref[0, slot(i), :], wo[0])
+    @each_tile(0, tokens)
+    def _(at_rows):
+        acc[at_rows, :] = nn(gated_ref[0, at_rows, :], wo[0])
+
+    def turn_rows(first, last):
+        @pl.loop(first, last)
+        def _(i):
+            turned_ref[:, tile(i, ROWS)] = normed_all[tile(i, ROWS), :].T
+
+    turn_rows(0, tokens // ROWS)
     for n in range(heads):
         head_copy(n).wait_recv()
     fold = copy_to(fold_src, fold_dst, s_send.at[2], s_recv.at[2], place.core_peer)
-    fold_src[...] = (acc[slot(1), :] + nn(gated_ref[1, slot(1), :], wo[1])).astype(BF16)
+
+    @each_tile(0, rows)
+    def _(at_rows):
+        there = pl.ds(pl.multiple_of(at_rows.start + rows, 32), at_rows.size)
+        fold_src[at_rows, :] = (acc[there, :] + nn(gated_ref[1, there, :], wo[1])).astype(BF16)
+
     fold.start()
-    acc[slot(0), :] += nn(gated_ref[1, slot(0), :], wo[1])
+
+    @each_tile(0, rows)
+    def _(at_rows):
+        acc[at_rows, :] += nn(gated_ref[1, at_rows, :], wo[1])
+
+    normed[2].wait_recv()
     fold.wait_recv()
     resid = tok_ref[...].astype(F32) + acc[slot(0), :] + fold_dst[...].astype(F32)
     resid_ref[...] = resid
     ss_send[1] = column(jnp.sum(resid * resid, axis=1, keepdims=True))
     squares(1).start()
+    turn_rows(tokens // ROWS, 2 * tokens // ROWS)
     for i in range(4):
         early(i).wait_recv()
         early_ref[slot(i), :] = (
@@ -816,7 +857,6 @@
     inv_two_ref[...] = inv_two
     h_ref[...] = (resid_ref[...] * inv_two[:, :1] * second_ref[...]).astype(BF16)
 
-    normed[2].wait_recv()
     for copy in (*tops, *normed, kv_copy, q_copy, fold):
         copy.wait_send()
     for i in range(4):
@@ -848,7 +888,7 @@
             struct((rows, 128), F32),
             struct((rows, width), F32),
             struct((rows, 128), F32),
-            struct((4 * rows, width), BF16),
+            struct((width, 4 * rows), BF16),
             struct((4 * rows, width), BF16),
             struct((4 * rows, early), BF16),
             struct((tokens, qw + 2 * kw), F32),
@@ -863,6 +903,7 @@
         in_specs=[local] * 12 + [anywhere] * 5,
         out_specs=(local,) * 16,
         scratch_shapes=[
+            pltpu.VMEM((4 * rows, width), BF16),
             pltpu.VMEM((2, width, qw), BF16),
             pltpu.VMEM((2, width, kw), BF16),
             pltpu.VMEM((2, width, kw), BF16),
@@ -909,7 +950,7 @@
     key_at_ref, q_gain_ref, k_gain_ref, turned_ref, gated_ref, w_gates_ref, hat_ref, inv_one_ref,
     norm_ref, wq_ref, wk_ref, wv_ref, wo_ref, late_pair_ref, late_down_ref, pair_in, down_in,
     grads_ref, input_ref, sums_ref, pair_grads_ref, down_grads_ref,
-    w_main, wo, branch, dg_own, dg_send, dg_came, dk, dv, gates, gates_came, own, came, across,
+    w_main, wo, branch, block_src, dg_own, dg_send, dg_came, dk, dv, gates, gates_came, own, came, across,
     total, landed, misc, misc_came, misc_landed, misc_home, acc, fold_src, fold_dst, in_send,
     in_came, late_pair, late_down, late_pair_came, late_down_came,
     w_sem, late_sem, b_send, b_recv, d_send, d_recv, x_send, x_recv, y_send, y_recv, s_send, s_recv,
@@ -1023,14 +1064,22 @@
     for copy in loads:
         copy.wait()
     halves_of = heads // 2
-    dg_send[slot(0), :] = nt(branch[slot(0), :], wo[1]).astype(BF16)
-    to_core.wait_recv()
-    dg_send[slot(1), :] = nt(branch[slot(1), :], wo[1]).astype(BF16)
+    for i in range(2):
+        if i == 1:
+            to_core.wait_recv()
+
+        @each_tile(i * rows, rows)
+        def _(at_rows):
+            dg_send[at_rows, :] = nt(branch[at_rows, :], wo[1]).astype(BF16)
+
     for n in range(halves_of):
         dg_copy(n).start()
     late.step(2, HOP)
-    for i in range(2):
-        dg_own[slot(i), :] = nt(branch[slot(i), :], wo[0])
+
+    @each_tile(0, tokens)
+    def _(at_rows):
+        dg_own[at_rows, :] = nt(branch[at_rows, :], wo[0])
+
     dk[...] = jnp.zeros_like(dk)
     dv[...] = jnp.zeros_like(dv)
     gates[...] = jnp.zeros_like(gates)
@@ -1146,13 +1195,16 @@
 
     def block(j):
         over_y(j, True).wait_recv()
-        first = jnp.where(side == 0, own[j], came[j])
+        block_src[...] = jnp.where(side == 0, own[j], came[j])
         for i in range(2):
-            at_rows = pl.ds(i * high, high)
-            total[outs + 2 * j + i] = (
-                nn(turned_ref[at_rows, pl.ds(0, tokens)], first)
-                + nn(turned_ref[at_rows, pl.ds(tokens, tokens)], across[j])
-            ).astype(BF16)
+
+            @each_tile(0, high, TILE)
+            def _(at_rows):
+                there = pl.ds(pl.multiple_of(at_rows.start + i * high, TILE), at_rows.size)
+                total[outs + 2 * j + i, at_rows, :] = (
+                    nn(turned_ref[there, pl.ds(0, tokens)], block_src[...])
+                    + nn(turned_ref[there, pl.ds(tokens, tokens)], across[j])
+                ).astype(BF16)
 
     def gates_copy():
         return copy_to(gates, gates_came, s_send.at[2], s_recv.at[2], place.x_peer)
@@ -1171,17 +1223,23 @@
             step(4)
     gates_copy().start()
 
-    def back_own(j):
-        acc[...] += nt(own[j], w_main[j])
-
     def back_came(j):
         take_chunk(j)
-        acc[...] += nt(came[j], w_main[parts + j])
+
+        @each_tile(0, tokens)
+        def _(at_rows):
+            acc[at_rows, :] += nt(came[j, at_rows, :], w_main[parts + j])
+
 
     step(5)
-    acc[...] = jnp.zeros_like(acc)
-    for j in range(parts):
-        back_own(j)
+
+    @each_tile(0, tokens)
+    def _(at_rows):
+        found = nt(own[0, at_rows, :], w_main[0])
+        for j in range(1, parts):
+            found += nt(own[j, at_rows, :], w_main[j])
+        acc[at_rows, :] = found
+
     step(6)
     back_came(0)
     step(7)
@@ -1196,10 +1254,15 @@
             back_came(t + 2)
     at = left + outs
 
-    gates_copy().wait_recv()
+    gates_copy().wait()
     moved = pltpu.roll(gates_came[...].astype(F32), heads, axis=1)
     both = (gates[...].astype(F32) + moved).astype(BF16)
-    acc[...] += nt(both, w_gates_ref[...])
+    gates[...] = both
+
+    @each_tile(0, tokens)
+    def _(at_rows):
+        acc[at_rows, :] += nt(gates[at_rows, :], w_gates_ref[...])
+
     fold = copy_to(fold_src, fold_dst, s_send.at[3], s_recv.at[3], place.core_peer)
     fold_src[...] = acc[rows:, :].astype(BF16)
     fold.start()
@@ -1260,7 +1323,7 @@
     sums_ref[...] = misc_home[...]
     chain.drain()
     late.drain()
-    for copy in (to_core, to_pair, forward, gates_copy(), fold):
+    for copy in (to_core, to_pair, forward, fold):
         copy.wait_send()
     for n in range(halves_of):
         dg_copy(n).wait_send()
@@ -1304,6 +1367,7 @@
             pltpu.VMEM((2 * parts, width, cols), BF16),
             pltpu.VMEM((2, qw, width), BF16),
             pltpu.VMEM((4 * rows, width), BF16),
+            pltpu.VMEM((tokens, cols), BF16),
             pltpu.VMEM((tokens, qw), F32),
             pltpu.VMEM((tokens, qw), BF16),
             pltpu.VMEM((tokens, qw), BF16),
@@ -1347,6 +1411,58 @@
     )
 
 
+def assemble_kernel(parts, outs, grads_ref, q_ref, k_ref, v_ref, o_ref, wide, sems):
+    row_at = lax.axis_index("row")
+    pieces = outs + 2 * parts
+    high = grads_ref.shape[1]
+    copies = []
+
+    def move(src, dst):
+        copies.append(pltpu.make_async_copy(src, dst, sems.at[len(copies)]))
+        copies[-1].start()
+
+    for s in range(2):
+        at = row_at if s == 0 else 1 - row_at
+        for p in range(pieces):
+            n = s * pieces + p
+            wide[n] = grads_ref[n].astype(F32)
+            if p < outs:
+                rows, cols = tile(at, high), pl.ds(p * 256, 256)
+                move(wide.at[n], o_ref.at[rows, cols])
+            else:
+                j, i = (p - outs) // 2, (p - outs) % 2
+                rows, head = pl.ds(i * high, high), at * (parts // 2) + j // 2
+                if j % 2 == 0:
+                    move(wide.at[n], q_ref.at[rows, tile(head, 256)])
+                else:
+                    for m, ref in enumerate((k_ref, v_ref)):
+                        half = wide.at[n, :, pl.ds(m * 128, 128)]
+                        move(half, ref.at[rows, tile(head, 128)])
+    for copy in copies:
+        copy.wait()
+
+
+def assemble(grads, q_shape, k_shape, o_shape, head_dim):
+    parts = q_shape[1] // 2 // head_dim // 2 + k_shape[1] // 2 // head_dim
+    outs = grads.shape[0] // 2 - 2 * parts
+    anywhere = pl.BlockSpec(memory_space=pl.ANY)
+    struct = jax.ShapeDtypeStruct
+    count = 2 * (outs + 3 * parts)
+    return pl.pallas_call(
+        functools.partial(assemble_kernel, parts, outs),
+        out_shape=(
+            struct(q_shape, F32), struct(k_shape, F32), struct(k_shape, F32), struct(o_shape, F32),
+        ),
+        in_specs=[pl.BlockSpec(memory_space=pltpu.VMEM)],
+        out_specs=(anywhere,) * 4,
+        scratch_shapes=[
+            pltpu.VMEM(grads.shape, F32),
+            pltpu.SemaphoreType.DMA((count,)),
+        ],
+        compiler_params=pltpu.CompilerParams(vmem_limit_bytes=40 << 20),
+    )(grads)
+
+
 def body(
     tokens, lengths, norm_gain, w_query, w_key, w_value, w_head_gate, query_gain, key_gain,
     w_out, ffn_gain, w_gate, w_up, w_down, grad_out,
@@ -1354,8 +1470,6 @@
     rows, d_loc = tokens.shape
     group_tok = 2 * rows
     head_dim = query_gain.shape[0]
-    q_half = w_query.shape[1] // 2
-    kv_half = w_key.shape[1] // 2
     gate_half = w_head_gate.shape[1] // 2
     row_at = lax.axis_index("row")
     col_at = lax.axis_index("col")
@@ -1377,13 +1491,12 @@
     )
     gains = (query_gain[None], key_gain[None])
     (
-        normed_two, resid, inverse_two, hat, inverse_one, permuted_pair, grad_all, early_grad,
+        normed_two, resid, inverse_two, hat, inverse_one, turned, grad_all, early_grad,
         raw, gate_sigmoid, query, keys, values, logsum, attended, gated_both,
     ) = front(
         tokens, grad_out, norm_gain[None], ffn_gain[None], *gains, cosines, signed, *positions,
         w_gates, w_query, w_key, w_value, w_out, w_down,
     )
-    turned = permuted_pair.T
     gated, gated_came = gated_both[0], gated_both[1]
     first_side = side == 0
     gated_pair = jnp.concatenate(
@@ -1410,33 +1523,20 @@
     grad_gates = grad_gates.reshape(2 * gate_half, d_loc)
     grad_head_gate = ordered(grad_gates[:gate_half], grad_gates[gate_half:], 0, row_at).T
 
-    grads = grads.reshape(2, -1, q_half, 256)
-    count = d_loc // 256
-    out_sum = grads[:, :count].transpose(0, 2, 1, 3).reshape(2 * q_half, d_loc)
-    grad_out_full = ordered(*jnp.split(out_sum, 2, axis=0), 0, row_at).astype(F32)
-    chunks = grads[:, count:].reshape(2, kv_half // head_dim, 2, 2, q_half, 256)
-
-    def collect(at, start, size):
-        def side_of(n):
-            pieces = [
-                chunks[n, i, at, :, :, start : start + size].reshape(d_loc, size)
-                for i in range(chunks.shape[1])
-            ]
-            return jnp.concatenate(pieces, axis=1)
-
-        return ordered(side_of(0), side_of(1), 1, row_at).astype(F32)
-
+    grad_query, grad_key, grad_value, grad_out_w = assemble(
+        grads, w_query.shape, w_key.shape, w_out.shape, head_dim
+    )
     return (
         output,
         input_grad,
         grad_norm_gain,
-        collect(0, 0, 256),
-        collect(1, 0, 128),
-        collect(1, 128, 128),
+        grad_query,
+        grad_key,
+        grad_value,
         grad_head_gate,
         sums[80],
         sums[81],
-        grad_out_full,
+        grad_out_w,
         grad_ffn_gain,
         pair_sum[0].astype(F32),
         pair_sum[1].astype(F32),

time: 656 us -> 643 us (0.980)
  local copies, waits for them, and re-layouts: 24.1 us -> 9.37 us
  Pallas kernels: 581 us -> 589 us
    convert_element_type x4 -> x0, other arithmetic: 8.26 us -> none  [the longest x3 5.81 us: collect(): return ordered(side_of(0), side_of(1), 1, row_at).astype(F32)]
  transfers between devices with their start and end apart: 2 -> 2, of which waited for: 0 -> 0; matrix products, arithmetic and copies ran while one was open for 7% -> 4% of each run, Pallas kernels for 72% -> 75%
where the time goes in v6:
time: 643 us; the launch traced here: 635 us
  Pallas kernels  589 us (92%)
  other arithmetic  32.8 us (5%)
  local copies, waits for them, and re-layouts  9.37 us (1%)
    pallas_call x1, Pallas kernels, ffn(): pl.pallas_call(functools.partial(ffn_kernel, count, chunks), out_shape=(j...  266 us
    pallas_call x1, Pallas kernels, rear(): pl.pallas_call(functools.partial(rear_kernel, count, heads, kv_heads), ou...  204 us
    pallas_call x1, Pallas kernels, front(): pl.pallas_call(functools.partial(front_kernel, count, heads, kv_heads), o...  114 us
    convert_element_type x1, other arithmetic, body(): pair_sum[1].astype(F32)  15.9 us
  transfers between devices with their start and end apart: 2, of which 0 were waited for; matrix products, arithmetic and copies ran while one was open for 4% of the time, Pallas kernels for 75%

profile of v6, /device:TPU:24, one launch (start us, length us, event | category | flops | bytes accessed | tf_op | source)
XLA Modules:
  0.0 635.1 jit_solution(8296194498805895631)
XLA Ops:
  0.7 0.8 reduce-window.8
  2.4 0.8 broadcast_select_fusion.1
  3.4 1.2 fusion
  4.7 0.9 pad_maximum_fusion.cos_ref
  5.5 0.8 pad.4.w_gates_ref
  6.3 0.9 pad_maximum_fusion.1.sin_ref
  7.8 0.9 broadcast_in_dim.18.at_ref
  8.7 0.9 broadcast_in_dim.19.start_ref
  9.5 113.9 %shard_map.254 = (bf16[320,1024]{1,0:T(8,128)(2,1)}, f32[320,1024]{1,0:T(8,128)}, f32[320,128]{1,0:T(8,128)}, f32[320,1024]{1,0:T(8,128)}, f32[320,128]{1,0:T(8,...) custom-call(bf16[320,1024]{1,0:T(8,128)(2,1)} %tok_ref.1, ...), custom_call_target="tpu_custom_call" | custom-call | flops 12079595520 | bytes 41943040 | tf_op jit(solution)/shard_map/pallas_call | solution.py:883
  123.4 1.7 copy.41
  125.1 1.0 select_bitcast_fusion.1
  126.1 0.8 collective-permute-start.1
  126.9 265.8 %shard_map.255 = (bf16[2,1024,3072]{2,1,0:T(8,128)(2,1)}, bf16[3072,1024]{1,0:T(8,128)(2,1)}, bf16[3,2,1024,128]{3,2,1,0:T(8,128)(2,1)}, bf16[3,128,1024]{2,1,0:...) custom-call(bf16[320,1024]{1,0:T(8,128)(2,1)} %get-tuple-element.47., ...), custom_call_target="tpu_custom_call" | custom-call | flops 32212254720 | bytes 209715200 | tf_op jit(solution)/shard_map/pallas_call | solution.py:559
  392.7 1.9 collective-permute-start
  394.6 2.2 maximum_bitcast_fusion.gated_ref
  396.9 204.2 %shard_map.256 = (bf16[24,512,256]{2,1,0:T(8,128)(2,1)}, f32[320,1024]{1,0:T(8,128)}, f32[88,128]{1,0:T(8,128)}, bf16[2,1024,3072]{2,1,0:T(8,128)(2,1)}, bf16[3072,1024]{1,0:T(8,128)(2,1)}) custom-call(f32[320,1024]{1,0:T(8,128)} %get-tuple-element.52.back_ref, ...), custom_call_target="tpu_custom_call", output_to_operand_aliasing={{3}: (31, {}), {4}: (32, {})} | custom-call | flops 8053063680 | bytes 104857600 | tf_op jit(solution)/shard_map/pallas_call | solution.py:1354
  601.1 0.8 slice_bitcast_fusion
  601.9 15.9 %bitcast_convert_fusion = (f32[1024,3072]{1,0:T(8,128)}, f32[1024,3072]{1,0:T(8,128)}) fusion(bf16[2,1024,3072]{2,1,0:T(8,128)(2,1)} %get-tuple-element.76), kind=kLoop, calls=%fused_computation | loop fusion | flops 6291456 | bytes 37748736 | tf_op jit(solution)/shard_map/convert_element_type | solution.py:1542
  617.8 6.4 %convert_element_type.38 = f32[3072,1024]{1,0:T(8,128)} convert(bf16[3072,1024]{1,0:T(8,128)(2,1)S(1)} %bitcast.37) | non-fusion elementwise | flops 3145728 | bytes 18874368 | tf_op jit(solution)/shard_map/convert_element_type | solution.py:1543
  624.1 5.1 shard_map.257
  629.9 1.3 slice_bitcast_fusion.3
  631.2 1.3 slice_bitcast_fusion.1
  632.5 1.2 add_convert_fusion
  633.6 1.1 copy.46
  (25 shorter events, 2.4 us)
Async XLA Ops:
  126.1 268.5 %collective-permute-start.1 = (bf16[640,512]{0,1:T(8,128)(2,1)}, bf16[640,512]{0,1:T(8,128)(2,1)}, u32[]{:S(2)}, u32[]{:S(2)}) collective-permute-start(bf16[640,512]{0,1:T(8,128)(2,1)} %get-tuple-element.81), channel_id=1, source_target_pairs={{0,4},{4,0},{8,12},{12,8},{16,20},{20,16},{24,28},{28,24},{1,5},{5... | collective-permute-start | bytes 1966088 | tf_op jit(solution)/shard_map/ppermute | solution.py:20
  392.7 239.8 %collective-permute-start = (bf16[320,1024]{1,0:T(8,128)(2,1)}, bf16[320,1024]{1,0:T(8,128)(2,1)S(1)}, u32[]{:S(2)}, u32[]{:S(2)}) collective-permute-start(bf16[320,1024]{1,0:T(8,128)(2,1)} %get-tuple-element.51), channel_id=1, source_target_pairs={{0,4},{4,0},{8,12},{12,8},{16,20},{20,16},{24,28},{28,24},{1,5},{5... | collective-permute-start | bytes 1966088 | tf_op jit(solution)/shard_map/ppermute | solution.py:20
  601.9 15.9 %slice-start = ((s8[6291456]{0:T(1024)(128)(4,1)}), s8[4194304]{0:T(1024)(128)(4,1)S(1)}, s32[]{:S(2)}) async-start(s8[6291456]{0:T(1024)(128)(4,1)} %bitcast.36), calls=%async_computation | async-start | bytes 8388608
  601.9 15.9 %slice-start.1 = ((s8[6291456]{0:T(1024)(128)(4,1)}), s8[2097152]{0:T(1024)(128)(4,1)S(1)}, s32[]{:S(2)}) async-start(s8[6291456]{0:T(1024)(128)(4,1)} %bitcast.36), calls=%async_computation.1 | async-start | bytes 4194304
  617.8 6.4 %copy-start = (bf16[24,512,256]{2,1,0:T(8,128)(2,1)S(1)}, bf16[24,512,256]{2,1,0:T(8,128)(2,1)}, u32[]{:S(2)}) copy-start(bf16[24,512,256]{2,1,0:T(8,128)(2,1)} %get-tuple-element.71.grads_ref) | copy-start | bytes 18874372
  624.1 8.3 %copy-start.1 = (f32[320,1024]{1,0:T(8,128)S(1)}, f32[320,1024]{1,0:T(8,128)}, u32[]{:S(2)}) copy-start(f32[320,1024]{1,0:T(8,128)} %get-tuple-element.46.resid_ref) | copy-start | bytes 3932164
  624.1 8.3 %copy-start.3 = (f32[320,1024]{1,0:T(8,128)S(1)}, f32[320,1024]{1,0:T(8,128)}, u32[]{:S(2)}) copy-start(f32[320,1024]{1,0:T(8,128)} %get-tuple-element.50) | copy-start | bytes 3932164
  629.3 4.4 copy-start.2

commit v7 on v6

--- a/solution.py
+++ b/solution.py
@@ -1028,7 +1028,7 @@
     inner_copy(0).start()
     for copy in late_loads:
         copy.wait()
-    late.step(0, HOP)
+    late.step(0, 1)
     inv_two = inv_two_ref[:, :1]
     store_row(8, jnp.sum(back_ref[...] * resid_ref[...] * inv_two, axis=0, keepdims=True))
     inner_copy(0).wait()
@@ -1052,7 +1052,7 @@
     )
     to_core.start()
     to_pair.start()
-    late.step(1, HOP)
+    late.step(1, 1)
 
     def dg_copy(n):
         at_cols = pl.ds(n * cols, cols)
@@ -1074,7 +1074,7 @@
 
     for n in range(halves_of):
         dg_copy(n).start()
-    late.step(2, HOP)
+    late.step(2, 1)
 
     @each_tile(0, tokens)
     def _(at_rows):
@@ -1185,10 +1185,10 @@
     outs = pieces - 2 * parts
 
     def step(u):
-        if u < late.steps(HOP):
-            late.step(u, HOP)
+        if u < late.steps(1):
+            late.step(u, 1)
         if u >= left:
-            chain.step(u - left, HOP)
+            chain.step(u - left, 1)
 
     def out_piece(t):
         total[t] = nn(gated_ref[...], branch[:, pl.ds(t * cols, cols)]).astype(BF16)
@@ -1308,14 +1308,14 @@
     small.step(1)
     step(at + 7)
 
-    @pl.loop(pieces, chain.steps(HOP))
+    @pl.loop(pieces, chain.steps(1))
     def _(u):
-        if late.steps(HOP) > left + pieces:
-            late.step(u + left, HOP)
+        if late.steps(1) > left + pieces:
+            late.step(u + left, 1)
         small.step(u - pieces + 2)
-        chain.step(u, HOP)
-
-    @pl.loop(chain.steps(HOP) - pieces + 2, small.steps())
+        chain.step(u, 1)
+
+    @pl.loop(chain.steps(1) - pieces + 2, small.steps())
     def _(u):
         small.step(u)
 

time: 643 us -> 634 us (0.986)
  Pallas kernels: 589 us -> 580 us
    pallas_call x1, Pallas kernels: 204 us -> 195 us  [rear(): pl.pallas_call(functools.partial(rear_kernel, count, heads, kv_heads), ou...]
  transfers between devices with their start and end apart: 2 -> 2, of which waited for: 0 -> 0; matrix products, arithmetic and copies ran while one was open for 4% -> 5% of each run, Pallas kernels for 75% -> 74%
where the time goes in v7:
time: 634 us; the launch traced here: 626 us
  Pallas kernels  580 us (91%)
  other arithmetic  32.8 us (5%)
  local copies, waits for them, and re-layouts  9.37 us (1%)
    pallas_call x1, Pallas kernels, ffn(): pl.pallas_call(functools.partial(ffn_kernel, count, chunks), out_shape=(j...  266 us
    pallas_call x1, Pallas kernels, rear(): pl.pallas_call(functools.partial(rear_kernel, count, heads, kv_heads), ou...  195 us
    pallas_call x1, Pallas kernels, front(): pl.pallas_call(functools.partial(front_kernel, count, heads, kv_heads), o...  114 us
    convert_element_type x1, other arithmetic, body(): pair_sum[1].astype(F32)  15.9 us
  transfers between devices with their start and end apart: 2, of which 0 were waited for; matrix products, arithmetic and copies ran while one was open for 5% of the time, Pallas kernels for 74%

profile of v7, /device:TPU:24, one launch (start us, length us, event | category | flops | bytes accessed | tf_op | source)
XLA Modules:
  0.0 625.8 jit_solution(5234668376054147264)
XLA Ops:
  0.7 0.8 reduce-window.8
  2.4 0.8 broadcast_select_fusion.1
  3.4 1.2 fusion
  4.7 0.9 pad_maximum_fusion.cos_ref
  5.5 0.8 pad.4.w_gates_ref
  6.3 0.9 pad_maximum_fusion.1.sin_ref
  7.8 0.9 broadcast_in_dim.18.at_ref
  8.7 0.9 broadcast_in_dim.19.start_ref
  9.5 113.9 %shard_map.254 = (bf16[320,1024]{1,0:T(8,128)(2,1)}, f32[320,1024]{1,0:T(8,128)}, f32[320,128]{1,0:T(8,128)}, f32[320,1024]{1,0:T(8,128)}, f32[320,128]{1,0:T(8,...) custom-call(bf16[320,1024]{1,0:T(8,128)(2,1)} %tok_ref.1, ...), custom_call_target="tpu_custom_call" | custom-call | flops 12079595520 | bytes 41943040 | tf_op jit(solution)/shard_map/pallas_call | solution.py:883
  123.4 1.7 copy.41
  125.1 1.0 select_bitcast_fusion.1
  126.1 0.8 collective-permute-start.1
  126.9 265.8 %shard_map.255 = (bf16[2,1024,3072]{2,1,0:T(8,128)(2,1)}, bf16[3072,1024]{1,0:T(8,128)(2,1)}, bf16[3,2,1024,128]{3,2,1,0:T(8,128)(2,1)}, bf16[3,128,1024]{2,1,0:...) custom-call(bf16[320,1024]{1,0:T(8,128)(2,1)} %get-tuple-element.47., ...), custom_call_target="tpu_custom_call" | custom-call | flops 32212254720 | bytes 209715200 | tf_op jit(solution)/shard_map/pallas_call | solution.py:559
  392.7 1.9 collective-permute-start
  394.6 2.2 maximum_bitcast_fusion.gated_ref
  396.9 194.9 %shard_map.256 = (bf16[24,512,256]{2,1,0:T(8,128)(2,1)}, f32[320,1024]{1,0:T(8,128)}, f32[88,128]{1,0:T(8,128)}, bf16[2,1024,3072]{2,1,0:T(8,128)(2,1)}, bf16[3072,1024]{1,0:T(8,128)(2,1)}) custom-call(f32[320,1024]{1,0:T(8,128)} %get-tuple-element.52.back_ref, ...), custom_call_target="tpu_custom_call", output_to_operand_aliasing={{3}: (31, {}), {4}: (32, {})} | custom-call | flops 8053063680 | bytes 104857600 | tf_op jit(solution)/shard_map/pallas_call | solution.py:1354
  591.7 0.8 slice_bitcast_fusion
  592.5 15.9 %bitcast_convert_fusion = (f32[1024,3072]{1,0:T(8,128)}, f32[1024,3072]{1,0:T(8,128)}) fusion(bf16[2,1024,3072]{2,1,0:T(8,128)(2,1)} %get-tuple-element.76), kind=kLoop, calls=%fused_computation | loop fusion | flops 6291456 | bytes 37748736 | tf_op jit(solution)/shard_map/convert_element_type | solution.py:1542
  608.4 6.4 %convert_element_type.38 = f32[3072,1024]{1,0:T(8,128)} convert(bf16[3072,1024]{1,0:T(8,128)(2,1)S(1)} %bitcast.37) | non-fusion elementwise | flops 3145728 | bytes 18874368 | tf_op jit(solution)/shard_map/convert_element_type | solution.py:1543
  614.8 5.1 shard_map.257
  620.5 1.3 slice_bitcast_fusion.3
  621.8 1.3 slice_bitcast_fusion.1
  623.1 1.2 add_convert_fusion
  624.3 1.1 copy.46
  (25 shorter events, 2.4 us)
Async XLA Ops:
  126.1 268.5 %collective-permute-start.1 = (bf16[640,512]{0,1:T(8,128)(2,1)}, bf16[640,512]{0,1:T(8,128)(2,1)}, u32[]{:S(2)}, u32[]{:S(2)}) collective-permute-start(bf16[640,512]{0,1:T(8,128)(2,1)} %get-tuple-element.81), channel_id=1, source_target_pairs={{0,4},{4,0},{8,12},{12,8},{16,20},{20,16},{24,28},{28,24},{1,5},{5... | collective-permute-start | bytes 1966088 | tf_op jit(solution)/shard_map/ppermute | solution.py:20
  392.7 230.4 %collective-permute-start = (bf16[320,1024]{1,0:T(8,128)(2,1)}, bf16[320,1024]{1,0:T(8,128)(2,1)S(1)}, u32[]{:S(2)}, u32[]{:S(2)}) collective-permute-start(bf16[320,1024]{1,0:T(8,128)(2,1)} %get-tuple-element.51), channel_id=1, source_target_pairs={{0,4},{4,0},{8,12},{12,8},{16,20},{20,16},{24,28},{28,24},{1,5},{5... | collective-permute-start | bytes 1966088 | tf_op jit(solution)/shard_map/ppermute | solution.py:20
  592.5 15.9 %slice-start = ((s8[6291456]{0:T(1024)(128)(4,1)}), s8[4194304]{0:T(1024)(128)(4,1)S(1)}, s32[]{:S(2)}) async-start(s8[6291456]{0:T(1024)(128)(4,1)} %bitcast.36), calls=%async_computation | async-start | bytes 8388608
  592.5 15.9 %slice-start.1 = ((s8[6291456]{0:T(1024)(128)(4,1)}), s8[2097152]{0:T(1024)(128)(4,1)S(1)}, s32[]{:S(2)}) async-start(s8[6291456]{0:T(1024)(128)(4,1)} %bitcast.36), calls=%async_computation.1 | async-start | bytes 4194304
  608.4 6.4 %copy-start = (bf16[24,512,256]{2,1,0:T(8,128)(2,1)S(1)}, bf16[24,512,256]{2,1,0:T(8,128)(2,1)}, u32[]{:S(2)}) copy-start(bf16[24,512,256]{2,1,0:T(8,128)(2,1)} %get-tuple-element.71.grads_ref) | copy-start | bytes 18874372
  614.8 8.3 %copy-start.1 = (f32[320,1024]{1,0:T(8,128)S(1)}, f32[320,1024]{1,0:T(8,128)}, u32[]{:S(2)}) copy-start(f32[320,1024]{1,0:T(8,128)} %get-tuple-element.46.resid_ref) | copy-start | bytes 3932164
  614.8 8.3 %copy-start.3 = (f32[320,1024]{1,0:T(8,128)S(1)}, f32[320,1024]{1,0:T(8,128)}, u32[]{:S(2)}) copy-start(f32[320,1024]{1,0:T(8,128)} %get-tuple-element.50) | copy-start | bytes 3932164
  619.9 4.4 copy-start.2

commit v8 on v7

--- a/solution.py
+++ b/solution.py
@@ -809,11 +809,6 @@
             gated_ref[0, at_rows, cols] = (result * sig_ref[at_rows, n : n + 1]).astype(BF16)
 
         head_copy(n).start()
-        if n == 0:
-            tops[2].wait_recv()
-            early_start(2)
-        if n == 2:
-            early_start(3)
 
     @each_tile(0, tokens)
     def _(at_rows):
@@ -835,6 +830,9 @@
         fold_src[at_rows, :] = (acc[there, :] + nn(gated_ref[1, there, :], wo[1])).astype(BF16)
 
     fold.start()
+    tops[2].wait_recv()
+    early_start(2)
+    early_start(3)
 
     @each_tile(0, rows)
     def _(at_rows):

time: 634 us -> 631 us (level)
  no operation moved by 1% of the time
where the time goes in v8:
time: 631 us; the launch traced here: 622 us
  Pallas kernels  577 us (91%)
  other arithmetic  32.8 us (5%)
  local copies, waits for them, and re-layouts  9.37 us (1%)
    pallas_call x1, Pallas kernels, ffn(): pl.pallas_call(functools.partial(ffn_kernel, count, chunks), out_shape=(j...  265 us
    pallas_call x1, Pallas kernels, rear(): pl.pallas_call(functools.partial(rear_kernel, count, heads, kv_heads), ou...  193 us
    pallas_call x1, Pallas kernels, front(): pl.pallas_call(functools.partial(front_kernel, count, heads, kv_heads), o...  113 us
    convert_element_type x1, other arithmetic, body(): pair_sum[1].astype(F32)  15.9 us
  transfers between devices with their start and end apart: 2, of which 0 were waited for; matrix products, arithmetic and copies ran while one was open for 5% of the time, Pallas kernels for 74%

profile of v8, /device:TPU:24, one launch (start us, length us, event | category | flops | bytes accessed | tf_op | source)
XLA Modules:
  0.0 622.4 jit_solution(15436825032011443566)
XLA Ops:
  0.7 0.8 reduce-window.8
  1.6 0.7 select_reduce_fusion
  2.4 0.8 broadcast_select_fusion.1
  3.4 1.2 fusion
  4.7 0.9 pad_maximum_fusion.cos_ref
  5.5 0.8 pad.4.w_gates_ref
  6.3 0.9 pad_maximum_fusion.1.sin_ref
  7.8 0.9 broadcast_in_dim.18.at_ref
  8.7 0.9 broadcast_in_dim.19.start_ref
  9.5 113.3 %shard_map.254 = (bf16[320,1024]{1,0:T(8,128)(2,1)}, f32[320,1024]{1,0:T(8,128)}, f32[320,128]{1,0:T(8,128)}, f32[320,1024]{1,0:T(8,128)}, f32[320,128]{1,0:T(8,...) custom-call(bf16[320,1024]{1,0:T(8,128)(2,1)} %tok_ref.1, ...), custom_call_target="tpu_custom_call" | custom-call | flops 12079595520 | bytes 41943040 | tf_op jit(solution)/shard_map/pallas_call | solution.py:881
  122.8 1.7 copy.41
  124.5 1.0 select_bitcast_fusion.1
  125.8 265.0 %shard_map.255 = (bf16[2,1024,3072]{2,1,0:T(8,128)(2,1)}, bf16[3072,1024]{1,0:T(8,128)(2,1)}, bf16[3,2,1024,128]{3,2,1,0:T(8,128)(2,1)}, bf16[3,128,1024]{2,1,0:...) custom-call(bf16[320,1024]{1,0:T(8,128)(2,1)} %get-tuple-element.47., ...), custom_call_target="tpu_custom_call" | custom-call | flops 32212254720 | bytes 209715200 | tf_op jit(solution)/shard_map/pallas_call | solution.py:559
  390.8 1.8 collective-permute-start
  392.6 2.2 maximum_bitcast_fusion.gated_ref
  394.9 193.4 %shard_map.256 = (bf16[24,512,256]{2,1,0:T(8,128)(2,1)}, f32[320,1024]{1,0:T(8,128)}, f32[88,128]{1,0:T(8,128)}, bf16[2,1024,3072]{2,1,0:T(8,128)(2,1)}, bf16[3072,1024]{1,0:T(8,128)(2,1)}) custom-call(f32[320,1024]{1,0:T(8,128)} %get-tuple-element.52.back_ref, ...), custom_call_target="tpu_custom_call", output_to_operand_aliasing={{3}: (31, {}), {4}: (32, {})} | custom-call | flops 8053063680 | bytes 104857600 | tf_op jit(solution)/shard_map/pallas_call | solution.py:1352
  588.3 0.8 slice_bitcast_fusion
  589.1 15.9 %bitcast_convert_fusion = (f32[1024,3072]{1,0:T(8,128)}, f32[1024,3072]{1,0:T(8,128)}) fusion(bf16[2,1024,3072]{2,1,0:T(8,128)(2,1)} %get-tuple-element.76), kind=kLoop, calls=%fused_computation | loop fusion | flops 6291456 | bytes 37748736 | tf_op jit(solution)/shard_map/convert_element_type | solution.py:1540
  605.0 6.4 %convert_element_type.38 = f32[3072,1024]{1,0:T(8,128)} convert(bf16[3072,1024]{1,0:T(8,128)(2,1)S(1)} %bitcast.37) | non-fusion elementwise | flops 3145728 | bytes 18874368 | tf_op jit(solution)/shard_map/convert_element_type | solution.py:1541
  611.3 5.1 shard_map.257
  617.1 1.3 slice_bitcast_fusion.3
  618.4 1.3 slice_bitcast_fusion.1
  619.7 1.2 add_convert_fusion
  620.9 1.1 copy.46
  (25 shorter events, 2.0 us)
Async XLA Ops:
  125.5 267.2 %collective-permute-start.1 = (bf16[640,512]{0,1:T(8,128)(2,1)}, bf16[640,512]{0,1:T(8,128)(2,1)}, u32[]{:S(2)}, u32[]{:S(2)}) collective-permute-start(bf16[640,512]{0,1:T(8,128)(2,1)} %get-tuple-element.81), channel_id=1, source_target_pairs={{0,4},{4,0},{8,12},{12,8},{16,20},{20,16},{24,28},{28,24},{1,5},{5... | collective-permute-start | bytes 1966088 | tf_op jit(solution)/shard_map/ppermute | solution.py:20
  390.8 228.8 %collective-permute-start = (bf16[320,1024]{1,0:T(8,128)(2,1)}, bf16[320,1024]{1,0:T(8,128)(2,1)S(1)}, u32[]{:S(2)}, u32[]{:S(2)}) collective-permute-start(bf16[320,1024]{1,0:T(8,128)(2,1)} %get-tuple-element.51), channel_id=1, source_target_pairs={{0,4},{4,0},{8,12},{12,8},{16,20},{20,16},{24,28},{28,24},{1,5},{5... | collective-permute-start | bytes 1966088 | tf_op jit(solution)/shard_map/ppermute | solution.py:20
  589.1 15.9 %slice-start = ((s8[6291456]{0:T(1024)(128)(4,1)}), s8[4194304]{0:T(1024)(128)(4,1)S(1)}, s32[]{:S(2)}) async-start(s8[6291456]{0:T(1024)(128)(4,1)} %bitcast.36), calls=%async_computation | async-start | bytes 8388608
  589.1 15.9 %slice-start.1 = ((s8[6291456]{0:T(1024)(128)(4,1)}), s8[2097152]{0:T(1024)(128)(4,1)S(1)}, s32[]{:S(2)}) async-start(s8[6291456]{0:T(1024)(128)(4,1)} %bitcast.36), calls=%async_computation.1 | async-start | bytes 4194304
  605.0 6.4 %copy-start = (bf16[24,512,256]{2,1,0:T(8,128)(2,1)S(1)}, bf16[24,512,256]{2,1,0:T(8,128)(2,1)}, u32[]{:S(2)}) copy-start(bf16[24,512,256]{2,1,0:T(8,128)(2,1)} %get-tuple-element.71.grads_ref) | copy-start | bytes 18874372
  611.3 8.3 %copy-start.1 = (f32[320,1024]{1,0:T(8,128)S(1)}, f32[320,1024]{1,0:T(8,128)}, u32[]{:S(2)}) copy-start(f32[320,1024]{1,0:T(8,128)} %get-tuple-element.46.resid_ref) | copy-start | bytes 3932164
  611.3 8.3 %copy-start.3 = (f32[320,1024]{1,0:T(8,128)S(1)}, f32[320,1024]{1,0:T(8,128)}, u32[]{:S(2)}) copy-start(f32[320,1024]{1,0:T(8,128)} %get-tuple-element.50) | copy-start | bytes 3932164
  616.5 4.4 copy-start.2
